TPU v7x, 32 devices: a whole 2x2x4 slice. The times are simulated.
32 devices in a mesh: dp: 4 (over y, x), expert: 8 (over z, core).
Axes of the slice: x: 2, y: 2, z: 4, core: 2. Of those that a mesh axis runs over, the one named last changes fastest.
Arguments:
- item_feats: bfloat16 [8, 2048, 256], P('expert', 'dp'), may hold values from -6 to 6
- expert_ids: int32 [8, 2048, 1], P('expert', 'dp'), may hold values from 0 to 31; in each aligned block of 512 rows (0 to 511, 512 to 1023, ..., all dimensions but the last counted through in order) at most 32 rows name the same one
- weight_in: bfloat16 [32, 256, 1024], P('expert'), may hold values from -0.375 to 0.375
- weight_out: bfloat16 [32, 1024, 256], P('expert'), may hold values from -0.1875 to 0.1875
- queries: bfloat16 [8, 2048, 256], P('expert', 'dp'), may hold values from -150 to 150
- query_weight: float32 [8, 2048], P('expert', 'dp'), may hold values from 0.25 to 2
- positives: int32 [8, 2048], P('expert', 'dp'), may hold values from 0 to 2047
- sample_counts: int32 [8, 2048], P('expert'), may hold values from 1 to 4095
Outputs:
- query_loss: float32 [8, 2048], P('expert', 'dp')
- grad_queries: float32 [8, 2048, 256], P('expert', 'dp')
- grad_items: float32 [8, 2048, 256], P('expert', 'dp')
- grad_weight_in: float32 [256, 32, 1024], P('dp', 'expert')
- grad_weight_out: float32 [1024, 32, 256], P('dp', 'expert')
Inputs may be any that keep to these rules, and one draw needn't show every extreme that they name: `expert_ids`: the 512 items of one device name each expert at most 32 times.
All inputs are finite; a program needn't handle non-finite values.
Results may differ from a plain program's by a relative error of at most 0.023.
The roundings to bfloat16 on the way count: a program that leaves them out, or rounds other values in their place, can miss the bound.
Values may be sent and summed in bfloat16 or wider, within the bound.
No kernel may reach another device: no remote copies, remote signals or barrier semaphores. Data moves between devices by JAX's collectives and lax.ppermute only.
A program may use at most 128 MiB of HBM per device.

v0:
```python
import functools

import jax
import jax.numpy as jnp
from jax import lax
from jax.experimental import pallas as pl
from jax.experimental.pallas import tpu as pltpu
from jax.sharding import PartitionSpec as P

CAP = 32
norm_eps = 1e-06
BF = jnp.bfloat16
F32 = jnp.float32
GELU_C = 0.7978845608028654
GELU_A = 0.044715


def dg(a, b, ca, cb):
    return lax.dot_general(a, b, (((ca,), (cb,)), ((), ())), preferred_element_type=F32)


def iota(shape, axis):
    return lax.broadcasted_iota(jnp.int32, shape, axis)


def eye(n):
    return jnp.where(iota((n, n), 0) == iota((n, n), 1), 1.0, 0.0).astype(BF)


def to_col(row):
    n = row.shape[1]
    sub = iota((16, n), 0)
    high = lax.shift_right_logical(row, 8)
    low = lax.bitwise_and(row, 255)
    halves = jnp.where(sub == 0, high, jnp.where(sub == 1, low, 0)).astype(F32).astype(BF)
    cols = dg(eye(n), halves, 1, 1)
    return cols[:, 0:1] * 256.0 + cols[:, 1:2]


def gelu(v):
    return 0.5 * v * (1.0 + jnp.tanh(GELU_C * (v + GELU_A * v * v * v)))


def gelu_both(v):
    sq = v * v
    th = jnp.tanh(GELU_C * (v + GELU_A * v * sq))
    half = 0.5 * (1.0 + th)
    slope = half + 0.5 * v * (1.0 - th * th) * (GELU_C + (3.0 * GELU_A * GELU_C) * sq)
    return v * half, slope


def scatter_matrix(slot_row, block, rows):
    return jnp.where(iota((rows, slot_row.shape[1]), 0) + block * rows == slot_row, 1.0, 0.0).astype(BF)


def gather_rows(slot_row, blocks):
    col = to_col(slot_row).astype(jnp.int32)
    n, rows = slot_row.shape[1], blocks[0].shape[0]
    total = jnp.concatenate([b[...] for b in blocks], axis=0)
    pick = jnp.where(iota((n, rows * len(blocks)), 1) == col, 1.0, 0.0).astype(BF)
    return dg(pick, total, 1, 0)


def inv_rms_of(x):
    return lax.rsqrt(jnp.mean(x * x, axis=1, keepdims=True) + norm_eps)


def pack_kernel(local_experts, experts_all, groups, ids_hbm, feats_hbm, *refs):
    slot_ref, blocks = refs[0], refs[1 : groups + 1]
    ids_ref, feats_ref, ids_sem, feats_sem = refs[groups + 1 :]
    ids_copy = pltpu.make_async_copy(ids_hbm, ids_ref, ids_sem)
    feats_copy = pltpu.make_async_copy(feats_hbm, feats_ref, feats_sem)
    ids_copy.start()
    feats_copy.start()
    me = lax.axis_index("expert")
    ids_copy.wait()
    ids = ids_ref[...]
    n = ids.shape[1]
    shift = local_experts.bit_length() - 1
    hot = iota((experts_all, n), 0) == ids
    tri = jnp.where(iota((n, n), 0) < iota((n, n), 1), 1.0, 0.0).astype(BF)
    before = dg(jnp.where(hot, 1.0, 0.0).astype(BF), tri, 1, 0)
    rank = jnp.sum(jnp.where(hot, before, 0.0), axis=0, keepdims=True).astype(jnp.int32)
    owner = lax.bitwise_xor(lax.shift_right_logical(ids, shift), me)
    local = lax.bitwise_and(ids, local_experts - 1)
    slot = (owner * local_experts + local) * CAP + rank
    slot_ref[...] = slot
    feats_copy.wait()
    x = feats_ref[...].astype(F32)
    normed = (x * inv_rms_of(x)).astype(BF)
    rows = local_experts * CAP
    for s in range(groups):
        blocks[s][...] = dg(scatter_matrix(slot, s, rows), normed, 1, 0).astype(BF)


def load_kernel(win_hbm, wout_hbm, win_ref, wout_ref, in_sem, out_sem):
    copies = (
        pltpu.make_async_copy(win_hbm, win_ref, in_sem),
        pltpu.make_async_copy(wout_hbm, wout_ref, out_sem),
    )
    for copy in copies:
        copy.start()
    for copy in copies:
        copy.wait()


def expert_rows(blocks, k):
    return jnp.concatenate([b[k * CAP : (k + 1) * CAP, :] for b in blocks], axis=0)


def forward_kernel(groups, win_ref, wout_ref, *refs):
    blocks, outs = refs[:groups], refs[groups:]
    for k in range(win_ref.shape[0]):
        x = expert_rows(blocks, k)
        act = gelu(dg(x, win_ref[k], 1, 0)).astype(BF)
        y = dg(act, wout_ref[k], 1, 0).astype(BF)
        for s in range(groups):
            outs[s][k * CAP : (k + 1) * CAP, :] = y[s * CAP : (s + 1) * CAP, :]


def slope_kernel(groups, win_ref, *refs):
    blocks, slope_ref = refs[:groups], refs[groups]
    for k in range(win_ref.shape[0]):
        _, slope = gelu_both(dg(expert_rows(blocks, k), win_ref[k], 1, 0))
        slope_ref[k] = slope


def regroup_kernel(groups, shards, *refs):
    blocks, outs = refs[:groups], refs[groups:]
    me = lax.axis_index("dp")
    for s in range(shards):
        start = pl.multiple_of(lax.bitwise_xor(me, s) * CAP, CAP)
        for g in range(groups):
            outs[s][g * CAP : (g + 1) * CAP, :] = blocks[g][pl.ds(start, CAP), :]


def log_counts_col(counts_ref, shard, rows):
    part = counts_ref[:, pl.ds(pl.multiple_of(shard * rows, 128), rows)]
    return jnp.log(to_col(part))


def unit_kernel(groups, shards, feats_ref, slot_ref, counts_ref, w_ref, pos_ref, *refs):
    blocks = refs[:groups]
    queries = refs[groups : groups + shards]
    low_ref, unit_ref, length_ref, stats_ref, terms_ref = refs[groups + shards :]
    rows = feats_ref.shape[0]
    branch = gather_rows(slot_ref[...], blocks)
    summed = feats_ref[...].astype(F32) + branch
    length = jnp.sqrt(jnp.sum(summed * summed, axis=1, keepdims=True) + norm_eps)
    unit = summed / length
    low = unit.astype(BF)
    low_ref[...] = low
    unit_ref[...] = unit
    length_ref[...] = jnp.broadcast_to(length, length_ref.shape)
    logs = log_counts_col(counts_ref, lax.axis_index("dp"), rows)
    for s in range(shards):
        scores = dg(low, queries[s][...], 1, 1) - logs
        high = jnp.max(scores, axis=0, keepdims=True)
        stats_ref[s : s + 1, :] = high
        terms = jnp.exp(scores - high)
        terms_ref[s] = terms
        stats_ref[shards + s : shards + s + 1, :] = jnp.sum(terms, axis=0, keepdims=True)
    stats_ref[2 * shards : 2 * shards + 1, :] = w_ref[...]
    stats_ref[2 * shards + 1 : 2 * shards + 2, :] = pos_ref[...].astype(F32)


def grad_kernel(groups, shards, slot_ref, unit_ref, length_ref, terms_ref, *refs):
    queries = refs[:shards]
    stats = refs[shards : 2 * shards]
    summed_ref, lse_ref = refs[2 * shards : 2 * shards + 2]
    outs = refs[2 * shards + 2 :]
    rows = unit_ref.shape[0]
    item = iota((rows, 1), 0) + lax.axis_index("dp") * rows
    total = None
    for u in range(shards):
        highs = [stats[t][(t ^ u) : (t ^ u) + 1, :] for t in range(shards)]
        sums = [stats[t][shards + (t ^ u) : shards + (t ^ u) + 1, :] for t in range(shards)]
        high = functools.reduce(jnp.maximum, highs)
        lse = high + jnp.log(sum(l * jnp.exp(m - high) for l, m in zip(sums, highs)))
        if u == 0:
            lse_ref[...] = lse
        weight = stats[u][2 * shards : 2 * shards + 1, :]
        target = stats[u][2 * shards + 1 : 2 * shards + 2, :].astype(jnp.int32)
        scale = weight * jnp.exp(highs[0] - lse)
        coeff = (terms_ref[u] * scale - jnp.where(item == target, weight, 0.0)).astype(BF)
        part = dg(coeff, queries[u][...], 1, 0)
        total = part if total is None else total + part
    unit = unit_ref[...]
    along = jnp.sum(unit * total, axis=1, keepdims=True)
    summed = (total - unit * along) / length_ref[:, 0:1]
    summed_ref[...] = summed
    low_grad = summed.astype(BF)
    slot = slot_ref[...]
    for s in range(groups):
        outs[s][...] = dg(scatter_matrix(slot, s, outs[s].shape[0]), low_grad, 1, 0).astype(BF)


def turned(row):
    return jnp.transpose(jnp.broadcast_to(row, (128, row.shape[1])))


def query_kernel(shards, query_ref, counts_ref, lse_ref, w_ref, pos_ref, *refs):
    units = refs[:shards]
    loss_ref, grad_ref = refs[shards:]
    rows = units[0].shape[0]
    me = lax.axis_index("dp")
    query = query_ref[...]
    lse, weight = turned(lse_ref[...])[:, 0:1], turned(w_ref[...])[:, 0:1]
    target = turned(pos_ref[...].astype(F32))[:, 0:1].astype(jnp.int32)
    picked, total = None, None
    for u in range(shards):
        shard = lax.bitwise_xor(me, u)
        unit = units[u][...]
        counts = counts_ref[:, pl.ds(pl.multiple_of(shard * rows, 128), rows)]
        scores = dg(query, unit, 1, 1) - jnp.log(counts.astype(F32))
        hit = iota((1, rows), 1) + shard * rows == target
        here = jnp.sum(jnp.where(hit, scores, 0.0), axis=1, keepdims=True)
        coeff = (weight * (jnp.exp(scores - lse) - jnp.where(hit, 1.0, 0.0))).astype(BF)
        part = dg(coeff, unit, 1, 0)
        picked = here if picked is None else picked + here
        total = part if total is None else total + part
    loss = jnp.broadcast_to(lse - picked, (query.shape[0], 128))
    loss_ref[...] = jnp.transpose(loss)[0:1, :]
    grad_ref[...] = total


def backward_kernel(groups, win_ref, wout_ref, slope_ref, *refs):
    gs, outs = refs[:groups], refs[groups:]
    for k in range(win_ref.shape[0]):
        hidden = (dg(expert_rows(gs, k), wout_ref[k], 1, 1) * slope_ref[k]).astype(BF)
        y = dg(hidden, win_ref[k], 1, 1).astype(BF)
        for s in range(groups):
            outs[s][k * CAP : (k + 1) * CAP, :] = y[s * CAP : (s + 1) * CAP, :]


def early_kernel(shards, win_ref, *refs):
    xs = refs[:shards]
    act_ref, slope_ref, xt_ref = refs[shards:]
    me = lax.axis_index("dp")
    win = win_ref[me]
    width = xs[0].shape[0]
    for s in range(shards):
        x = xs[s][...]
        act, slope = gelu_both(dg(win, x, 0, 1))
        act_ref[:, s * width : (s + 1) * width] = act.astype(BF)
        slope_ref[:, s * width : (s + 1) * width] = slope.astype(BF)
        xt_ref[:, s * width : (s + 1) * width] = dg(eye(x.shape[1]), x, 1, 1).astype(BF)


def weight_kernel(shards, wout_ref, act_ref, slope_ref, xt_ref, *refs):
    gs, outs, full = refs[:shards], refs[shards:-1], refs[-1]
    me = lax.axis_index("dp")
    g = jnp.concatenate([r[...] for r in gs], axis=0)
    width = g.shape[1]
    hidden = (dg(wout_ref[me], g, 1, 1) * slope_ref[...].astype(F32)).astype(BF)
    full[...] = dg(xt_ref[...], hidden, 1, 1)
    out_rows, in_rows = act_ref.shape[0] // shards, full.shape[0] // shards
    for s in range(shards):
        peer = lax.bitwise_xor(me, s)
        start = pl.multiple_of(peer * out_rows, out_rows)
        outs[s][:out_rows, :] = dg(act_ref[pl.ds(start, out_rows), :], g, 1, 0).astype(BF)
        start = pl.multiple_of(peer * in_rows, in_rows)
        for c in range(full.shape[1] // width):
            piece = full[pl.ds(start, in_rows), c * width : (c + 1) * width]
            first = out_rows + c * in_rows
            outs[s][first : first + in_rows, :] = piece.astype(BF)


def assemble_kernel(shards, *refs):
    parts, (in_ref, out_ref) = refs[:shards], refs[shards:]
    me = lax.axis_index("dp")
    in_rows, experts, units = in_ref.shape
    out_rows, _, width = out_ref.shape
    size = in_rows * experts
    row, col = iota((size, size), 0), iota((size, size), 1)
    bits = experts.bit_length() - 1
    wanted = lax.bitwise_xor(lax.bitwise_and(row, experts - 1), me) * in_rows
    spread_rows = jnp.where(wanted + lax.shift_right_logical(row, bits) == col, 1.0, 0.0).astype(BF)
    for c in range(units // width):
        first = out_rows + c * in_rows
        stacked = jnp.concatenate([r[first : first + in_rows, :] for r in parts], axis=0)
        block = dg(spread_rows, stacked, 1, 0)
        in_ref[:, :, c * width : (c + 1) * width] = block.reshape(in_rows, experts, width)
    for c in range(out_rows // in_rows):
        first = c * in_rows
        stacked = jnp.concatenate([r[first : first + in_rows, :] for r in parts], axis=0)
        block = dg(spread_rows, stacked, 1, 0)
        out_ref[first : first + in_rows] = block.reshape(in_rows, experts, width)


def final_kernel(groups, feats_ref, slot_ref, summed_ref, *refs):
    blocks, out_ref = refs[:groups], refs[groups]
    x = feats_ref[...].astype(F32)
    r = inv_rms_of(x)
    rows = gather_rows(slot_ref[...], blocks)
    projected = jnp.mean(rows * x, axis=1, keepdims=True)
    out_ref[...] = summed_ref[...] + r * (rows - x * (r * r) * projected)


def call(body, outs, args, flops=0, touched=0, trans=0, scratch=(), space=pltpu.VMEM, limit=24):
    shapes = [jax.ShapeDtypeStruct(s, d) for s, d in outs]
    return pl.pallas_call(
        body,
        out_shape=shapes,
        in_specs=[pl.BlockSpec(memory_space=space)] * len(args),
        out_specs=[pl.BlockSpec(memory_space=pltpu.VMEM)] * len(outs),
        scratch_shapes=list(scratch),
        cost_estimate=pl.CostEstimate(flops=flops, bytes_accessed=touched, transcendentals=trans),
        compiler_params=pltpu.CompilerParams(vmem_limit_bytes=limit << 20),
    )(*args)


def shift_by(values, axis, s):
    n = lax.axis_size(axis)
    return lax.ppermute(values, axis, [(i, i ^ s) for i in range(n)])


def exchange(blocks, axis):
    return [blocks[0]] + [shift_by(b, axis, s) for s, b in enumerate(blocks) if s > 0]


def spread(block, axis):
    return exchange([block] * lax.axis_size(axis), axis)


def per_device(
    item_feats, expert_ids, weight_in, weight_out, queries, query_weight, positives, sample_counts
):
    groups, shards = lax.axis_size("expert"), lax.axis_size("dp")
    local_experts, width, units = weight_in.shape
    rows, q_rows = item_feats.shape[1], queries.shape[1]
    experts_all = local_experts * groups
    feats = item_feats[0]
    ids = expert_ids.reshape(1, rows)
    slots = local_experts * CAP
    query = queries[0]
    block = ((slots, width), BF)
    matmul = 2 * rows * q_rows * shards * width
    expert_flops = 2 * groups * slots * width * units

    slot, *packed = call(
        functools.partial(pack_kernel, local_experts, experts_all, groups),
        [((1, rows), jnp.int32)] + [block] * groups,
        (ids, feats),
        flops=2 * groups * slots * rows * width,
        touched=1 << 20,
        scratch=[
            pltpu.VMEM((1, rows), jnp.int32),
            pltpu.VMEM((rows, width), BF),
            pltpu.SemaphoreType.DMA(()),
            pltpu.SemaphoreType.DMA(()),
        ],
        space=pltpu.HBM,
        limit=60,
    )
    received = exchange(packed, "expert")
    all_queries = spread(query, "dp")
    weight_in, weight_out = call(
        load_kernel,
        [(weight_in.shape, BF), (weight_out.shape, BF)],
        (weight_in, weight_out),
        touched=16 << 20,
        scratch=[pltpu.SemaphoreType.DMA(()), pltpu.SemaphoreType.DMA(())],
        space=pltpu.HBM,
    )
    output = call(
        functools.partial(forward_kernel, groups),
        [block] * groups,
        (weight_in, weight_out, *received),
        flops=2 * expert_flops,
        touched=6 << 20,
        trans=groups * slots * units,
    )
    returned = exchange(output, "expert")
    (slope,) = call(
        functools.partial(slope_kernel, groups),
        [((local_experts, groups * CAP, units), F32)],
        (weight_in, *received),
        flops=expert_flops,
        touched=6 << 20,
        trans=groups * slots * units,
    )
    low, unit, length, stats, terms = call(
        functools.partial(unit_kernel, groups, shards),
        [
            ((rows, width), BF),
            ((rows, width), F32),
            ((rows, 128), F32),
            ((2 * shards + 2, q_rows), F32),
            ((shards, rows, q_rows), F32),
        ],
        (feats, slot, sample_counts, query_weight, positives, *returned, *all_queries),
        flops=2 * matmul,
        touched=4 << 20,
        trans=rows * q_rows * shards,
    )
    all_stats = spread(stats, "dp")
    summed, lse, *packed_grads = call(
        functools.partial(grad_kernel, groups, shards),
        [((rows, width), F32), ((1, q_rows), F32)] + [block] * groups,
        (slot, unit, length, terms, *all_queries, *all_stats),
        flops=3 * matmul,
        touched=4 << 20,
        trans=rows * q_rows * shards,
    )
    received_grads = exchange(packed_grads, "expert")
    all_units = spread(low, "dp")
    query_loss, grad_queries = call(
        functools.partial(query_kernel, shards),
        [((1, q_rows), F32), ((q_rows, width), F32)],
        (query, sample_counts, lse, query_weight, positives, *all_units),
        flops=2 * matmul,
        touched=3 << 20,
        trans=rows * q_rows * shards,
    )
    grad_out = call(
        functools.partial(backward_kernel, groups),
        [block] * groups,
        (weight_in, weight_out, slope, *received_grads),
        flops=2 * expert_flops,
        touched=6 << 20,
        trans=groups * slots * units,
    )
    grad_back = exchange(grad_out, "expert")
    (grad_items,) = call(
        functools.partial(final_kernel, groups),
        [((rows, width), F32)],
        (feats, slot, summed, *grad_back),
        flops=2 * groups * slots * rows * width,
        touched=2 << 20,
    )
    if shards == local_experts:
        tokens = ((groups * CAP, width), BF)
        regroup = functools.partial(regroup_kernel, groups, shards)
        own_x = exchange(call(regroup, [tokens] * shards, received, touched=1 << 20), "dp")
        total_rows = shards * groups * CAP
        act, act_slope, xt = call(
            functools.partial(early_kernel, shards),
            [((units, total_rows), BF), ((units, total_rows), BF), ((width, total_rows), BF)],
            (weight_in, *own_x),
            flops=expert_flops,
            touched=6 << 20,
            trans=total_rows * units,
        )
        own_g = exchange(call(regroup, [tokens] * shards, received_grads, touched=1 << 20), "dp")
        parts = exchange(
            call(
                functools.partial(weight_kernel, shards),
                [((units // shards + units // shards, width), BF)] * shards,
                (weight_out, act, act_slope, xt, *own_g),
                flops=3 * expert_flops,
                touched=6 << 20,
                scratch=[pltpu.VMEM((width, units), F32)],
            ),
            "dp",
        )
        grad_weight_in, grad_weight_out = call(
            functools.partial(assemble_kernel, shards),
            [
                ((width // shards, local_experts, units), F32),
                ((units // shards, local_experts, width), F32),
            ],
            parts,
            flops=expert_flops,
            touched=6 << 20,
        )
    else:
        x = jnp.stack(received).reshape(groups, local_experts, CAP, width)
        g = jnp.stack(received_grads).reshape(groups, local_experts, CAP, width)
        hidden = jnp.einsum("skcd,kdf->skcf", x, weight_in, preferred_element_type=F32)
        active, slope = gelu_both(hidden)
        grad_active = jnp.einsum("skcd,kfd->skcf", g, weight_out, preferred_element_type=F32)
        grad_hidden = (grad_active * slope).astype(BF)

        def reduce(a, b):
            part = jnp.einsum("skcr,skcf->rkf", a, b, preferred_element_type=F32).astype(BF)
            return lax.psum_scatter(part, "dp", scatter_dimension=0, tiled=True).astype(F32)

        grad_weight_in, grad_weight_out = reduce(x, grad_hidden), reduce(active.astype(BF), g)
    return (query_loss, grad_queries[None], grad_items[None], grad_weight_in, grad_weight_out)


def solution(mesh):
    placed = (
        P("expert", "dp", None),
        P("expert", "dp", None),
        P("expert", None, None),
        P("expert", None, None),
        P("expert", "dp", None),
        P("expert", "dp"),
        P("expert", "dp"),
        P("expert", None),
    )

    return jax.shard_map(
        per_device,
        mesh=mesh,
        in_specs=placed,
        out_specs=(
            P("expert", "dp"),
            P("expert", "dp", None),
            P("expert", "dp", None),
            P("dp", "expert", None),
            P("dp", "expert", None),
        ),
        check_vma=False,
    )
```

profile of v0, /device:TPU:0, one launch (start us, length us, event | category | flops | bytes accessed | tf_op | source)
XLA Modules:
  0.0 116.7 jit_solution(12416427326847671000)
XLA Ops:
  0.6 2.2 %shard_map.119 = (s32[1,512]{1,0:T(1,128)}, bf16[128,256]{1,0:T(8,128)(2,1)}, bf16[128,256]{1,0:T(8,128)(2,1)}, bf16[128,256]{1,0:T(8,128)(2,1)}, bf16[128,256]{...) custom-call(s32[1,512]{1,0:T(1,128)} %bitcast.15, ...), custom_call_target="tpu_custom_call" | custom-call | flops 268435456 | bytes 1048576 | tf_op jit(solution)/shard_map/pallas_call | solution.py:302
  3.4 2.6 %collective-permute-start.1 = (bf16[128,256]{1,0:T(8,128)(2,1)}, bf16[128,256]{1,0:T(8,128)(2,1)S(1)}, u32[]{:S(2)}, u32[]{:S(2)}) collective-permute-start(bf16[128,256]{1,0:T(8,128)(2,1)} %get-tuple-element.71), channel_id=1, source_target_pairs={{0,2},{1,3},{2,0},{3,1},{4,6},{5,7},{6,4},{7,5},{8,10},{9,11},{10,... | collective-permute-start | bytes 196616 | tf_op jit(solution)/shard_map/ppermute | solution.py:315
  6.0 2.8 %collective-permute-start.3 = (bf16[128,256]{1,0:T(8,128)(2,1)}, bf16[128,256]{1,0:T(8,128)(2,1)S(1)}, u32[]{:S(2)}, u32[]{:S(2)}) collective-permute-start(bf16[128,256]{1,0:T(8,128)(2,1)} %get-tuple-element.73), channel_id=1, source_target_pairs={{0,4},{1,5},{2,6},{3,7},{4,0},{5,1},{6,2},{7,3},{8,12},{9,13},{10,... | collective-permute-start | bytes 196616 | tf_op jit(solution)/shard_map/ppermute | solution.py:315
  8.8 3.6 %collective-permute-start.5 = (bf16[128,256]{1,0:T(8,128)(2,1)}, bf16[128,256]{1,0:T(8,128)(2,1)S(1)}, u32[]{:S(2)}, u32[]{:S(2)}) collective-permute-start(bf16[128,256]{1,0:T(8,128)(2,1)} %get-tuple-element.75), channel_id=1, source_target_pairs={{0,6},{1,7},{2,4},{3,5},{4,2},{5,3},{6,0},{7,1},{8,14},{9,15},{10,... | collective-permute-start | bytes 196616 | tf_op jit(solution)/shard_map/ppermute | solution.py:315
  12.5 1.6 %copy-done = bf16[4,256,1024]{2,1,0:T(8,128)(2,1)S(1)} copy-done((bf16[4,256,1024]{2,1,0:T(8,128)(2,1)S(1)}, bf16[4,256,1024]{2,1,0:T(8,128)(2,1)}, u32[]{:S(2)}) %copy-start) | copy-done | bytes 2097176
  14.1 1.6 %copy-done.1 = bf16[4,1024,256]{2,1,0:T(8,128)(2,1)S(1)} copy-done((bf16[4,1024,256]{2,1,0:T(8,128)(2,1)S(1)}, bf16[4,1024,256]{2,1,0:T(8,128)(2,1)}, u32[]{:S(2)}) %copy-start.1) | copy-done | bytes 2097176
  16.1 3.4 %collective-permute-done.4.refs_5_ = bf16[128,256]{1,0:T(8,128)(2,1)S(1)} collective-permute-done((bf16[128,256]{1,0:T(8,128)(2,1)}, bf16[128,256]{1,0:T(8,128)(2,1)S(1)}, u32[]{:S(2)}, u32[]{:S(2)}) %collective-permute-start.4) | collective-permute-done | bytes 65568 | tf_op jit(solution)/shard_map/ppermute | solution.py:315
  19.6 1.7 %shard_map.121 = (bf16[128,256]{1,0:T(8,128)(2,1)S(1)}, bf16[128,256]{1,0:T(8,128)(2,1)S(1)}, bf16[128,256]{1,0:T(8,128)(2,1)S(1)}, bf16[128,256]{1,0:T(8,128)(2...) custom-call(bf16[4,256,1024]{2,1,0:T(8,128)(2,1)S(1)} %get-tuple-ele, ...), custom_call_target="tpu_custom_call" | custom-call | flops 1073741824 | bytes 6291456 | tf_op jit(solution)/shard_map/pallas_call | solution.py:302
  21.5 1.5 %collective-permute-start.14 = (bf16[512,256]{1,0:T(8,128)(2,1)S(1)}, bf16[512,256]{1,0:T(8,128)(2,1)S(1)}, u32[]{:S(2)}, u32[]{:S(2)}) collective-permute-start(bf16[512,256]{1,0:T(8,128)(2,1)S(1)} %bitcast.5), channel_id=1, source_target_pairs={{0,8},{8,0},{16,24},{24,16},{1,9},{9,1},{17,25},{25,17},{2,10},{10... | collective-permute-start | bytes 786440 | tf_op jit(solution)/shard_map/ppermute | solution.py:315
  23.0 1.5 %collective-permute-start.15 = (bf16[512,256]{1,0:T(8,128)(2,1)S(1)}, bf16[512,256]{1,0:T(8,128)(2,1)S(1)}, u32[]{:S(2)}, u32[]{:S(2)}) collective-permute-start(bf16[512,256]{1,0:T(8,128)(2,1)S(1)} %bitcast.6), channel_id=1, source_target_pairs={{0,16},{8,24},{16,0},{24,8},{1,17},{9,25},{17,1},{25,9},{2,18},{10... | collective-permute-start | bytes 786440 | tf_op jit(solution)/shard_map/ppermute | solution.py:315
  25.0 3.3 %collective-permute-start.8 = (bf16[128,256]{1,0:T(8,128)(2,1)S(1)}, bf16[128,256]{1,0:T(8,128)(2,1)S(1)}, u32[]{:S(2)}, u32[]{:S(2)}) collective-permute-start(bf16[128,256]{1,0:T(8,128)(2,1)S(1)} %get-tuple-element.79), channel_id=1, source_target_pairs={{0,2},{1,3},{2,0},{3,1},{4,6},{5,7},{6,4},{7,5},{8,10},{9,11},{10,... | collective-permute-start | bytes 196616 | tf_op jit(solution)/shard_map/ppermute | solution.py:315
  28.3 2.2 %collective-permute-done.8.refs_2_ = bf16[128,256]{1,0:T(8,128)(2,1)S(1)} collective-permute-done((bf16[128,256]{1,0:T(8,128)(2,1)S(1)}, bf16[128,256]{1,0:T(8,128)(2,1)S(1)}, u32[]{:S(2)}, u32[]{:S(2)}) %collective-permute-start.8) | collective-permute-done | bytes 65568 | tf_op jit(solution)/shard_map/ppermute | solution.py:315
  30.5 3.3 %collective-permute-start.10 = (bf16[128,256]{1,0:T(8,128)(2,1)S(1)}, bf16[128,256]{1,0:T(8,128)(2,1)S(1)}, u32[]{:S(2)}, u32[]{:S(2)}) collective-permute-start(bf16[128,256]{1,0:T(8,128)(2,1)S(1)} %get-tuple-element.81), channel_id=1, source_target_pairs={{0,4},{1,5},{2,6},{3,7},{4,0},{5,1},{6,2},{7,3},{8,12},{9,13},{10,... | collective-permute-start | bytes 196616 | tf_op jit(solution)/shard_map/ppermute | solution.py:315
  34.3 1.8 %collective-permute-done.10.refs_4_ = bf16[128,256]{1,0:T(8,128)(2,1)S(1)} collective-permute-done((bf16[128,256]{1,0:T(8,128)(2,1)S(1)}, bf16[128,256]{1,0:T(8,128)(2,1)S(1)}, u32[]{:S(2)}, u32[]{:S(2)}) %collective-permute-start.10) | collective-permute-done | bytes 65568 | tf_op jit(solution)/shard_map/ppermute | solution.py:315
  36.1 2.2 %collective-permute-start.12 = (bf16[128,256]{1,0:T(8,128)(2,1)S(1)}, bf16[128,256]{1,0:T(8,128)(2,1)S(1)}, u32[]{:S(2)}, u32[]{:S(2)}) collective-permute-start(bf16[128,256]{1,0:T(8,128)(2,1)S(1)} %get-tuple-element.83), channel_id=1, source_target_pairs={{0,6},{1,7},{2,4},{3,5},{4,2},{5,3},{6,0},{7,1},{8,14},{9,15},{10,... | collective-permute-start | bytes 196616 | tf_op jit(solution)/shard_map/ppermute | solution.py:315
  38.3 2.1 %collective-permute-done.11.refs_5_ = bf16[128,256]{1,0:T(8,128)(2,1)S(1)} collective-permute-done((bf16[128,256]{1,0:T(8,128)(2,1)S(1)}, bf16[128,256]{1,0:T(8,128)(2,1)S(1)}, u32[]{:S(2)}, u32[]{:S(2)}) %collective-permute-start.11) | collective-permute-done | bytes 65568 | tf_op jit(solution)/shard_map/ppermute | solution.py:315
  40.4 1.6 %collective-permute-start.13 = (bf16[128,256]{1,0:T(8,128)(2,1)S(1)}, bf16[128,256]{1,0:T(8,128)(2,1)S(1)}, u32[]{:S(2)}, u32[]{:S(2)}) collective-permute-start(bf16[128,256]{1,0:T(8,128)(2,1)S(1)} %get-tuple-element.84), channel_id=1, source_target_pairs={{0,7},{1,6},{2,5},{3,4},{4,3},{5,2},{6,1},{7,0},{8,15},{9,14},{10,... | collective-permute-start | bytes 196616 | tf_op jit(solution)/shard_map/ppermute | solution.py:315
  42.3 4.2 %collective-permute-done.13.refs_7_ = bf16[128,256]{1,0:T(8,128)(2,1)S(1)} collective-permute-done((bf16[128,256]{1,0:T(8,128)(2,1)S(1)}, bf16[128,256]{1,0:T(8,128)(2,1)S(1)}, u32[]{:S(2)}, u32[]{:S(2)}) %collective-permute-start.13) | collective-permute-done | bytes 65568 | tf_op jit(solution)/shard_map/ppermute | solution.py:315
  46.5 2.7 %shard_map.122 = (bf16[512,256]{1,0:T(8,128)(2,1)S(1)}, f32[512,256]{1,0:T(8,128)S(1)}, f32[512,128]{1,0:T(8,128)S(1)}, f32[10,512]{1,0:T(8,128)S(1)}, f32[4,512,512]{2,1,0:T(8,128)S(1)}) custom-call(bf16[512,256]{1,0:T(8,128)(2,1)S(1)} %bitcast.12, s32[1,512]{1,0:T(1,128)S(1)} %copy-done.5, s32[1,2048]{1,0:T(1,128)S(1)} %copy-done.6, ...), custom_call_target="tpu_custom_call" | custom-call | flops 1073741824 | bytes 4194304 | tf_op jit(solution)/shard_map/pallas_call | solution.py:302
  49.2 1.5 %collective-permute-start.17 = (f32[10,512]{1,0:T(8,128)S(1)}, f32[10,512]{1,0:T(8,128)S(1)}, u32[]{:S(2)}, u32[]{:S(2)}) collective-permute-start(f32[10,512]{1,0:T(8,128)S(1)} %get-tuple-element.88.refs_4_), channel_id=1, source_target_pairs={{0,8},{8,0},{16,24},{24,16},{1,9},{9,1},{17,25},{25,17},{2,10},{10... | collective-permute-start | bytes 61448 | tf_op jit(solution)/shard_map/ppermute | solution.py:315
  50.8 1.5 %collective-permute-start.18 = (f32[10,512]{1,0:T(8,128)S(1)}, f32[10,512]{1,0:T(8,128)S(1)}, u32[]{:S(2)}, u32[]{:S(2)}) collective-permute-start(f32[10,512]{1,0:T(8,128)S(1)} %get-tuple-element.88.refs_4_), channel_id=1, source_target_pairs={{0,16},{8,24},{16,0},{24,8},{1,17},{9,25},{17,1},{25,9},{2,18},{10... | collective-permute-start | bytes 61448 | tf_op jit(solution)/shard_map/ppermute | solution.py:315
  53.2 1.5 %collective-permute-done.18.refs_6_ = f32[10,512]{1,0:T(8,128)S(1)} collective-permute-done((f32[10,512]{1,0:T(8,128)S(1)}, f32[10,512]{1,0:T(8,128)S(1)}, u32[]{:S(2)}, u32[]{:S(2)}) %collective-permute-start.18) | collective-permute-done | bytes 20512 | tf_op jit(solution)/shard_map/ppermute | solution.py:315
  54.7 2.4 %collective-permute-done.19.refs_7_ = f32[10,512]{1,0:T(8,128)S(1)} collective-permute-done((f32[10,512]{1,0:T(8,128)S(1)}, f32[10,512]{1,0:T(8,128)S(1)}, u32[]{:S(2)}, u32[]{:S(2)}) %collective-permute-start.19) | collective-permute-done | bytes 20512 | tf_op jit(solution)/shard_map/ppermute | solution.py:315
  57.1 1.7 %shard_map.123 = (f32[512,256]{1,0:T(8,128)S(1)}, f32[1,512]{1,0:T(1,128)S(1)}, bf16[128,256]{1,0:T(8,128)(2,1)S(1)}, bf16[128,256]{1,0:T(8,128)(2,1)S(1)}, bf16...) custom-call(s32[1,512]{1,0:T(1,128)S(1)} %copy-done.5, ...), custom_call_target="tpu_custom_call" | custom-call | flops 1610612736 | bytes 4194304 | tf_op jit(solution)/shard_map/pallas_call | solution.py:302
  59.0 1.8 %collective-permute-start.25 = (bf16[128,256]{1,0:T(8,128)(2,1)S(1)}, bf16[128,256]{1,0:T(8,128)(2,1)S(1)}, u32[]{:S(2)}, u32[]{:S(2)}) collective-permute-start(bf16[128,256]{1,0:T(8,128)(2,1)S(1)} %get-tuple-element.97), channel_id=1, source_target_pairs={{0,3},{1,2},{2,1},{3,0},{4,7},{5,6},{6,5},{7,4},{8,11},{9,10},{10,... | collective-permute-start | bytes 196616 | tf_op jit(solution)/shard_map/ppermute | solution.py:315
  60.8 1.2 collective-permute-start.26
  61.9 1.5 %collective-permute-start.27 = (bf16[128,256]{1,0:T(8,128)(2,1)S(1)}, bf16[128,256]{1,0:T(8,128)(2,1)S(1)}, u32[]{:S(2)}, u32[]{:S(2)}) collective-permute-start(bf16[128,256]{1,0:T(8,128)(2,1)S(1)} %get-tuple-element.99), channel_id=1, source_target_pairs={{0,5},{1,4},{2,7},{3,6},{4,1},{5,0},{6,3},{7,2},{8,13},{9,12},{10,... | collective-permute-start | bytes 196616 | tf_op jit(solution)/shard_map/ppermute | solution.py:315
  63.4 2.3 %collective-permute-start.28 = (bf16[128,256]{1,0:T(8,128)(2,1)S(1)}, bf16[128,256]{1,0:T(8,128)(2,1)S(1)}, u32[]{:S(2)}, u32[]{:S(2)}) collective-permute-start(bf16[128,256]{1,0:T(8,128)(2,1)S(1)} %get-tuple-element.100), channel_id=1, source_target_pairs={{0,6},{1,7},{2,4},{3,5},{4,2},{5,3},{6,0},{7,1},{8,14},{9,15},{10,... | collective-permute-start | bytes 196616 | tf_op jit(solution)/shard_map/ppermute | solution.py:315
  65.7 1.2 %collective-permute-start.29 = (bf16[128,256]{1,0:T(8,128)(2,1)S(1)}, bf16[128,256]{1,0:T(8,128)(2,1)S(1)}, u32[]{:S(2)}, u32[]{:S(2)}) collective-permute-start(bf16[128,256]{1,0:T(8,128)(2,1)S(1)} %get-tuple-element.101), channel_id=1, source_target_pairs={{0,7},{1,6},{2,5},{3,4},{4,3},{5,2},{6,1},{7,0},{8,15},{9,14},{10,... | collective-permute-start | bytes 196616 | tf_op jit(solution)/shard_map/ppermute | solution.py:315
  67.6 2.5 %shard_map.125.slope_ref = f32[4,256,1024]{2,1,0:T(8,128)S(1)} custom-call(bf16[4,256,1024]{2,1,0:T(8,128)(2,1)S(1)} %get-tuple-element.67.win_ref, bf16[128,256]{1,0:T(8,128)(2,1)S(1)} %copy-done.2, bf16[128,256]{1,0:T(8,128)(2,1)S(1)} %collective-permute-done.refs_1_, bf16[128,256]{1,0:T(8,128)(2,1)S(1)} %collective-permute-done.1.refs_2_, ...), custom_call_target="tpu_custom_call" | custom-call | flops 536870912 | bytes 6291456 | tf_op jit(solution)/shard_map/pallas_call | solution.py:302
  70.1 2.0 %collective-permute-done.26.refs_4_ = bf16[128,256]{1,0:T(8,128)(2,1)S(1)} collective-permute-done((bf16[128,256]{1,0:T(8,128)(2,1)S(1)}, bf16[128,256]{1,0:T(8,128)(2,1)S(1)}, u32[]{:S(2)}, u32[]{:S(2)}) %collective-permute-start.26) | collective-permute-done | bytes 65568 | tf_op jit(solution)/shard_map/ppermute | solution.py:315
  72.6 1.4 %collective-permute-start.39 = (bf16[256,256]{1,0:T(8,128)(2,1)S(1)}, bf16[256,256]{1,0:T(8,128)(2,1)S(1)}, u32[]{:S(2)}, u32[]{:S(2)}) collective-permute-start(bf16[256,256]{1,0:T(8,128)(2,1)S(1)} %get-tuple-element.113), channel_id=1, source_target_pairs={{0,24},{8,16},{16,8},{24,0},{1,25},{9,17},{17,9},{25,1},{2,26},{10... | collective-permute-start | bytes 393224 | tf_op jit(solution)/shard_map/ppermute | solution.py:315
  74.1 1.4 %shard_map.126 = (bf16[128,256]{1,0:T(8,128)(2,1)S(1)}, bf16[128,256]{1,0:T(8,128)(2,1)S(1)}, bf16[128,256]{1,0:T(8,128)(2,1)S(1)}, bf16[128,256]{1,0:T(8,128)(2...) custom-call(bf16[4,256,1024]{2,1,0:T(8,128)(2,1)S(1)} %get-tuple-ele, ...), custom_call_target="tpu_custom_call" | custom-call | flops 1073741824 | bytes 6291456 | tf_op jit(solution)/shard_map/pallas_call | solution.py:302
  75.5 2.5 %collective-permute-start.31 = (bf16[128,256]{1,0:T(8,128)(2,1)S(1)}, bf16[128,256]{1,0:T(8,128)(2,1)S(1)}, u32[]{:S(2)}, u32[]{:S(2)}) collective-permute-start(bf16[128,256]{1,0:T(8,128)(2,1)S(1)} %get-tuple-element.104), channel_id=1, source_target_pairs={{0,2},{1,3},{2,0},{3,1},{4,6},{5,7},{6,4},{7,5},{8,10},{9,11},{10,... | collective-permute-start | bytes 196616 | tf_op jit(solution)/shard_map/ppermute | solution.py:315
  78.1 1.8 %collective-permute-done.38.refs_2_ = bf16[256,256]{1,0:T(8,128)(2,1)S(1)} collective-permute-done((bf16[256,256]{1,0:T(8,128)(2,1)S(1)}, bf16[256,256]{1,0:T(8,128)(2,1)S(1)}, u32[]{:S(2)}, u32[]{:S(2)}) %collective-permute-start.38) | collective-permute-done | bytes 131104 | tf_op jit(solution)/shard_map/ppermute | solution.py:315
  81.5 2.4 %collective-permute-start.42 = (bf16[256,256]{1,0:T(8,128)(2,1)S(1)}, bf16[256,256]{1,0:T(8,128)(2,1)S(1)}, u32[]{:S(2)}, u32[]{:S(2)}) collective-permute-start(bf16[256,256]{1,0:T(8,128)(2,1)S(1)} %get-tuple-element.120), channel_id=1, source_target_pairs={{0,24},{8,16},{16,8},{24,0},{1,25},{9,17},{17,9},{25,1},{2,26},{10... | collective-permute-start | bytes 393224 | tf_op jit(solution)/shard_map/ppermute | solution.py:315
  84.4 1.4 %collective-permute-done.33.refs_4_ = bf16[128,256]{1,0:T(8,128)(2,1)S(1)} collective-permute-done((bf16[128,256]{1,0:T(8,128)(2,1)S(1)}, bf16[128,256]{1,0:T(8,128)(2,1)S(1)}, u32[]{:S(2)}, u32[]{:S(2)}) %collective-permute-start.33) | collective-permute-done | bytes 65568 | tf_op jit(solution)/shard_map/ppermute | solution.py:315
  85.9 2.9 %shard_map.129 = (bf16[1024,1024]{1,0:T(8,128)(2,1)S(1)}, bf16[1024,1024]{1,0:T(8,128)(2,1)S(1)}, bf16[256,1024]{1,0:T(8,128)(2,1)S(1)}) custom-call(bf16[4,256,1024]{2,1,0:T(8,128)(2,1)S(1)} %get-tuple-element.67.win_ref, bf16[256,256]{1,0:T(8,128)(2,1)S(1)} %get-tuple-element.110.refs_0_, bf16[256,256]{1,0:T(8,128)(2,1)S(1)} %collective-permute-done.37.refs_1_, ...), custom_call_target="tpu_custom_call" | custom-call | flops 536870912 | bytes 6291456 | tf_op jit(solution)/shard_map/pallas_call | solution.py:302
  88.8 2.4 %collective-permute-done.34.refs_5_ = bf16[128,256]{1,0:T(8,128)(2,1)S(1)} collective-permute-done((bf16[128,256]{1,0:T(8,128)(2,1)S(1)}, bf16[128,256]{1,0:T(8,128)(2,1)S(1)}, u32[]{:S(2)}, u32[]{:S(2)}) %collective-permute-start.34) | collective-permute-done | bytes 65568 | tf_op jit(solution)/shard_map/ppermute | solution.py:315
  91.7 2.2 %collective-permute-start.22 = (bf16[512,256]{1,0:T(8,128)(2,1)S(1)}, bf16[512,256]{1,0:T(8,128)(2,1)S(1)}, u32[]{:S(2)}, u32[]{:S(2)}) collective-permute-start(bf16[512,256]{1,0:T(8,128)(2,1)S(1)} %get-tuple-element.90.refs_0_), channel_id=1, source_target_pairs={{0,24},{8,16},{16,8},{24,0},{1,25},{9,17},{17,9},{25,1},{2,26},{10... | collective-permute-start | bytes 786440 | tf_op jit(solution)/shard_map/ppermute | solution.py:315
  93.9 2.1 %collective-permute-start.35 = (bf16[128,256]{1,0:T(8,128)(2,1)S(1)}, bf16[128,256]{1,0:T(8,128)(2,1)S(1)}, u32[]{:S(2)}, u32[]{:S(2)}) collective-permute-start(bf16[128,256]{1,0:T(8,128)(2,1)S(1)} %get-tuple-element.108), channel_id=1, source_target_pairs={{0,6},{1,7},{2,4},{3,5},{4,2},{5,3},{6,0},{7,1},{8,14},{9,15},{10,... | collective-permute-start | bytes 196616 | tf_op jit(solution)/shard_map/ppermute | solution.py:315
  96.6 1.9 %shard_map.131 = (bf16[512,256]{1,0:T(8,128)(2,1)S(1)}, bf16[512,256]{1,0:T(8,128)(2,1)S(1)}, bf16[512,256]{1,0:T(8,128)(2,1)S(1)}, bf16[512,256]{1,0:T(8,128)(2,1)S(1)}) custom-call(bf16[4,1024,256]{2,1,0:T(8,128)(2,1)S(1)} %get-tuple-element.68.wout_ref, bf16[1024,1024]{1,0:T(8,128)(2,1)S(1)} %get-tuple-element.114.act_ref, ...), custom_call_target="tpu_custom_call" | custom-call | flops 1610612736 | bytes 6291456 | tf_op jit(solution)/shard_map/pallas_call | solution.py:302
  98.5 1.6 %collective-permute-done.35.refs_6_ = bf16[128,256]{1,0:T(8,128)(2,1)S(1)} collective-permute-done((bf16[128,256]{1,0:T(8,128)(2,1)S(1)}, bf16[128,256]{1,0:T(8,128)(2,1)S(1)}, u32[]{:S(2)}, u32[]{:S(2)}) %collective-permute-start.35) | collective-permute-done | bytes 65568 | tf_op jit(solution)/shard_map/ppermute | solution.py:315
  102.3 1.5 %collective-permute-start.45 = (bf16[512,256]{1,0:T(8,128)(2,1)S(1)}, bf16[512,256]{1,0:T(8,128)(2,1)S(1)}, u32[]{:S(2)}, u32[]{:S(2)}) collective-permute-start(bf16[512,256]{1,0:T(8,128)(2,1)S(1)} %get-tuple-element.124), channel_id=1, source_target_pairs={{0,24},{8,16},{16,8},{24,0},{1,25},{9,17},{17,9},{25,1},{2,26},{10... | collective-permute-start | bytes 786440 | tf_op jit(solution)/shard_map/ppermute | solution.py:315
  103.8 1.9 %shard_map.127 = f32[512,256]{1,0:T(8,128)} custom-call(bf16[512,256]{1,0:T(8,128)(2,1)S(1)} %bitcast.13, s32[1,512]{1,0:T(1,128)S(1)} %copy-done.5, f32[512,256]{1,0:T(8,128)S(1)} %get-tuple-element.93.summed_ref, bf16[128,256]{1,0:T(8,128)(2,1)S(1)} %get-tuple-element.102.refs_0_, bf16[128,256]{1,0:T(8,128)(2,1)S(1)} %collective-permute-done.30.refs_1_, ...), custom_call_target="tpu_custom_call" | custom-call | flops 268435456 | bytes 2097152 | tf_op jit(solution)/shard_map/pallas_call | solution.py:302
  105.7 3.0 %shard_map.124 = (f32[1,512]{1,0:T(1,128)}, f32[512,256]{1,0:T(8,128)}) custom-call(bf16[512,256]{1,0:T(8,128)(2,1)S(1)} %bitcast.10, s32[1,2048]{1,0:T(1,128)S(1)} %copy-done.6, f32[1,512]{1,0:T(1,128)S(1)} %get-tuple-element.89.lse_ref, f32[1,512]{1,0:T(1,128)S(1)} %copy-done.7, s32[1,512]{1,0:T(1,128)S(1)} %copy-done.8, ...), custom_call_target="tpu_custom_call" | custom-call | flops 1073741824 | bytes 3145728 | tf_op jit(solution)/shard_map/pallas_call | solution.py:302
  109.3 5.8 %collective-permute-done.44.refs_2_ = bf16[512,256]{1,0:T(8,128)(2,1)S(1)} collective-permute-done((bf16[512,256]{1,0:T(8,128)(2,1)S(1)}, bf16[512,256]{1,0:T(8,128)(2,1)S(1)}, u32[]{:S(2)}, u32[]{:S(2)}) %collective-permute-start.44) | collective-permute-done | bytes 262176 | tf_op jit(solution)/shard_map/ppermute | solution.py:315
  115.1 1.6 %shard_map.132 = (f32[64,4,1024]{2,1,0:T(4,128)}, f32[256,4,256]{2,1,0:T(4,128)}) custom-call(bf16[512,256]{1,0:T(8,128)(2,1)S(1)} %get-tuple-element.121.refs_0_, bf16[512,256]{1,0:T(8,128)(2,1)S(1)} %collective-permute-done.43.refs_1_, bf16[512,256]{1,0:T(8,128)(2,1)S(1)} %collective-permute-done.44.refs_2_, ...), custom_call_target="tpu_custom_call" | custom-call | flops 536870912 | bytes 6291456 | tf_op jit(solution)/shard_map/pallas_call | solution.py:302
  (76 shorter events, 10.8 us)
Async XLA Ops:
  2.8 6.0 %collective-permute-start = (bf16[128,256]{1,0:T(8,128)(2,1)}, bf16[128,256]{1,0:T(8,128)(2,1)S(1)}, u32[]{:S(2)}, u32[]{:S(2)}) collective-permute-start(bf16[128,256]{1,0:T(8,128)(2,1)} %get-tuple-element.70), channel_id=1, source_target_pairs={{0,1},{1,0},{2,3},{3,2},{4,5},{5,4},{6,7},{7,6},{8,9},{9,8},{10,11... | collective-permute-start | bytes 196616 | tf_op jit(solution)/shard_map/ppermute | solution.py:315
  3.4 9.1 %collective-permute-start.1 = (bf16[128,256]{1,0:T(8,128)(2,1)}, bf16[128,256]{1,0:T(8,128)(2,1)S(1)}, u32[]{:S(2)}, u32[]{:S(2)}) collective-permute-start(bf16[128,256]{1,0:T(8,128)(2,1)} %get-tuple-element.71), channel_id=1, source_target_pairs={{0,2},{1,3},{2,0},{3,1},{4,6},{5,7},{6,4},{7,5},{8,10},{9,11},{10,... | collective-permute-start | bytes 196616 | tf_op jit(solution)/shard_map/ppermute | solution.py:315
  6.0 10.0 %collective-permute-start.2 = (bf16[128,256]{1,0:T(8,128)(2,1)}, bf16[128,256]{1,0:T(8,128)(2,1)S(1)}, u32[]{:S(2)}, u32[]{:S(2)}) collective-permute-start(bf16[128,256]{1,0:T(8,128)(2,1)} %get-tuple-element.72), channel_id=1, source_target_pairs={{0,3},{1,2},{2,1},{3,0},{4,7},{5,6},{6,5},{7,4},{8,11},{9,10},{10,... | collective-permute-start | bytes 196616 | tf_op jit(solution)/shard_map/ppermute | solution.py:315
  6.0 10.0 %collective-permute-start.3 = (bf16[128,256]{1,0:T(8,128)(2,1)}, bf16[128,256]{1,0:T(8,128)(2,1)S(1)}, u32[]{:S(2)}, u32[]{:S(2)}) collective-permute-start(bf16[128,256]{1,0:T(8,128)(2,1)} %get-tuple-element.73), channel_id=1, source_target_pairs={{0,4},{1,5},{2,6},{3,7},{4,0},{5,1},{6,2},{7,3},{8,12},{9,13},{10,... | collective-permute-start | bytes 196616 | tf_op jit(solution)/shard_map/ppermute | solution.py:315
  8.8 10.7 %collective-permute-start.4 = (bf16[128,256]{1,0:T(8,128)(2,1)}, bf16[128,256]{1,0:T(8,128)(2,1)S(1)}, u32[]{:S(2)}, u32[]{:S(2)}) collective-permute-start(bf16[128,256]{1,0:T(8,128)(2,1)} %get-tuple-element.74), channel_id=1, source_target_pairs={{0,5},{1,4},{2,7},{3,6},{4,1},{5,0},{6,3},{7,2},{8,13},{9,12},{10,... | collective-permute-start | bytes 196616 | tf_op jit(solution)/shard_map/ppermute | solution.py:315
  8.8 10.7 %collective-permute-start.5 = (bf16[128,256]{1,0:T(8,128)(2,1)}, bf16[128,256]{1,0:T(8,128)(2,1)S(1)}, u32[]{:S(2)}, u32[]{:S(2)}) collective-permute-start(bf16[128,256]{1,0:T(8,128)(2,1)} %get-tuple-element.75), channel_id=1, source_target_pairs={{0,6},{1,7},{2,4},{3,5},{4,2},{5,3},{6,0},{7,1},{8,14},{9,15},{10,... | collective-permute-start | bytes 196616 | tf_op jit(solution)/shard_map/ppermute | solution.py:315
  12.4 7.1 %collective-permute-start.6 = (bf16[128,256]{1,0:T(8,128)(2,1)}, bf16[128,256]{1,0:T(8,128)(2,1)S(1)}, u32[]{:S(2)}, u32[]{:S(2)}) collective-permute-start(bf16[128,256]{1,0:T(8,128)(2,1)} %get-tuple-element.76), channel_id=1, source_target_pairs={{0,7},{1,6},{2,5},{3,4},{4,3},{5,2},{6,1},{7,0},{8,15},{9,14},{10,... | collective-permute-start | bytes 196616 | tf_op jit(solution)/shard_map/ppermute | solution.py:315
  19.5 27.0 %copy-start.4 = (bf16[1,512,256]{2,1,0:T(8,128)(2,1)S(1)}, bf16[1,512,256]{2,1,0:T(8,128)(2,1)}, u32[]{:S(2)}) copy-start(bf16[1,512,256]{2,1,0:T(8,128)(2,1)} %param.8) | copy-start | bytes 786436
  19.5 27.0 %copy-start.5 = (s32[1,512]{1,0:T(1,128)S(1)}, s32[1,512]{1,0:T(1,128)}, u32[]{:S(2)}) copy-start(s32[1,512]{1,0:T(1,128)} %get-tuple-element.66.slot_ref) | copy-start | bytes 6148
  21.3 7.0 %collective-permute-start.7 = (bf16[128,256]{1,0:T(8,128)(2,1)S(1)}, bf16[128,256]{1,0:T(8,128)(2,1)S(1)}, u32[]{:S(2)}, u32[]{:S(2)}) collective-permute-start(bf16[128,256]{1,0:T(8,128)(2,1)S(1)} %get-tuple-element.78), channel_id=1, source_target_pairs={{0,1},{1,0},{2,3},{3,2},{4,5},{5,4},{6,7},{7,6},{8,9},{9,8},{10,11... | collective-permute-start | bytes 196616 | tf_op jit(solution)/shard_map/ppermute | solution.py:315
  21.5 25.0 %collective-permute-start.14 = (bf16[512,256]{1,0:T(8,128)(2,1)S(1)}, bf16[512,256]{1,0:T(8,128)(2,1)S(1)}, u32[]{:S(2)}, u32[]{:S(2)}) collective-permute-start(bf16[512,256]{1,0:T(8,128)(2,1)S(1)} %bitcast.5), channel_id=1, source_target_pairs={{0,8},{8,0},{16,24},{24,16},{1,9},{9,1},{17,25},{25,17},{2,10},{10... | collective-permute-start | bytes 786440 | tf_op jit(solution)/shard_map/ppermute | solution.py:315
  23.0 23.5 %collective-permute-start.15 = (bf16[512,256]{1,0:T(8,128)(2,1)S(1)}, bf16[512,256]{1,0:T(8,128)(2,1)S(1)}, u32[]{:S(2)}, u32[]{:S(2)}) collective-permute-start(bf16[512,256]{1,0:T(8,128)(2,1)S(1)} %bitcast.6), channel_id=1, source_target_pairs={{0,16},{8,24},{16,0},{24,8},{1,17},{9,25},{17,1},{25,9},{2,18},{10... | collective-permute-start | bytes 786440 | tf_op jit(solution)/shard_map/ppermute | solution.py:315
  24.5 22.0 %collective-permute-start.16 = (bf16[512,256]{1,0:T(8,128)(2,1)S(1)}, bf16[512,256]{1,0:T(8,128)(2,1)S(1)}, u32[]{:S(2)}, u32[]{:S(2)}) collective-permute-start(bf16[512,256]{1,0:T(8,128)(2,1)S(1)} %bitcast.7), channel_id=1, source_target_pairs={{0,24},{8,16},{16,8},{24,0},{1,25},{9,17},{17,9},{25,1},{2,26},{10... | collective-permute-start | bytes 786440 | tf_op jit(solution)/shard_map/ppermute | solution.py:315
  25.0 5.6 %collective-permute-start.8 = (bf16[128,256]{1,0:T(8,128)(2,1)S(1)}, bf16[128,256]{1,0:T(8,128)(2,1)S(1)}, u32[]{:S(2)}, u32[]{:S(2)}) collective-permute-start(bf16[128,256]{1,0:T(8,128)(2,1)S(1)} %get-tuple-element.79), channel_id=1, source_target_pairs={{0,2},{1,3},{2,0},{3,1},{4,6},{5,7},{6,4},{7,5},{8,10},{9,11},{10,... | collective-permute-start | bytes 196616 | tf_op jit(solution)/shard_map/ppermute | solution.py:315
  28.3 5.6 %collective-permute-start.9 = (bf16[128,256]{1,0:T(8,128)(2,1)S(1)}, bf16[128,256]{1,0:T(8,128)(2,1)S(1)}, u32[]{:S(2)}, u32[]{:S(2)}) collective-permute-start(bf16[128,256]{1,0:T(8,128)(2,1)S(1)} %get-tuple-element.80), channel_id=1, source_target_pairs={{0,3},{1,2},{2,1},{3,0},{4,7},{5,6},{6,5},{7,4},{8,11},{9,10},{10,... | collective-permute-start | bytes 196616 | tf_op jit(solution)/shard_map/ppermute | solution.py:315
  30.5 5.6 %collective-permute-start.10 = (bf16[128,256]{1,0:T(8,128)(2,1)S(1)}, bf16[128,256]{1,0:T(8,128)(2,1)S(1)}, u32[]{:S(2)}, u32[]{:S(2)}) collective-permute-start(bf16[128,256]{1,0:T(8,128)(2,1)S(1)} %get-tuple-element.81), channel_id=1, source_target_pairs={{0,4},{1,5},{2,6},{3,7},{4,0},{5,1},{6,2},{7,3},{8,12},{9,13},{10,... | collective-permute-start | bytes 196616 | tf_op jit(solution)/shard_map/ppermute | solution.py:315
  33.9 6.6 %collective-permute-start.11 = (bf16[128,256]{1,0:T(8,128)(2,1)S(1)}, bf16[128,256]{1,0:T(8,128)(2,1)S(1)}, u32[]{:S(2)}, u32[]{:S(2)}) collective-permute-start(bf16[128,256]{1,0:T(8,128)(2,1)S(1)} %get-tuple-element.82), channel_id=1, source_target_pairs={{0,5},{1,4},{2,7},{3,6},{4,1},{5,0},{6,3},{7,2},{8,13},{9,12},{10,... | collective-permute-start | bytes 196616 | tf_op jit(solution)/shard_map/ppermute | solution.py:315
  36.1 6.2 %collective-permute-start.12 = (bf16[128,256]{1,0:T(8,128)(2,1)S(1)}, bf16[128,256]{1,0:T(8,128)(2,1)S(1)}, u32[]{:S(2)}, u32[]{:S(2)}) collective-permute-start(bf16[128,256]{1,0:T(8,128)(2,1)S(1)} %get-tuple-element.83), channel_id=1, source_target_pairs={{0,6},{1,7},{2,4},{3,5},{4,2},{5,3},{6,0},{7,1},{8,14},{9,15},{10,... | collective-permute-start | bytes 196616 | tf_op jit(solution)/shard_map/ppermute | solution.py:315
  40.4 6.0 %collective-permute-start.13 = (bf16[128,256]{1,0:T(8,128)(2,1)S(1)}, bf16[128,256]{1,0:T(8,128)(2,1)S(1)}, u32[]{:S(2)}, u32[]{:S(2)}) collective-permute-start(bf16[128,256]{1,0:T(8,128)(2,1)S(1)} %get-tuple-element.84), channel_id=1, source_target_pairs={{0,7},{1,6},{2,5},{3,4},{4,3},{5,2},{6,1},{7,0},{8,15},{9,14},{10,... | collective-permute-start | bytes 196616 | tf_op jit(solution)/shard_map/ppermute | solution.py:315
  49.2 4.0 %collective-permute-start.17 = (f32[10,512]{1,0:T(8,128)S(1)}, f32[10,512]{1,0:T(8,128)S(1)}, u32[]{:S(2)}, u32[]{:S(2)}) collective-permute-start(f32[10,512]{1,0:T(8,128)S(1)} %get-tuple-element.88.refs_4_), channel_id=1, source_target_pairs={{0,8},{8,0},{16,24},{24,16},{1,9},{9,1},{17,25},{25,17},{2,10},{10... | collective-permute-start | bytes 61448 | tf_op jit(solution)/shard_map/ppermute | solution.py:315
  50.8 3.9 %collective-permute-start.18 = (f32[10,512]{1,0:T(8,128)S(1)}, f32[10,512]{1,0:T(8,128)S(1)}, u32[]{:S(2)}, u32[]{:S(2)}) collective-permute-start(f32[10,512]{1,0:T(8,128)S(1)} %get-tuple-element.88.refs_4_), channel_id=1, source_target_pairs={{0,16},{8,24},{16,0},{24,8},{1,17},{9,25},{17,1},{25,9},{2,18},{10... | collective-permute-start | bytes 61448 | tf_op jit(solution)/shard_map/ppermute | solution.py:315
  52.3 4.8 %collective-permute-start.19 = (f32[10,512]{1,0:T(8,128)S(1)}, f32[10,512]{1,0:T(8,128)S(1)}, u32[]{:S(2)}, u32[]{:S(2)}) collective-permute-start(f32[10,512]{1,0:T(8,128)S(1)} %get-tuple-element.88.refs_4_), channel_id=1, source_target_pairs={{0,24},{8,16},{16,8},{24,0},{1,25},{9,17},{17,9},{25,1},{2,26},{10... | collective-permute-start | bytes 61448 | tf_op jit(solution)/shard_map/ppermute | solution.py:315
  58.8 4.5 %collective-permute-start.23 = (bf16[128,256]{1,0:T(8,128)(2,1)S(1)}, bf16[128,256]{1,0:T(8,128)(2,1)S(1)}, u32[]{:S(2)}, u32[]{:S(2)}) collective-permute-start(bf16[128,256]{1,0:T(8,128)(2,1)S(1)} %get-tuple-element.95), channel_id=1, source_target_pairs={{0,1},{1,0},{2,3},{3,2},{4,5},{5,4},{6,7},{7,6},{8,9},{9,8},{10,11... | collective-permute-start | bytes 196616 | tf_op jit(solution)/shard_map/ppermute | solution.py:315
  58.9 6.8 %collective-permute-start.24 = (bf16[128,256]{1,0:T(8,128)(2,1)S(1)}, bf16[128,256]{1,0:T(8,128)(2,1)S(1)}, u32[]{:S(2)}, u32[]{:S(2)}) collective-permute-start(bf16[128,256]{1,0:T(8,128)(2,1)S(1)} %get-tuple-element.96), channel_id=1, source_target_pairs={{0,2},{1,3},{2,0},{3,1},{4,6},{5,7},{6,4},{7,5},{8,10},{9,11},{10,... | collective-permute-start | bytes 196616 | tf_op jit(solution)/shard_map/ppermute | solution.py:315
  59.0 8.0 %collective-permute-start.25 = (bf16[128,256]{1,0:T(8,128)(2,1)S(1)}, bf16[128,256]{1,0:T(8,128)(2,1)S(1)}, u32[]{:S(2)}, u32[]{:S(2)}) collective-permute-start(bf16[128,256]{1,0:T(8,128)(2,1)S(1)} %get-tuple-element.97), channel_id=1, source_target_pairs={{0,3},{1,2},{2,1},{3,0},{4,7},{5,6},{6,5},{7,4},{8,11},{9,10},{10,... | collective-permute-start | bytes 196616 | tf_op jit(solution)/shard_map/ppermute | solution.py:315
  60.8 11.3 %collective-permute-start.26 = (bf16[128,256]{1,0:T(8,128)(2,1)S(1)}, bf16[128,256]{1,0:T(8,128)(2,1)S(1)}, u32[]{:S(2)}, u32[]{:S(2)}) collective-permute-start(bf16[128,256]{1,0:T(8,128)(2,1)S(1)} %get-tuple-element.98), channel_id=1, source_target_pairs={{0,4},{1,5},{2,6},{3,7},{4,0},{5,1},{6,2},{7,3},{8,12},{9,13},{10,... | collective-permute-start | bytes 196616 | tf_op jit(solution)/shard_map/ppermute | solution.py:315
  61.9 10.7 %collective-permute-start.27 = (bf16[128,256]{1,0:T(8,128)(2,1)S(1)}, bf16[128,256]{1,0:T(8,128)(2,1)S(1)}, u32[]{:S(2)}, u32[]{:S(2)}) collective-permute-start(bf16[128,256]{1,0:T(8,128)(2,1)S(1)} %get-tuple-element.99), channel_id=1, source_target_pairs={{0,5},{1,4},{2,7},{3,6},{4,1},{5,0},{6,3},{7,2},{8,13},{9,12},{10,... | collective-permute-start | bytes 196616 | tf_op jit(solution)/shard_map/ppermute | solution.py:315
  63.4 10.7 %collective-permute-start.28 = (bf16[128,256]{1,0:T(8,128)(2,1)S(1)}, bf16[128,256]{1,0:T(8,128)(2,1)S(1)}, u32[]{:S(2)}, u32[]{:S(2)}) collective-permute-start(bf16[128,256]{1,0:T(8,128)(2,1)S(1)} %get-tuple-element.100), channel_id=1, source_target_pairs={{0,6},{1,7},{2,4},{3,5},{4,2},{5,3},{6,0},{7,1},{8,14},{9,15},{10,... | collective-permute-start | bytes 196616 | tf_op jit(solution)/shard_map/ppermute | solution.py:315
  65.7 8.3 %collective-permute-start.29 = (bf16[128,256]{1,0:T(8,128)(2,1)S(1)}, bf16[128,256]{1,0:T(8,128)(2,1)S(1)}, u32[]{:S(2)}, u32[]{:S(2)}) collective-permute-start(bf16[128,256]{1,0:T(8,128)(2,1)S(1)} %get-tuple-element.101), channel_id=1, source_target_pairs={{0,7},{1,6},{2,5},{3,4},{4,3},{5,2},{6,1},{7,0},{8,15},{9,14},{10,... | collective-permute-start | bytes 196616 | tf_op jit(solution)/shard_map/ppermute | solution.py:315
  67.0 11.0 %collective-permute-start.37 = (bf16[256,256]{1,0:T(8,128)(2,1)S(1)}, bf16[256,256]{1,0:T(8,128)(2,1)S(1)}, u32[]{:S(2)}, u32[]{:S(2)}) collective-permute-start(bf16[256,256]{1,0:T(8,128)(2,1)S(1)} %get-tuple-element.111), channel_id=1, source_target_pairs={{0,8},{8,0},{16,24},{24,16},{1,9},{9,1},{17,25},{25,17},{2,10},{10... | collective-permute-start | bytes 393224 | tf_op jit(solution)/shard_map/ppermute | solution.py:315
  72.1 7.8 %collective-permute-start.38 = (bf16[256,256]{1,0:T(8,128)(2,1)S(1)}, bf16[256,256]{1,0:T(8,128)(2,1)S(1)}, u32[]{:S(2)}, u32[]{:S(2)}) collective-permute-start(bf16[256,256]{1,0:T(8,128)(2,1)S(1)} %get-tuple-element.112), channel_id=1, source_target_pairs={{0,16},{8,24},{16,0},{24,8},{1,17},{9,25},{17,1},{25,9},{2,18},{10... | collective-permute-start | bytes 393224 | tf_op jit(solution)/shard_map/ppermute | solution.py:315
  72.6 7.8 %collective-permute-start.39 = (bf16[256,256]{1,0:T(8,128)(2,1)S(1)}, bf16[256,256]{1,0:T(8,128)(2,1)S(1)}, u32[]{:S(2)}, u32[]{:S(2)}) collective-permute-start(bf16[256,256]{1,0:T(8,128)(2,1)S(1)} %get-tuple-element.113), channel_id=1, source_target_pairs={{0,24},{8,16},{16,8},{24,0},{1,25},{9,17},{17,9},{25,1},{2,26},{10... | collective-permute-start | bytes 393224 | tf_op jit(solution)/shard_map/ppermute | solution.py:315
  75.5 5.5 %collective-permute-start.30 = (bf16[128,256]{1,0:T(8,128)(2,1)S(1)}, bf16[128,256]{1,0:T(8,128)(2,1)S(1)}, u32[]{:S(2)}, u32[]{:S(2)}) collective-permute-start(bf16[128,256]{1,0:T(8,128)(2,1)S(1)} %get-tuple-element.103), channel_id=1, source_target_pairs={{0,1},{1,0},{2,3},{3,2},{4,5},{5,4},{6,7},{7,6},{8,9},{9,8},{10,11... | collective-permute-start | bytes 196616 | tf_op jit(solution)/shard_map/ppermute | solution.py:315
  75.5 5.9 %collective-permute-start.31 = (bf16[128,256]{1,0:T(8,128)(2,1)S(1)}, bf16[128,256]{1,0:T(8,128)(2,1)S(1)}, u32[]{:S(2)}, u32[]{:S(2)}) collective-permute-start(bf16[128,256]{1,0:T(8,128)(2,1)S(1)} %get-tuple-element.104), channel_id=1, source_target_pairs={{0,2},{1,3},{2,0},{3,1},{4,6},{5,7},{6,4},{7,5},{8,10},{9,11},{10,... | collective-permute-start | bytes 196616 | tf_op jit(solution)/shard_map/ppermute | solution.py:315
  78.0 5.9 %collective-permute-start.32 = (bf16[128,256]{1,0:T(8,128)(2,1)S(1)}, bf16[128,256]{1,0:T(8,128)(2,1)S(1)}, u32[]{:S(2)}, u32[]{:S(2)}) collective-permute-start(bf16[128,256]{1,0:T(8,128)(2,1)S(1)} %get-tuple-element.105), channel_id=1, source_target_pairs={{0,3},{1,2},{2,1},{3,0},{4,7},{5,6},{6,5},{7,4},{8,11},{9,10},{10,... | collective-permute-start | bytes 196616 | tf_op jit(solution)/shard_map/ppermute | solution.py:315
  79.8 6.0 %collective-permute-start.33 = (bf16[128,256]{1,0:T(8,128)(2,1)S(1)}, bf16[128,256]{1,0:T(8,128)(2,1)S(1)}, u32[]{:S(2)}, u32[]{:S(2)}) collective-permute-start(bf16[128,256]{1,0:T(8,128)(2,1)S(1)} %get-tuple-element.106), channel_id=1, source_target_pairs={{0,4},{1,5},{2,6},{3,7},{4,0},{5,1},{6,2},{7,3},{8,12},{9,13},{10,... | collective-permute-start | bytes 196616 | tf_op jit(solution)/shard_map/ppermute | solution.py:315
  80.4 11.3 %collective-permute-start.40 = (bf16[256,256]{1,0:T(8,128)(2,1)S(1)}, bf16[256,256]{1,0:T(8,128)(2,1)S(1)}, u32[]{:S(2)}, u32[]{:S(2)}) collective-permute-start(bf16[256,256]{1,0:T(8,128)(2,1)S(1)} %get-tuple-element.118), channel_id=1, source_target_pairs={{0,8},{8,0},{16,24},{24,16},{1,9},{9,1},{17,25},{25,17},{2,10},{10... | collective-permute-start | bytes 393224 | tf_op jit(solution)/shard_map/ppermute | solution.py:315
  80.9 13.0 %collective-permute-start.41 = (bf16[256,256]{1,0:T(8,128)(2,1)S(1)}, bf16[256,256]{1,0:T(8,128)(2,1)S(1)}, u32[]{:S(2)}, u32[]{:S(2)}) collective-permute-start(bf16[256,256]{1,0:T(8,128)(2,1)S(1)} %get-tuple-element.119), channel_id=1, source_target_pairs={{0,16},{8,24},{16,0},{24,8},{1,17},{9,25},{17,1},{25,9},{2,18},{10... | collective-permute-start | bytes 393224 | tf_op jit(solution)/shard_map/ppermute | solution.py:315
  81.5 14.6 %collective-permute-start.42 = (bf16[256,256]{1,0:T(8,128)(2,1)S(1)}, bf16[256,256]{1,0:T(8,128)(2,1)S(1)}, u32[]{:S(2)}, u32[]{:S(2)}) collective-permute-start(bf16[256,256]{1,0:T(8,128)(2,1)S(1)} %get-tuple-element.120), channel_id=1, source_target_pairs={{0,24},{8,16},{16,8},{24,0},{1,25},{9,17},{17,9},{25,1},{2,26},{10... | collective-permute-start | bytes 393224 | tf_op jit(solution)/shard_map/ppermute | solution.py:315
  83.9 18.4 %collective-permute-start.20 = (bf16[512,256]{1,0:T(8,128)(2,1)S(1)}, bf16[512,256]{1,0:T(8,128)(2,1)S(1)}, u32[]{:S(2)}, u32[]{:S(2)}) collective-permute-start(bf16[512,256]{1,0:T(8,128)(2,1)S(1)} %get-tuple-element.90.refs_0_), channel_id=1, source_target_pairs={{0,8},{8,0},{16,24},{24,16},{1,9},{9,1},{17,25},{25,17},{2,10},{10... | collective-permute-start | bytes 786440 | tf_op jit(solution)/shard_map/ppermute | solution.py:315
  85.9 5.3 %collective-permute-start.34 = (bf16[128,256]{1,0:T(8,128)(2,1)S(1)}, bf16[128,256]{1,0:T(8,128)(2,1)S(1)}, u32[]{:S(2)}, u32[]{:S(2)}) collective-permute-start(bf16[128,256]{1,0:T(8,128)(2,1)S(1)} %get-tuple-element.107), channel_id=1, source_target_pairs={{0,5},{1,4},{2,7},{3,6},{4,1},{5,0},{6,3},{7,2},{8,13},{9,12},{10,... | collective-permute-start | bytes 196616 | tf_op jit(solution)/shard_map/ppermute | solution.py:315
  91.2 14.6 %collective-permute-start.21 = (bf16[512,256]{1,0:T(8,128)(2,1)S(1)}, bf16[512,256]{1,0:T(8,128)(2,1)S(1)}, u32[]{:S(2)}, u32[]{:S(2)}) collective-permute-start(bf16[512,256]{1,0:T(8,128)(2,1)S(1)} %get-tuple-element.90.refs_0_), channel_id=1, source_target_pairs={{0,16},{8,24},{16,0},{24,8},{1,17},{9,25},{17,1},{25,9},{2,18},{10... | collective-permute-start | bytes 786440 | tf_op jit(solution)/shard_map/ppermute | solution.py:315
  91.7 14.0 %collective-permute-start.22 = (bf16[512,256]{1,0:T(8,128)(2,1)S(1)}, bf16[512,256]{1,0:T(8,128)(2,1)S(1)}, u32[]{:S(2)}, u32[]{:S(2)}) collective-permute-start(bf16[512,256]{1,0:T(8,128)(2,1)S(1)} %get-tuple-element.90.refs_0_), channel_id=1, source_target_pairs={{0,24},{8,16},{16,8},{24,0},{1,25},{9,17},{17,9},{25,1},{2,26},{10... | collective-permute-start | bytes 786440 | tf_op jit(solution)/shard_map/ppermute | solution.py:315
  93.9 6.2 %collective-permute-start.35 = (bf16[128,256]{1,0:T(8,128)(2,1)S(1)}, bf16[128,256]{1,0:T(8,128)(2,1)S(1)}, u32[]{:S(2)}, u32[]{:S(2)}) collective-permute-start(bf16[128,256]{1,0:T(8,128)(2,1)S(1)} %get-tuple-element.108), channel_id=1, source_target_pairs={{0,6},{1,7},{2,4},{3,5},{4,2},{5,3},{6,0},{7,1},{8,14},{9,15},{10,... | collective-permute-start | bytes 196616 | tf_op jit(solution)/shard_map/ppermute | solution.py:315
  96.0 5.6 %collective-permute-start.36 = (bf16[128,256]{1,0:T(8,128)(2,1)S(1)}, bf16[128,256]{1,0:T(8,128)(2,1)S(1)}, u32[]{:S(2)}, u32[]{:S(2)}) collective-permute-start(bf16[128,256]{1,0:T(8,128)(2,1)S(1)} %get-tuple-element.109), channel_id=1, source_target_pairs={{0,7},{1,6},{2,5},{3,4},{4,3},{5,2},{6,1},{7,0},{8,15},{9,14},{10,... | collective-permute-start | bytes 196616 | tf_op jit(solution)/shard_map/ppermute | solution.py:315
  100.1 9.2 %collective-permute-start.43 = (bf16[512,256]{1,0:T(8,128)(2,1)S(1)}, bf16[512,256]{1,0:T(8,128)(2,1)S(1)}, u32[]{:S(2)}, u32[]{:S(2)}) collective-permute-start(bf16[512,256]{1,0:T(8,128)(2,1)S(1)} %get-tuple-element.122), channel_id=1, source_target_pairs={{0,8},{8,0},{16,24},{24,16},{1,9},{9,1},{17,25},{25,17},{2,10},{10... | collective-permute-start | bytes 786440 | tf_op jit(solution)/shard_map/ppermute | solution.py:315
  101.7 13.4 %collective-permute-start.44 = (bf16[512,256]{1,0:T(8,128)(2,1)S(1)}, bf16[512,256]{1,0:T(8,128)(2,1)S(1)}, u32[]{:S(2)}, u32[]{:S(2)}) collective-permute-start(bf16[512,256]{1,0:T(8,128)(2,1)S(1)} %get-tuple-element.123), channel_id=1, source_target_pairs={{0,16},{8,24},{16,0},{24,8},{1,17},{9,25},{17,1},{25,9},{2,18},{10... | collective-permute-start | bytes 786440 | tf_op jit(solution)/shard_map/ppermute | solution.py:315
  102.3 12.8 %collective-permute-start.45 = (bf16[512,256]{1,0:T(8,128)(2,1)S(1)}, bf16[512,256]{1,0:T(8,128)(2,1)S(1)}, u32[]{:S(2)}, u32[]{:S(2)}) collective-permute-start(bf16[512,256]{1,0:T(8,128)(2,1)S(1)} %get-tuple-element.124), channel_id=1, source_target_pairs={{0,24},{8,16},{16,8},{24,0},{1,25},{9,17},{17,9},{25,1},{2,26},{10... | collective-permute-start | bytes 786440 | tf_op jit(solution)/shard_map/ppermute | solution.py:315
  (7 other events, 89.8 us)
where the time goes:
time: 117 us
  starting transfers between devices  53.8 us (46%)
  waiting for transfers between devices  34.8 us (30%)
  Pallas kernels  23.9 us (20%)
  local copies, waits for them, and re-layouts  3.22 us (3%)
    ppermute x46, starting transfers between devices, shift_by(): return lax.ppermute(values, axis, [(i, i ^ s) for i in range(n)])  53.8 us
    ppermute x46, waiting for transfers between devices, shift_by(): return lax.ppermute(values, axis, [(i, i ^ s) for i in range(n)])  34.8 us
    pallas_call x14, Pallas kernels, call(): pl.pallas_call(body, out_shape=shapes, in_specs=[pl.BlockSpec(memory_spac...  23.9 us
    unnamed x18, local copies, waits for them, and re-layouts  3.22 us
  transfers between devices with their start and end apart: 46, of which 17 were waited for; matrix products, arithmetic and copies ran while one was open for 0% of the time, Pallas kernels for 12%

commit v1 on v0

--- a/solution.py
+++ b/solution.py
@@ -53,12 +53,8 @@
     return jnp.where(iota((rows, slot_row.shape[1]), 0) + block * rows == slot_row, 1.0, 0.0).astype(BF)
 
 
-def gather_rows(slot_row, blocks):
-    col = to_col(slot_row).astype(jnp.int32)
-    n, rows = slot_row.shape[1], blocks[0].shape[0]
-    total = jnp.concatenate([b[...] for b in blocks], axis=0)
-    pick = jnp.where(iota((n, rows * len(blocks)), 1) == col, 1.0, 0.0).astype(BF)
-    return dg(pick, total, 1, 0)
+def gather_rows(pick_ref, blocks):
+    return dg(pick_ref[...], jnp.concatenate([b[...] for b in blocks], axis=0), 1, 0)
 
 
 def inv_rms_of(x):
@@ -93,13 +89,21 @@
         blocks[s][...] = dg(scatter_matrix(slot, s, rows), normed, 1, 0).astype(BF)
 
 
-def load_kernel(win_hbm, wout_hbm, win_ref, wout_ref, in_sem, out_sem):
+def load_kernel(
+    win_hbm, wout_hbm, slot_ref, counts_ref, win_ref, wout_ref, pick_ref, put_ref, logs_ref, in_sem, out_sem
+):
     copies = (
         pltpu.make_async_copy(win_hbm, win_ref, in_sem),
         pltpu.make_async_copy(wout_hbm, wout_ref, out_sem),
     )
     for copy in copies:
         copy.start()
+    slot = slot_ref[...]
+    col = to_col(slot).astype(jnp.int32)
+    pick_ref[...] = jnp.where(iota(pick_ref.shape, 1) == col, 1.0, 0.0).astype(BF)
+    put_ref[...] = scatter_matrix(slot, 0, put_ref.shape[0])
+    logs = log_counts_col(counts_ref, lax.axis_index("dp"), slot.shape[1])
+    logs_ref[...] = jnp.broadcast_to(logs, logs_ref.shape)
     for copy in copies:
         copy.wait()
 
@@ -139,12 +143,11 @@
     return jnp.log(to_col(part))
 
 
-def unit_kernel(groups, shards, feats_ref, slot_ref, counts_ref, w_ref, pos_ref, *refs):
+def unit_kernel(groups, shards, feats_ref, pick_ref, logs_ref, w_ref, pos_ref, *refs):
     blocks = refs[:groups]
     queries = refs[groups : groups + shards]
     low_ref, unit_ref, length_ref, stats_ref, terms_ref = refs[groups + shards :]
-    rows = feats_ref.shape[0]
-    branch = gather_rows(slot_ref[...], blocks)
+    branch = gather_rows(pick_ref, blocks)
     summed = feats_ref[...].astype(F32) + branch
     length = jnp.sqrt(jnp.sum(summed * summed, axis=1, keepdims=True) + norm_eps)
     unit = summed / length
@@ -152,7 +155,7 @@
     low_ref[...] = low
     unit_ref[...] = unit
     length_ref[...] = jnp.broadcast_to(length, length_ref.shape)
-    logs = log_counts_col(counts_ref, lax.axis_index("dp"), rows)
+    logs = logs_ref[:, 0:1]
     for s in range(shards):
         scores = dg(low, queries[s][...], 1, 1) - logs
         high = jnp.max(scores, axis=0, keepdims=True)
@@ -164,7 +167,7 @@
     stats_ref[2 * shards + 1 : 2 * shards + 2, :] = pos_ref[...].astype(F32)
 
 
-def grad_kernel(groups, shards, slot_ref, unit_ref, length_ref, terms_ref, *refs):
+def grad_kernel(groups, shards, put_ref, unit_ref, length_ref, terms_ref, *refs):
     queries = refs[:shards]
     stats = refs[shards : 2 * shards]
     summed_ref, lse_ref = refs[2 * shards : 2 * shards + 2]
@@ -190,9 +193,9 @@
     summed = (total - unit * along) / length_ref[:, 0:1]
     summed_ref[...] = summed
     low_grad = summed.astype(BF)
-    slot = slot_ref[...]
+    size = outs[0].shape[0]
     for s in range(groups):
-        outs[s][...] = dg(scatter_matrix(slot, s, outs[s].shape[0]), low_grad, 1, 0).astype(BF)
+        outs[s][...] = dg(put_ref[s * size : (s + 1) * size, :], low_grad, 1, 0).astype(BF)
 
 
 def turned(row):
@@ -288,25 +291,26 @@
         out_ref[first : first + in_rows] = block.reshape(in_rows, experts, width)
 
 
-def final_kernel(groups, feats_ref, slot_ref, summed_ref, *refs):
+def final_kernel(groups, feats_ref, pick_ref, summed_ref, *refs):
     blocks, out_ref = refs[:groups], refs[groups]
     x = feats_ref[...].astype(F32)
     r = inv_rms_of(x)
-    rows = gather_rows(slot_ref[...], blocks)
+    rows = gather_rows(pick_ref, blocks)
     projected = jnp.mean(rows * x, axis=1, keepdims=True)
     out_ref[...] = summed_ref[...] + r * (rows - x * (r * r) * projected)
 
 
-def call(body, outs, args, flops=0, touched=0, trans=0, scratch=(), space=pltpu.VMEM, limit=24):
+def call(body, outs, args, flops=0, touched=0, trans=0, scratch=(), space=pltpu.VMEM):
     shapes = [jax.ShapeDtypeStruct(s, d) for s, d in outs]
+    spaces = space if isinstance(space, list) else [space] * len(args)
     return pl.pallas_call(
         body,
         out_shape=shapes,
-        in_specs=[pl.BlockSpec(memory_space=space)] * len(args),
+        in_specs=[pl.BlockSpec(memory_space=m) for m in spaces],
         out_specs=[pl.BlockSpec(memory_space=pltpu.VMEM)] * len(outs),
         scratch_shapes=list(scratch),
         cost_estimate=pl.CostEstimate(flops=flops, bytes_accessed=touched, transcendentals=trans),
-        compiler_params=pltpu.CompilerParams(vmem_limit_bytes=limit << 20),
+        compiler_params=pltpu.CompilerParams(vmem_limit_bytes=24 << 20),
     )(*args)
 
 
@@ -341,7 +345,7 @@
     slot, *packed = call(
         functools.partial(pack_kernel, local_experts, experts_all, groups),
         [((1, rows), jnp.int32)] + [block] * groups,
-        (ids, feats),
+        [pltpu.with_memory_space_constraint(v, pltpu.HBM) for v in (ids, feats)],
         flops=2 * groups * slots * rows * width,
         touched=1 << 20,
         scratch=[
@@ -351,17 +355,27 @@
             pltpu.SemaphoreType.DMA(()),
         ],
         space=pltpu.HBM,
-        limit=60,
     )
     received = exchange(packed, "expert")
     all_queries = spread(query, "dp")
-    weight_in, weight_out = call(
+    weight_in, weight_out, pick, put, logs = call(
         load_kernel,
-        [(weight_in.shape, BF), (weight_out.shape, BF)],
-        (weight_in, weight_out),
+        [
+            (weight_in.shape, BF),
+            (weight_out.shape, BF),
+            ((rows, groups * slots), BF),
+            ((groups * slots, rows), BF),
+            ((rows, 128), F32),
+        ],
+        (
+            pltpu.with_memory_space_constraint(weight_in, pltpu.HBM),
+            pltpu.with_memory_space_constraint(weight_out, pltpu.HBM),
+            slot,
+            sample_counts,
+        ),
         touched=16 << 20,
         scratch=[pltpu.SemaphoreType.DMA(()), pltpu.SemaphoreType.DMA(())],
-        space=pltpu.HBM,
+        space=[pltpu.HBM, pltpu.HBM, pltpu.VMEM, pltpu.VMEM],
     )
     output = call(
         functools.partial(forward_kernel, groups),
@@ -389,7 +403,7 @@
             ((2 * shards + 2, q_rows), F32),
             ((shards, rows, q_rows), F32),
         ],
-        (feats, slot, sample_counts, query_weight, positives, *returned, *all_queries),
+        (feats, pick, logs, query_weight, positives, *returned, *all_queries),
         flops=2 * matmul,
         touched=4 << 20,
         trans=rows * q_rows * shards,
@@ -398,7 +412,7 @@
     summed, lse, *packed_grads = call(
         functools.partial(grad_kernel, groups, shards),
         [((rows, width), F32), ((1, q_rows), F32)] + [block] * groups,
-        (slot, unit, length, terms, *all_queries, *all_stats),
+        (put, unit, length, terms, *all_queries, *all_stats),
         flops=3 * matmul,
         touched=4 << 20,
         trans=rows * q_rows * shards,
@@ -425,7 +439,7 @@
     (grad_items,) = call(
         functools.partial(final_kernel, groups),
         [((rows, width), F32)],
-        (feats, slot, summed, *grad_back),
+        (feats, pick, summed, *grad_back),
         flops=2 * groups * slots * rows * width,
         touched=2 << 20,
     )

time: 117 us -> 117 us (level)
  waiting for transfers between devices: 34.8 us -> 37.3 us
  local copies, waits for them, and re-layouts: 3.22 us -> 0.73 us
    unnamed x18 -> x12, local copies, waits for them, and re-layouts: 3.22 us -> 0.73 us
    ppermute x46, waiting for transfers between devices: 34.8 us -> 37.3 us  [shift_by(): return lax.ppermute(values, axis, [(i, i ^ s) for i in range(n)])]
  transfers between devices with their start and end apart: 46 -> 46, of which waited for: 17 -> 16; matrix products, arithmetic and copies ran while one was open for 0% -> 0% of each run, Pallas kernels for 12% -> 13%
where the time goes in v1:
time: 117 us; the launch traced here: 116 us
  starting transfers between devices  53.3 us (46%)
  waiting for transfers between devices  37.3 us (32%)
  Pallas kernels  24.2 us (21%)
    ppermute x46, starting transfers between devices, shift_by(): return lax.ppermute(values, axis, [(i, i ^ s) for i in range(n)])  53.3 us
    ppermute x46, waiting for transfers between devices, shift_by(): return lax.ppermute(values, axis, [(i, i ^ s) for i in range(n)])  37.3 us
    pallas_call x14, Pallas kernels, call(): pl.pallas_call(body, out_shape=shapes, in_specs=[pl.BlockSpec(memory_spac...  24.2 us
  transfers between devices with their start and end apart: 46, of which 16 were waited for; matrix products, arithmetic and copies ran while one was open for 0% of the time, Pallas kernels for 13%

profile of v1, /device:TPU:0, one launch (start us, length us, event | category | flops | bytes accessed | tf_op | source)
XLA Modules:
  0.0 116.4 jit_solution(1199173576226588478)
XLA Ops:
  0.6 1.5 %shard_map.119 = (s32[1,512]{1,0:T(1,128)S(1)}, bf16[128,256]{1,0:T(8,128)(2,1)S(1)}, bf16[128,256]{1,0:T(8,128)(2,1)S(1)}, bf16[128,256]{1,0:T(8,128)(2,1)S(1)}...) custom-call(s32[1,512]{1,0:T(1,128)} %bitcast.15, ...), custom_call_target="tpu_custom_call" | custom-call | flops 268435456 | bytes 1048576 | tf_op jit(solution)/shard_map/pallas_call | solution.py:306
  2.7 2.6 %collective-permute-start.1 = (bf16[128,256]{1,0:T(8,128)(2,1)S(1)}, bf16[128,256]{1,0:T(8,128)(2,1)S(1)}, u32[]{:S(2)}, u32[]{:S(2)}) collective-permute-start(bf16[128,256]{1,0:T(8,128)(2,1)S(1)} %get-tuple-element.77), channel_id=1, source_target_pairs={{0,2},{1,3},{2,0},{3,1},{4,6},{5,7},{6,4},{7,5},{8,10},{9,11},{10,... | collective-permute-start | bytes 196616 | tf_op jit(solution)/shard_map/ppermute | solution.py:319
  5.4 2.8 %collective-permute-start.3 = (bf16[128,256]{1,0:T(8,128)(2,1)S(1)}, bf16[128,256]{1,0:T(8,128)(2,1)S(1)}, u32[]{:S(2)}, u32[]{:S(2)}) collective-permute-start(bf16[128,256]{1,0:T(8,128)(2,1)S(1)} %get-tuple-element.79), channel_id=1, source_target_pairs={{0,4},{1,5},{2,6},{3,7},{4,0},{5,1},{6,2},{7,3},{8,12},{9,13},{10,... | collective-permute-start | bytes 196616 | tf_op jit(solution)/shard_map/ppermute | solution.py:319
  8.2 3.6 %collective-permute-start.5 = (bf16[128,256]{1,0:T(8,128)(2,1)S(1)}, bf16[128,256]{1,0:T(8,128)(2,1)S(1)}, u32[]{:S(2)}, u32[]{:S(2)}) collective-permute-start(bf16[128,256]{1,0:T(8,128)(2,1)S(1)} %get-tuple-element.81), channel_id=1, source_target_pairs={{0,6},{1,7},{2,4},{3,5},{4,2},{5,3},{6,0},{7,1},{8,14},{9,15},{10,... | collective-permute-start | bytes 196616 | tf_op jit(solution)/shard_map/ppermute | solution.py:319
  11.9 0.7 copy-done.2
  12.6 2.2 %shard_map.120 = (bf16[4,256,1024]{2,1,0:T(8,128)(2,1)S(1)}, bf16[4,1024,256]{2,1,0:T(8,128)(2,1)S(1)}, bf16[512,1024]{1,0:T(8,128)(2,1)S(1)}, bf16[1024,512]{1,0:T(8,128)(2,1)S(1)}, f32[512,128]{1,0:T(8,128)S(1)}) custom-call(bf16[4,256,1024]{2,1,0:T(8,128)(2,1)} %win_hbm.1, bf16[4,1024,256]{2,1,0:T(8,128)(2,1)} %wout_hbm.1, ...), custom_call_target="tpu_custom_call" | custom-call | bytes 16777216 | tf_op jit(solution)/shard_map/pallas_call | solution.py:306
  14.9 3.8 %collective-permute-done.4.refs_5_ = bf16[128,256]{1,0:T(8,128)(2,1)S(1)} collective-permute-done((bf16[128,256]{1,0:T(8,128)(2,1)S(1)}, bf16[128,256]{1,0:T(8,128)(2,1)S(1)}, u32[]{:S(2)}, u32[]{:S(2)}) %collective-permute-start.4) | collective-permute-done | bytes 65568 | tf_op jit(solution)/shard_map/ppermute | solution.py:319
  18.7 1.7 %shard_map.121 = (bf16[128,256]{1,0:T(8,128)(2,1)S(1)}, bf16[128,256]{1,0:T(8,128)(2,1)S(1)}, bf16[128,256]{1,0:T(8,128)(2,1)S(1)}, bf16[128,256]{1,0:T(8,128)(2...) custom-call(bf16[4,256,1024]{2,1,0:T(8,128)(2,1)S(1)} %get-tuple-ele, ...), custom_call_target="tpu_custom_call" | custom-call | flops 1073741824 | bytes 6291456 | tf_op jit(solution)/shard_map/pallas_call | solution.py:306
  20.4 4.6 %collective-permute-start.10 = (bf16[128,256]{1,0:T(8,128)(2,1)S(1)}, bf16[128,256]{1,0:T(8,128)(2,1)S(1)}, u32[]{:S(2)}, u32[]{:S(2)}) collective-permute-start(bf16[128,256]{1,0:T(8,128)(2,1)S(1)} %get-tuple-element.87), channel_id=1, source_target_pairs={{0,4},{1,5},{2,6},{3,7},{4,0},{5,1},{6,2},{7,3},{8,12},{9,13},{10,... | collective-permute-start | bytes 196616 | tf_op jit(solution)/shard_map/ppermute | solution.py:319
  25.0 1.5 %collective-permute-start.14 = (bf16[512,256]{1,0:T(8,128)(2,1)S(1)}, bf16[512,256]{1,0:T(8,128)(2,1)S(1)}, u32[]{:S(2)}, u32[]{:S(2)}) collective-permute-start(bf16[512,256]{1,0:T(8,128)(2,1)S(1)} %bitcast.5), channel_id=1, source_target_pairs={{0,8},{8,0},{16,24},{24,16},{1,9},{9,1},{17,25},{25,17},{2,10},{10... | collective-permute-start | bytes 786440 | tf_op jit(solution)/shard_map/ppermute | solution.py:319
  26.5 1.5 %collective-permute-start.15 = (bf16[512,256]{1,0:T(8,128)(2,1)S(1)}, bf16[512,256]{1,0:T(8,128)(2,1)S(1)}, u32[]{:S(2)}, u32[]{:S(2)}) collective-permute-start(bf16[512,256]{1,0:T(8,128)(2,1)S(1)} %bitcast.6), channel_id=1, source_target_pairs={{0,16},{8,24},{16,0},{24,8},{1,17},{9,25},{17,1},{25,9},{2,18},{10... | collective-permute-start | bytes 786440 | tf_op jit(solution)/shard_map/ppermute | solution.py:319
  28.8 0.9 collective-permute-start.12
  29.7 5.5 %collective-permute-done.11.refs_5_ = bf16[128,256]{1,0:T(8,128)(2,1)S(1)} collective-permute-done((bf16[128,256]{1,0:T(8,128)(2,1)S(1)}, bf16[128,256]{1,0:T(8,128)(2,1)S(1)}, u32[]{:S(2)}, u32[]{:S(2)}) %collective-permute-start.11) | collective-permute-done | bytes 65568 | tf_op jit(solution)/shard_map/ppermute | solution.py:319
  35.2 2.6 %collective-permute-start.7 = (bf16[128,256]{1,0:T(8,128)(2,1)S(1)}, bf16[128,256]{1,0:T(8,128)(2,1)S(1)}, u32[]{:S(2)}, u32[]{:S(2)}) collective-permute-start(bf16[128,256]{1,0:T(8,128)(2,1)S(1)} %get-tuple-element.84), channel_id=1, source_target_pairs={{0,1},{1,0},{2,3},{3,2},{4,5},{5,4},{6,7},{7,6},{8,9},{9,8},{10,11... | collective-permute-start | bytes 196616 | tf_op jit(solution)/shard_map/ppermute | solution.py:319
  37.8 2.9 %collective-permute-done.13.refs_7_ = bf16[128,256]{1,0:T(8,128)(2,1)S(1)} collective-permute-done((bf16[128,256]{1,0:T(8,128)(2,1)S(1)}, bf16[128,256]{1,0:T(8,128)(2,1)S(1)}, u32[]{:S(2)}, u32[]{:S(2)}) %collective-permute-start.13) | collective-permute-done | bytes 65568 | tf_op jit(solution)/shard_map/ppermute | solution.py:319
  41.1 4.0 %collective-permute-done.8.refs_2_ = bf16[128,256]{1,0:T(8,128)(2,1)S(1)} collective-permute-done((bf16[128,256]{1,0:T(8,128)(2,1)S(1)}, bf16[128,256]{1,0:T(8,128)(2,1)S(1)}, u32[]{:S(2)}, u32[]{:S(2)}) %collective-permute-start.8) | collective-permute-done | bytes 65568 | tf_op jit(solution)/shard_map/ppermute | solution.py:319
  45.1 2.3 %shard_map.122 = (bf16[512,256]{1,0:T(8,128)(2,1)S(1)}, f32[512,256]{1,0:T(8,128)S(1)}, f32[512,128]{1,0:T(8,128)S(1)}, f32[10,512]{1,0:T(8,128)S(1)}, f32[4,512,512]{2,1,0:T(8,128)S(1)}) custom-call(bf16[512,256]{1,0:T(8,128)(2,1)S(1)} %bitcast.12, bf16[512,1024]{1,0:T(8,128)(2,1)S(1)} %get-tuple-element.71.pick_ref, ...), custom_call_target="tpu_custom_call" | custom-call | flops 1073741824 | bytes 4194304 | tf_op jit(solution)/shard_map/pallas_call | solution.py:306
  47.4 1.5 %collective-permute-start.17 = (f32[10,512]{1,0:T(8,128)S(1)}, f32[10,512]{1,0:T(8,128)S(1)}, u32[]{:S(2)}, u32[]{:S(2)}) collective-permute-start(f32[10,512]{1,0:T(8,128)S(1)} %get-tuple-element.94.refs_4_), channel_id=1, source_target_pairs={{0,8},{8,0},{16,24},{24,16},{1,9},{9,1},{17,25},{25,17},{2,10},{10... | collective-permute-start | bytes 61448 | tf_op jit(solution)/shard_map/ppermute | solution.py:319
  48.9 1.5 %collective-permute-start.18 = (f32[10,512]{1,0:T(8,128)S(1)}, f32[10,512]{1,0:T(8,128)S(1)}, u32[]{:S(2)}, u32[]{:S(2)}) collective-permute-start(f32[10,512]{1,0:T(8,128)S(1)} %get-tuple-element.94.refs_4_), channel_id=1, source_target_pairs={{0,16},{8,24},{16,0},{24,8},{1,17},{9,25},{17,1},{25,9},{2,18},{10... | collective-permute-start | bytes 61448 | tf_op jit(solution)/shard_map/ppermute | solution.py:319
  51.4 1.5 %collective-permute-done.18.refs_6_ = f32[10,512]{1,0:T(8,128)S(1)} collective-permute-done((f32[10,512]{1,0:T(8,128)S(1)}, f32[10,512]{1,0:T(8,128)S(1)}, u32[]{:S(2)}, u32[]{:S(2)}) %collective-permute-start.18) | collective-permute-done | bytes 20512 | tf_op jit(solution)/shard_map/ppermute | solution.py:319
  52.8 2.4 %collective-permute-done.19.refs_7_ = f32[10,512]{1,0:T(8,128)S(1)} collective-permute-done((f32[10,512]{1,0:T(8,128)S(1)}, f32[10,512]{1,0:T(8,128)S(1)}, u32[]{:S(2)}, u32[]{:S(2)}) %collective-permute-start.19) | collective-permute-done | bytes 20512 | tf_op jit(solution)/shard_map/ppermute | solution.py:319
  55.3 1.7 %shard_map.123 = (f32[512,256]{1,0:T(8,128)S(1)}, f32[1,512]{1,0:T(1,128)S(1)}, bf16[128,256]{1,0:T(8,128)(2,1)S(1)}, bf16[128,256]{1,0:T(8,128)(2,1)S(1)}, bf16...) custom-call(bf16[1024,512]{1,0:T(8,128)(2,1)S(1)} %get-tuple-element, ...), custom_call_target="tpu_custom_call" | custom-call | flops 1610612736 | bytes 4194304 | tf_op jit(solution)/shard_map/pallas_call | solution.py:306
  57.1 1.4 %collective-permute-start.24 = (bf16[128,256]{1,0:T(8,128)(2,1)S(1)}, bf16[128,256]{1,0:T(8,128)(2,1)S(1)}, u32[]{:S(2)}, u32[]{:S(2)}) collective-permute-start(bf16[128,256]{1,0:T(8,128)(2,1)S(1)} %get-tuple-element.102), channel_id=1, source_target_pairs={{0,2},{1,3},{2,0},{3,1},{4,6},{5,7},{6,4},{7,5},{8,10},{9,11},{10,... | collective-permute-start | bytes 196616 | tf_op jit(solution)/shard_map/ppermute | solution.py:319
  58.9 2.3 %collective-permute-start.26 = (bf16[128,256]{1,0:T(8,128)(2,1)S(1)}, bf16[128,256]{1,0:T(8,128)(2,1)S(1)}, u32[]{:S(2)}, u32[]{:S(2)}) collective-permute-start(bf16[128,256]{1,0:T(8,128)(2,1)S(1)} %get-tuple-element.104), channel_id=1, source_target_pairs={{0,4},{1,5},{2,6},{3,7},{4,0},{5,1},{6,2},{7,3},{8,12},{9,13},{10,... | collective-permute-start | bytes 196616 | tf_op jit(solution)/shard_map/ppermute | solution.py:319
  61.6 2.5 %collective-permute-start.28 = (bf16[128,256]{1,0:T(8,128)(2,1)S(1)}, bf16[128,256]{1,0:T(8,128)(2,1)S(1)}, u32[]{:S(2)}, u32[]{:S(2)}) collective-permute-start(bf16[128,256]{1,0:T(8,128)(2,1)S(1)} %get-tuple-element.106), channel_id=1, source_target_pairs={{0,6},{1,7},{2,4},{3,5},{4,2},{5,3},{6,0},{7,1},{8,14},{9,15},{10,... | collective-permute-start | bytes 196616 | tf_op jit(solution)/shard_map/ppermute | solution.py:319
  64.0 1.1 collective-permute-start.29
  65.8 2.5 %shard_map.125.slope_ref = f32[4,256,1024]{2,1,0:T(8,128)S(1)} custom-call(bf16[4,256,1024]{2,1,0:T(8,128)(2,1)S(1)} %get-tuple-element.73.win_ref, bf16[128,256]{1,0:T(8,128)(2,1)S(1)} %get-tuple-element.75.refs_0_, bf16[128,256]{1,0:T(8,128)(2,1)S(1)} %collective-permute-done.refs_1_, bf16[128,256]{1,0:T(8,128)(2,1)S(1)} %collective-permute-done.1.refs_2_, ...), custom_call_target="tpu_custom_call" | custom-call | flops 536870912 | bytes 6291456 | tf_op jit(solution)/shard_map/pallas_call | solution.py:306
  68.9 2.6 %collective-permute-done.27.refs_5_ = bf16[128,256]{1,0:T(8,128)(2,1)S(1)} collective-permute-done((bf16[128,256]{1,0:T(8,128)(2,1)S(1)}, bf16[128,256]{1,0:T(8,128)(2,1)S(1)}, u32[]{:S(2)}, u32[]{:S(2)}) %collective-permute-start.27) | collective-permute-done | bytes 65568 | tf_op jit(solution)/shard_map/ppermute | solution.py:319
  72.0 1.6 %shard_map.126 = (bf16[128,256]{1,0:T(8,128)(2,1)S(1)}, bf16[128,256]{1,0:T(8,128)(2,1)S(1)}, bf16[128,256]{1,0:T(8,128)(2,1)S(1)}, bf16[128,256]{1,0:T(8,128)(2...) custom-call(bf16[4,256,1024]{2,1,0:T(8,128)(2,1)S(1)} %get-tuple-ele, ...), custom_call_target="tpu_custom_call" | custom-call | flops 1073741824 | bytes 6291456 | tf_op jit(solution)/shard_map/pallas_call | solution.py:306
  73.7 3.2 %collective-permute-start.31 = (bf16[128,256]{1,0:T(8,128)(2,1)S(1)}, bf16[128,256]{1,0:T(8,128)(2,1)S(1)}, u32[]{:S(2)}, u32[]{:S(2)}) collective-permute-start(bf16[128,256]{1,0:T(8,128)(2,1)S(1)} %get-tuple-element.110), channel_id=1, source_target_pairs={{0,2},{1,3},{2,0},{3,1},{4,6},{5,7},{6,4},{7,5},{8,10},{9,11},{10,... | collective-permute-start | bytes 196616 | tf_op jit(solution)/shard_map/ppermute | solution.py:319
  76.9 1.9 %collective-permute-start.33 = (bf16[128,256]{1,0:T(8,128)(2,1)S(1)}, bf16[128,256]{1,0:T(8,128)(2,1)S(1)}, u32[]{:S(2)}, u32[]{:S(2)}) collective-permute-start(bf16[128,256]{1,0:T(8,128)(2,1)S(1)} %get-tuple-element.112), channel_id=1, source_target_pairs={{0,4},{1,5},{2,6},{3,7},{4,0},{5,1},{6,2},{7,3},{8,12},{9,13},{10,... | collective-permute-start | bytes 196616 | tf_op jit(solution)/shard_map/ppermute | solution.py:319
  78.8 0.7 collective-permute-start.40
  80.0 2.3 %collective-permute-start.42 = (bf16[256,256]{1,0:T(8,128)(2,1)S(1)}, bf16[256,256]{1,0:T(8,128)(2,1)S(1)}, u32[]{:S(2)}, u32[]{:S(2)}) collective-permute-start(bf16[256,256]{1,0:T(8,128)(2,1)S(1)} %get-tuple-element.126), channel_id=1, source_target_pairs={{0,24},{8,16},{16,8},{24,0},{1,25},{9,17},{17,9},{25,1},{2,26},{10... | collective-permute-start | bytes 393224 | tf_op jit(solution)/shard_map/ppermute | solution.py:319
  83.1 0.9 collective-permute-start.34
  84.0 2.7 %shard_map.129 = (bf16[1024,1024]{1,0:T(8,128)(2,1)S(1)}, bf16[1024,1024]{1,0:T(8,128)(2,1)S(1)}, bf16[256,1024]{1,0:T(8,128)(2,1)S(1)}) custom-call(bf16[4,256,1024]{2,1,0:T(8,128)(2,1)S(1)} %get-tuple-element.73.win_ref, bf16[256,256]{1,0:T(8,128)(2,1)S(1)} %get-tuple-element.116.refs_0_, bf16[256,256]{1,0:T(8,128)(2,1)S(1)} %collective-permute-done.37.refs_1_, ...), custom_call_target="tpu_custom_call" | custom-call | flops 536870912 | bytes 6291456 | tf_op jit(solution)/shard_map/pallas_call | solution.py:306
  86.7 2.9 %collective-permute-done.34.refs_5_ = bf16[128,256]{1,0:T(8,128)(2,1)S(1)} collective-permute-done((bf16[128,256]{1,0:T(8,128)(2,1)S(1)}, bf16[128,256]{1,0:T(8,128)(2,1)S(1)}, u32[]{:S(2)}, u32[]{:S(2)}) %collective-permute-start.34) | collective-permute-done | bytes 65568 | tf_op jit(solution)/shard_map/ppermute | solution.py:319
  90.2 2.5 %collective-permute-start.22 = (bf16[512,256]{1,0:T(8,128)(2,1)S(1)}, bf16[512,256]{1,0:T(8,128)(2,1)S(1)}, u32[]{:S(2)}, u32[]{:S(2)}) collective-permute-start(bf16[512,256]{1,0:T(8,128)(2,1)S(1)} %get-tuple-element.96.refs_0_), channel_id=1, source_target_pairs={{0,24},{8,16},{16,8},{24,0},{1,25},{9,17},{17,9},{25,1},{2,26},{10... | collective-permute-start | bytes 786440 | tf_op jit(solution)/shard_map/ppermute | solution.py:319
  92.7 1.7 %collective-permute-start.35 = (bf16[128,256]{1,0:T(8,128)(2,1)S(1)}, bf16[128,256]{1,0:T(8,128)(2,1)S(1)}, u32[]{:S(2)}, u32[]{:S(2)}) collective-permute-start(bf16[128,256]{1,0:T(8,128)(2,1)S(1)} %get-tuple-element.114), channel_id=1, source_target_pairs={{0,6},{1,7},{2,4},{3,5},{4,2},{5,3},{6,0},{7,1},{8,14},{9,15},{10,... | collective-permute-start | bytes 196616 | tf_op jit(solution)/shard_map/ppermute | solution.py:319
  94.4 1.0 collective-permute-start.36
  95.4 1.9 %shard_map.131 = (bf16[512,256]{1,0:T(8,128)(2,1)S(1)}, bf16[512,256]{1,0:T(8,128)(2,1)S(1)}, bf16[512,256]{1,0:T(8,128)(2,1)S(1)}, bf16[512,256]{1,0:T(8,128)(2,1)S(1)}) custom-call(bf16[4,1024,256]{2,1,0:T(8,128)(2,1)S(1)} %get-tuple-element.74.wout_ref, bf16[1024,1024]{1,0:T(8,128)(2,1)S(1)} %get-tuple-element.120.act_ref, ...), custom_call_target="tpu_custom_call" | custom-call | flops 1610612736 | bytes 6291456 | tf_op jit(solution)/shard_map/pallas_call | solution.py:306
  97.3 1.5 %collective-permute-done.35.refs_6_ = bf16[128,256]{1,0:T(8,128)(2,1)S(1)} collective-permute-done((bf16[128,256]{1,0:T(8,128)(2,1)S(1)}, bf16[128,256]{1,0:T(8,128)(2,1)S(1)}, u32[]{:S(2)}, u32[]{:S(2)}) %collective-permute-start.35) | collective-permute-done | bytes 65568 | tf_op jit(solution)/shard_map/ppermute | solution.py:319
  99.3 0.9 collective-permute-done.36.refs_7_
  100.8 1.5 %collective-permute-start.45 = (bf16[512,256]{1,0:T(8,128)(2,1)S(1)}, bf16[512,256]{1,0:T(8,128)(2,1)S(1)}, u32[]{:S(2)}, u32[]{:S(2)}) collective-permute-start(bf16[512,256]{1,0:T(8,128)(2,1)S(1)} %get-tuple-element.130), channel_id=1, source_target_pairs={{0,24},{8,16},{16,8},{24,0},{1,25},{9,17},{17,9},{25,1},{2,26},{10... | collective-permute-start | bytes 786440 | tf_op jit(solution)/shard_map/ppermute | solution.py:319
  102.3 1.3 %shard_map.127 = f32[512,256]{1,0:T(8,128)} custom-call(bf16[512,256]{1,0:T(8,128)(2,1)S(1)} %bitcast.13, bf16[512,1024]{1,0:T(8,128)(2,1)S(1)} %get-tuple-element.71.pick_ref, f32[512,256]{1,0:T(8,128)S(1)} %get-tuple-element.99.summed_ref, bf16[128,256]{1,0:T(8,128)(2,1)S(1)} %get-tuple-element.108.refs_0_, ...), custom_call_target="tpu_custom_call" | custom-call | flops 268435456 | bytes 2097152 | tf_op jit(solution)/shard_map/pallas_call | solution.py:306
  103.6 0.8 collective-permute-done.21.refs_2_
  104.4 3.0 %shard_map.124 = (f32[1,512]{1,0:T(1,128)}, f32[512,256]{1,0:T(8,128)}) custom-call(bf16[512,256]{1,0:T(8,128)(2,1)S(1)} %bitcast.10, s32[1,2048]{1,0:T(1,128)S(1)} %copy-done.3, f32[1,512]{1,0:T(1,128)S(1)} %get-tuple-element.95.lse_ref, f32[1,512]{1,0:T(1,128)S(1)} %copy-done.4, s32[1,512]{1,0:T(1,128)S(1)} %copy-done.5, ...), custom_call_target="tpu_custom_call" | custom-call | flops 1073741824 | bytes 3145728 | tf_op jit(solution)/shard_map/pallas_call | solution.py:306
  108.0 6.8 %collective-permute-done.44.refs_2_ = bf16[512,256]{1,0:T(8,128)(2,1)S(1)} collective-permute-done((bf16[512,256]{1,0:T(8,128)(2,1)S(1)}, bf16[512,256]{1,0:T(8,128)(2,1)S(1)}, u32[]{:S(2)}, u32[]{:S(2)}) %collective-permute-start.44) | collective-permute-done | bytes 262176 | tf_op jit(solution)/shard_map/ppermute | solution.py:319
  114.8 1.6 %shard_map.132 = (f32[64,4,1024]{2,1,0:T(4,128)}, f32[256,4,256]{2,1,0:T(4,128)}) custom-call(bf16[512,256]{1,0:T(8,128)(2,1)S(1)} %get-tuple-element.127.refs_0_, bf16[512,256]{1,0:T(8,128)(2,1)S(1)} %collective-permute-done.43.refs_1_, bf16[512,256]{1,0:T(8,128)(2,1)S(1)} %collective-permute-done.44.refs_2_, ...), custom_call_target="tpu_custom_call" | custom-call | flops 536870912 | bytes 6291456 | tf_op jit(solution)/shard_map/pallas_call | solution.py:306
  (70 shorter events, 9.0 us)
Async XLA Ops:
  2.2 6.0 %collective-permute-start = (bf16[128,256]{1,0:T(8,128)(2,1)S(1)}, bf16[128,256]{1,0:T(8,128)(2,1)S(1)}, u32[]{:S(2)}, u32[]{:S(2)}) collective-permute-start(bf16[128,256]{1,0:T(8,128)(2,1)S(1)} %get-tuple-element.76), channel_id=1, source_target_pairs={{0,1},{1,0},{2,3},{3,2},{4,5},{5,4},{6,7},{7,6},{8,9},{9,8},{10,11... | collective-permute-start | bytes 196616 | tf_op jit(solution)/shard_map/ppermute | solution.py:319
  2.7 9.1 %collective-permute-start.1 = (bf16[128,256]{1,0:T(8,128)(2,1)S(1)}, bf16[128,256]{1,0:T(8,128)(2,1)S(1)}, u32[]{:S(2)}, u32[]{:S(2)}) collective-permute-start(bf16[128,256]{1,0:T(8,128)(2,1)S(1)} %get-tuple-element.77), channel_id=1, source_target_pairs={{0,2},{1,3},{2,0},{3,1},{4,6},{5,7},{6,4},{7,5},{8,10},{9,11},{10,... | collective-permute-start | bytes 196616 | tf_op jit(solution)/shard_map/ppermute | solution.py:319
  5.4 9.5 %collective-permute-start.2 = (bf16[128,256]{1,0:T(8,128)(2,1)S(1)}, bf16[128,256]{1,0:T(8,128)(2,1)S(1)}, u32[]{:S(2)}, u32[]{:S(2)}) collective-permute-start(bf16[128,256]{1,0:T(8,128)(2,1)S(1)} %get-tuple-element.78), channel_id=1, source_target_pairs={{0,3},{1,2},{2,1},{3,0},{4,7},{5,6},{6,5},{7,4},{8,11},{9,10},{10,... | collective-permute-start | bytes 196616 | tf_op jit(solution)/shard_map/ppermute | solution.py:319
  5.4 9.5 %collective-permute-start.3 = (bf16[128,256]{1,0:T(8,128)(2,1)S(1)}, bf16[128,256]{1,0:T(8,128)(2,1)S(1)}, u32[]{:S(2)}, u32[]{:S(2)}) collective-permute-start(bf16[128,256]{1,0:T(8,128)(2,1)S(1)} %get-tuple-element.79), channel_id=1, source_target_pairs={{0,4},{1,5},{2,6},{3,7},{4,0},{5,1},{6,2},{7,3},{8,12},{9,13},{10,... | collective-permute-start | bytes 196616 | tf_op jit(solution)/shard_map/ppermute | solution.py:319
  8.2 10.5 %collective-permute-start.4 = (bf16[128,256]{1,0:T(8,128)(2,1)S(1)}, bf16[128,256]{1,0:T(8,128)(2,1)S(1)}, u32[]{:S(2)}, u32[]{:S(2)}) collective-permute-start(bf16[128,256]{1,0:T(8,128)(2,1)S(1)} %get-tuple-element.80), channel_id=1, source_target_pairs={{0,5},{1,4},{2,7},{3,6},{4,1},{5,0},{6,3},{7,2},{8,13},{9,12},{10,... | collective-permute-start | bytes 196616 | tf_op jit(solution)/shard_map/ppermute | solution.py:319
  8.2 10.5 %collective-permute-start.5 = (bf16[128,256]{1,0:T(8,128)(2,1)S(1)}, bf16[128,256]{1,0:T(8,128)(2,1)S(1)}, u32[]{:S(2)}, u32[]{:S(2)}) collective-permute-start(bf16[128,256]{1,0:T(8,128)(2,1)S(1)} %get-tuple-element.81), channel_id=1, source_target_pairs={{0,6},{1,7},{2,4},{3,5},{4,2},{5,3},{6,0},{7,1},{8,14},{9,15},{10,... | collective-permute-start | bytes 196616 | tf_op jit(solution)/shard_map/ppermute | solution.py:319
  11.8 6.9 %collective-permute-start.6 = (bf16[128,256]{1,0:T(8,128)(2,1)S(1)}, bf16[128,256]{1,0:T(8,128)(2,1)S(1)}, u32[]{:S(2)}, u32[]{:S(2)}) collective-permute-start(bf16[128,256]{1,0:T(8,128)(2,1)S(1)} %get-tuple-element.82), channel_id=1, source_target_pairs={{0,7},{1,6},{2,5},{3,4},{4,3},{5,2},{6,1},{7,0},{8,15},{9,14},{10,... | collective-permute-start | bytes 196616 | tf_op jit(solution)/shard_map/ppermute | solution.py:319
  18.7 26.4 %copy-start.1 = (bf16[1,512,256]{2,1,0:T(8,128)(2,1)S(1)}, bf16[1,512,256]{2,1,0:T(8,128)(2,1)}, u32[]{:S(2)}) copy-start(bf16[1,512,256]{2,1,0:T(8,128)(2,1)} %param.8) | copy-start | bytes 786436
  18.7 26.4 %copy-start.4 = (f32[1,512]{1,0:T(1,128)S(1)}, f32[1,512]{1,0:T(1,128)}, u32[]{:S(2)}) copy-start(f32[1,512]{1,0:T(1,128)} %w_ref.3) | copy-start | bytes 6148
  20.4 8.3 %collective-permute-start.10 = (bf16[128,256]{1,0:T(8,128)(2,1)S(1)}, bf16[128,256]{1,0:T(8,128)(2,1)S(1)}, u32[]{:S(2)}, u32[]{:S(2)}) collective-permute-start(bf16[128,256]{1,0:T(8,128)(2,1)S(1)} %get-tuple-element.87), channel_id=1, source_target_pairs={{0,4},{1,5},{2,6},{3,7},{4,0},{5,1},{6,2},{7,3},{8,12},{9,13},{10,... | collective-permute-start | bytes 196616 | tf_op jit(solution)/shard_map/ppermute | solution.py:319
  25.0 20.1 %collective-permute-start.14 = (bf16[512,256]{1,0:T(8,128)(2,1)S(1)}, bf16[512,256]{1,0:T(8,128)(2,1)S(1)}, u32[]{:S(2)}, u32[]{:S(2)}) collective-permute-start(bf16[512,256]{1,0:T(8,128)(2,1)S(1)} %bitcast.5), channel_id=1, source_target_pairs={{0,8},{8,0},{16,24},{24,16},{1,9},{9,1},{17,25},{25,17},{2,10},{10... | collective-permute-start | bytes 786440 | tf_op jit(solution)/shard_map/ppermute | solution.py:319
  26.5 18.6 %collective-permute-start.15 = (bf16[512,256]{1,0:T(8,128)(2,1)S(1)}, bf16[512,256]{1,0:T(8,128)(2,1)S(1)}, u32[]{:S(2)}, u32[]{:S(2)}) collective-permute-start(bf16[512,256]{1,0:T(8,128)(2,1)S(1)} %bitcast.6), channel_id=1, source_target_pairs={{0,16},{8,24},{16,0},{24,8},{1,17},{9,25},{17,1},{25,9},{2,18},{10... | collective-permute-start | bytes 786440 | tf_op jit(solution)/shard_map/ppermute | solution.py:319
  28.0 17.1 %collective-permute-start.16 = (bf16[512,256]{1,0:T(8,128)(2,1)S(1)}, bf16[512,256]{1,0:T(8,128)(2,1)S(1)}, u32[]{:S(2)}, u32[]{:S(2)}) collective-permute-start(bf16[512,256]{1,0:T(8,128)(2,1)S(1)} %bitcast.7), channel_id=1, source_target_pairs={{0,24},{8,16},{16,8},{24,0},{1,25},{9,17},{17,9},{25,1},{2,26},{10... | collective-permute-start | bytes 786440 | tf_op jit(solution)/shard_map/ppermute | solution.py:319
  28.5 6.7 %collective-permute-start.11 = (bf16[128,256]{1,0:T(8,128)(2,1)S(1)}, bf16[128,256]{1,0:T(8,128)(2,1)S(1)}, u32[]{:S(2)}, u32[]{:S(2)}) collective-permute-start(bf16[128,256]{1,0:T(8,128)(2,1)S(1)} %get-tuple-element.88), channel_id=1, source_target_pairs={{0,5},{1,4},{2,7},{3,6},{4,1},{5,0},{6,3},{7,2},{8,13},{9,12},{10,... | collective-permute-start | bytes 196616 | tf_op jit(solution)/shard_map/ppermute | solution.py:319
  28.8 6.4 %collective-permute-start.12 = (bf16[128,256]{1,0:T(8,128)(2,1)S(1)}, bf16[128,256]{1,0:T(8,128)(2,1)S(1)}, u32[]{:S(2)}, u32[]{:S(2)}) collective-permute-start(bf16[128,256]{1,0:T(8,128)(2,1)S(1)} %get-tuple-element.89), channel_id=1, source_target_pairs={{0,6},{1,7},{2,4},{3,5},{4,2},{5,3},{6,0},{7,1},{8,14},{9,15},{10,... | collective-permute-start | bytes 196616 | tf_op jit(solution)/shard_map/ppermute | solution.py:319
  35.2 5.5 %collective-permute-start.13 = (bf16[128,256]{1,0:T(8,128)(2,1)S(1)}, bf16[128,256]{1,0:T(8,128)(2,1)S(1)}, u32[]{:S(2)}, u32[]{:S(2)}) collective-permute-start(bf16[128,256]{1,0:T(8,128)(2,1)S(1)} %get-tuple-element.90), channel_id=1, source_target_pairs={{0,7},{1,6},{2,5},{3,4},{4,3},{5,2},{6,1},{7,0},{8,15},{9,14},{10,... | collective-permute-start | bytes 196616 | tf_op jit(solution)/shard_map/ppermute | solution.py:319
  35.2 5.5 %collective-permute-start.7 = (bf16[128,256]{1,0:T(8,128)(2,1)S(1)}, bf16[128,256]{1,0:T(8,128)(2,1)S(1)}, u32[]{:S(2)}, u32[]{:S(2)}) collective-permute-start(bf16[128,256]{1,0:T(8,128)(2,1)S(1)} %get-tuple-element.84), channel_id=1, source_target_pairs={{0,1},{1,0},{2,3},{3,2},{4,5},{5,4},{6,7},{7,6},{8,9},{9,8},{10,11... | collective-permute-start | bytes 196616 | tf_op jit(solution)/shard_map/ppermute | solution.py:319
  40.7 4.4 %collective-permute-start.8 = (bf16[128,256]{1,0:T(8,128)(2,1)S(1)}, bf16[128,256]{1,0:T(8,128)(2,1)S(1)}, u32[]{:S(2)}, u32[]{:S(2)}) collective-permute-start(bf16[128,256]{1,0:T(8,128)(2,1)S(1)} %get-tuple-element.85), channel_id=1, source_target_pairs={{0,2},{1,3},{2,0},{3,1},{4,6},{5,7},{6,4},{7,5},{8,10},{9,11},{10,... | collective-permute-start | bytes 196616 | tf_op jit(solution)/shard_map/ppermute | solution.py:319
  40.7 4.4 %collective-permute-start.9 = (bf16[128,256]{1,0:T(8,128)(2,1)S(1)}, bf16[128,256]{1,0:T(8,128)(2,1)S(1)}, u32[]{:S(2)}, u32[]{:S(2)}) collective-permute-start(bf16[128,256]{1,0:T(8,128)(2,1)S(1)} %get-tuple-element.86), channel_id=1, source_target_pairs={{0,3},{1,2},{2,1},{3,0},{4,7},{5,6},{6,5},{7,4},{8,11},{9,10},{10,... | collective-permute-start | bytes 196616 | tf_op jit(solution)/shard_map/ppermute | solution.py:319
  47.4 4.0 %collective-permute-start.17 = (f32[10,512]{1,0:T(8,128)S(1)}, f32[10,512]{1,0:T(8,128)S(1)}, u32[]{:S(2)}, u32[]{:S(2)}) collective-permute-start(f32[10,512]{1,0:T(8,128)S(1)} %get-tuple-element.94.refs_4_), channel_id=1, source_target_pairs={{0,8},{8,0},{16,24},{24,16},{1,9},{9,1},{17,25},{25,17},{2,10},{10... | collective-permute-start | bytes 61448 | tf_op jit(solution)/shard_map/ppermute | solution.py:319
  48.9 3.9 %collective-permute-start.18 = (f32[10,512]{1,0:T(8,128)S(1)}, f32[10,512]{1,0:T(8,128)S(1)}, u32[]{:S(2)}, u32[]{:S(2)}) collective-permute-start(f32[10,512]{1,0:T(8,128)S(1)} %get-tuple-element.94.refs_4_), channel_id=1, source_target_pairs={{0,16},{8,24},{16,0},{24,8},{1,17},{9,25},{17,1},{25,9},{2,18},{10... | collective-permute-start | bytes 61448 | tf_op jit(solution)/shard_map/ppermute | solution.py:319
  50.5 4.8 %collective-permute-start.19 = (f32[10,512]{1,0:T(8,128)S(1)}, f32[10,512]{1,0:T(8,128)S(1)}, u32[]{:S(2)}, u32[]{:S(2)}) collective-permute-start(f32[10,512]{1,0:T(8,128)S(1)} %get-tuple-element.94.refs_4_), channel_id=1, source_target_pairs={{0,24},{8,16},{16,8},{24,0},{1,25},{9,17},{17,9},{25,1},{2,26},{10... | collective-permute-start | bytes 61448 | tf_op jit(solution)/shard_map/ppermute | solution.py:319
  57.0 4.5 %collective-permute-start.23 = (bf16[128,256]{1,0:T(8,128)(2,1)S(1)}, bf16[128,256]{1,0:T(8,128)(2,1)S(1)}, u32[]{:S(2)}, u32[]{:S(2)}) collective-permute-start(bf16[128,256]{1,0:T(8,128)(2,1)S(1)} %get-tuple-element.101), channel_id=1, source_target_pairs={{0,1},{1,0},{2,3},{3,2},{4,5},{5,4},{6,7},{7,6},{8,9},{9,8},{10,11... | collective-permute-start | bytes 196616 | tf_op jit(solution)/shard_map/ppermute | solution.py:319
  57.1 6.9 %collective-permute-start.24 = (bf16[128,256]{1,0:T(8,128)(2,1)S(1)}, bf16[128,256]{1,0:T(8,128)(2,1)S(1)}, u32[]{:S(2)}, u32[]{:S(2)}) collective-permute-start(bf16[128,256]{1,0:T(8,128)(2,1)S(1)} %get-tuple-element.102), channel_id=1, source_target_pairs={{0,2},{1,3},{2,0},{3,1},{4,6},{5,7},{6,4},{7,5},{8,10},{9,11},{10,... | collective-permute-start | bytes 196616 | tf_op jit(solution)/shard_map/ppermute | solution.py:319
  58.5 6.7 %collective-permute-start.25 = (bf16[128,256]{1,0:T(8,128)(2,1)S(1)}, bf16[128,256]{1,0:T(8,128)(2,1)S(1)}, u32[]{:S(2)}, u32[]{:S(2)}) collective-permute-start(bf16[128,256]{1,0:T(8,128)(2,1)S(1)} %get-tuple-element.103), channel_id=1, source_target_pairs={{0,3},{1,2},{2,1},{3,0},{4,7},{5,6},{6,5},{7,4},{8,11},{9,10},{10,... | collective-permute-start | bytes 196616 | tf_op jit(solution)/shard_map/ppermute | solution.py:319
  58.9 9.3 %collective-permute-start.26 = (bf16[128,256]{1,0:T(8,128)(2,1)S(1)}, bf16[128,256]{1,0:T(8,128)(2,1)S(1)}, u32[]{:S(2)}, u32[]{:S(2)}) collective-permute-start(bf16[128,256]{1,0:T(8,128)(2,1)S(1)} %get-tuple-element.104), channel_id=1, source_target_pairs={{0,4},{1,5},{2,6},{3,7},{4,0},{5,1},{6,2},{7,3},{8,12},{9,13},{10,... | collective-permute-start | bytes 196616 | tf_op jit(solution)/shard_map/ppermute | solution.py:319
  61.3 10.3 %collective-permute-start.27 = (bf16[128,256]{1,0:T(8,128)(2,1)S(1)}, bf16[128,256]{1,0:T(8,128)(2,1)S(1)}, u32[]{:S(2)}, u32[]{:S(2)}) collective-permute-start(bf16[128,256]{1,0:T(8,128)(2,1)S(1)} %get-tuple-element.105), channel_id=1, source_target_pairs={{0,5},{1,4},{2,7},{3,6},{4,1},{5,0},{6,3},{7,2},{8,13},{9,12},{10,... | collective-permute-start | bytes 196616 | tf_op jit(solution)/shard_map/ppermute | solution.py:319
  61.6 10.5 %collective-permute-start.28 = (bf16[128,256]{1,0:T(8,128)(2,1)S(1)}, bf16[128,256]{1,0:T(8,128)(2,1)S(1)}, u32[]{:S(2)}, u32[]{:S(2)}) collective-permute-start(bf16[128,256]{1,0:T(8,128)(2,1)S(1)} %get-tuple-element.106), channel_id=1, source_target_pairs={{0,6},{1,7},{2,4},{3,5},{4,2},{5,3},{6,0},{7,1},{8,14},{9,15},{10,... | collective-permute-start | bytes 196616 | tf_op jit(solution)/shard_map/ppermute | solution.py:319
  64.0 8.0 %collective-permute-start.29 = (bf16[128,256]{1,0:T(8,128)(2,1)S(1)}, bf16[128,256]{1,0:T(8,128)(2,1)S(1)}, u32[]{:S(2)}, u32[]{:S(2)}) collective-permute-start(bf16[128,256]{1,0:T(8,128)(2,1)S(1)} %get-tuple-element.107), channel_id=1, source_target_pairs={{0,7},{1,6},{2,5},{3,4},{4,3},{5,2},{6,1},{7,0},{8,15},{9,14},{10,... | collective-permute-start | bytes 196616 | tf_op jit(solution)/shard_map/ppermute | solution.py:319
  65.2 11.7 %collective-permute-start.37 = (bf16[256,256]{1,0:T(8,128)(2,1)S(1)}, bf16[256,256]{1,0:T(8,128)(2,1)S(1)}, u32[]{:S(2)}, u32[]{:S(2)}) collective-permute-start(bf16[256,256]{1,0:T(8,128)(2,1)S(1)} %get-tuple-element.117), channel_id=1, source_target_pairs={{0,8},{8,0},{16,24},{24,16},{1,9},{9,1},{17,25},{25,17},{2,10},{10... | collective-permute-start | bytes 393224 | tf_op jit(solution)/shard_map/ppermute | solution.py:319
  68.3 8.6 %collective-permute-start.38 = (bf16[256,256]{1,0:T(8,128)(2,1)S(1)}, bf16[256,256]{1,0:T(8,128)(2,1)S(1)}, u32[]{:S(2)}, u32[]{:S(2)}) collective-permute-start(bf16[256,256]{1,0:T(8,128)(2,1)S(1)} %get-tuple-element.118), channel_id=1, source_target_pairs={{0,16},{8,24},{16,0},{24,8},{1,17},{9,25},{17,1},{25,9},{2,18},{10... | collective-permute-start | bytes 393224 | tf_op jit(solution)/shard_map/ppermute | solution.py:319
  71.5 7.3 %collective-permute-start.39 = (bf16[256,256]{1,0:T(8,128)(2,1)S(1)}, bf16[256,256]{1,0:T(8,128)(2,1)S(1)}, u32[]{:S(2)}, u32[]{:S(2)}) collective-permute-start(bf16[256,256]{1,0:T(8,128)(2,1)S(1)} %get-tuple-element.119), channel_id=1, source_target_pairs={{0,24},{8,16},{16,8},{24,0},{1,25},{9,17},{17,9},{25,1},{2,26},{10... | collective-permute-start | bytes 393224 | tf_op jit(solution)/shard_map/ppermute | solution.py:319
  73.6 5.8 %collective-permute-start.30 = (bf16[128,256]{1,0:T(8,128)(2,1)S(1)}, bf16[128,256]{1,0:T(8,128)(2,1)S(1)}, u32[]{:S(2)}, u32[]{:S(2)}) collective-permute-start(bf16[128,256]{1,0:T(8,128)(2,1)S(1)} %get-tuple-element.109), channel_id=1, source_target_pairs={{0,1},{1,0},{2,3},{3,2},{4,5},{5,4},{6,7},{7,6},{8,9},{9,8},{10,11... | collective-permute-start | bytes 196616 | tf_op jit(solution)/shard_map/ppermute | solution.py:319
  73.7 6.3 %collective-permute-start.31 = (bf16[128,256]{1,0:T(8,128)(2,1)S(1)}, bf16[128,256]{1,0:T(8,128)(2,1)S(1)}, u32[]{:S(2)}, u32[]{:S(2)}) collective-permute-start(bf16[128,256]{1,0:T(8,128)(2,1)S(1)} %get-tuple-element.110), channel_id=1, source_target_pairs={{0,2},{1,3},{2,0},{3,1},{4,6},{5,7},{6,4},{7,5},{8,10},{9,11},{10,... | collective-permute-start | bytes 196616 | tf_op jit(solution)/shard_map/ppermute | solution.py:319
  76.9 5.7 %collective-permute-start.32 = (bf16[128,256]{1,0:T(8,128)(2,1)S(1)}, bf16[128,256]{1,0:T(8,128)(2,1)S(1)}, u32[]{:S(2)}, u32[]{:S(2)}) collective-permute-start(bf16[128,256]{1,0:T(8,128)(2,1)S(1)} %get-tuple-element.111), channel_id=1, source_target_pairs={{0,3},{1,2},{2,1},{3,0},{4,7},{5,6},{6,5},{7,4},{8,11},{9,10},{10,... | collective-permute-start | bytes 196616 | tf_op jit(solution)/shard_map/ppermute | solution.py:319
  76.9 6.1 %collective-permute-start.33 = (bf16[128,256]{1,0:T(8,128)(2,1)S(1)}, bf16[128,256]{1,0:T(8,128)(2,1)S(1)}, u32[]{:S(2)}, u32[]{:S(2)}) collective-permute-start(bf16[128,256]{1,0:T(8,128)(2,1)S(1)} %get-tuple-element.112), channel_id=1, source_target_pairs={{0,4},{1,5},{2,6},{3,7},{4,0},{5,1},{6,2},{7,3},{8,12},{9,13},{10,... | collective-permute-start | bytes 196616 | tf_op jit(solution)/shard_map/ppermute | solution.py:319
  78.8 11.4 %collective-permute-start.40 = (bf16[256,256]{1,0:T(8,128)(2,1)S(1)}, bf16[256,256]{1,0:T(8,128)(2,1)S(1)}, u32[]{:S(2)}, u32[]{:S(2)}) collective-permute-start(bf16[256,256]{1,0:T(8,128)(2,1)S(1)} %get-tuple-element.124), channel_id=1, source_target_pairs={{0,8},{8,0},{16,24},{24,16},{1,9},{9,1},{17,25},{25,17},{2,10},{10... | collective-permute-start | bytes 393224 | tf_op jit(solution)/shard_map/ppermute | solution.py:319
  79.5 13.3 %collective-permute-start.41 = (bf16[256,256]{1,0:T(8,128)(2,1)S(1)}, bf16[256,256]{1,0:T(8,128)(2,1)S(1)}, u32[]{:S(2)}, u32[]{:S(2)}) collective-permute-start(bf16[256,256]{1,0:T(8,128)(2,1)S(1)} %get-tuple-element.125), channel_id=1, source_target_pairs={{0,16},{8,24},{16,0},{24,8},{1,17},{9,25},{17,1},{25,9},{2,18},{10... | collective-permute-start | bytes 393224 | tf_op jit(solution)/shard_map/ppermute | solution.py:319
  80.0 14.4 %collective-permute-start.42 = (bf16[256,256]{1,0:T(8,128)(2,1)S(1)}, bf16[256,256]{1,0:T(8,128)(2,1)S(1)}, u32[]{:S(2)}, u32[]{:S(2)}) collective-permute-start(bf16[256,256]{1,0:T(8,128)(2,1)S(1)} %get-tuple-element.126), channel_id=1, source_target_pairs={{0,24},{8,16},{16,8},{24,0},{1,25},{9,17},{17,9},{25,1},{2,26},{10... | collective-permute-start | bytes 393224 | tf_op jit(solution)/shard_map/ppermute | solution.py:319
  82.5 18.2 %collective-permute-start.20 = (bf16[512,256]{1,0:T(8,128)(2,1)S(1)}, bf16[512,256]{1,0:T(8,128)(2,1)S(1)}, u32[]{:S(2)}, u32[]{:S(2)}) collective-permute-start(bf16[512,256]{1,0:T(8,128)(2,1)S(1)} %get-tuple-element.96.refs_0_), channel_id=1, source_target_pairs={{0,8},{8,0},{16,24},{24,16},{1,9},{9,1},{17,25},{25,17},{2,10},{10... | collective-permute-start | bytes 786440 | tf_op jit(solution)/shard_map/ppermute | solution.py:319
  83.1 6.6 %collective-permute-start.34 = (bf16[128,256]{1,0:T(8,128)(2,1)S(1)}, bf16[128,256]{1,0:T(8,128)(2,1)S(1)}, u32[]{:S(2)}, u32[]{:S(2)}) collective-permute-start(bf16[128,256]{1,0:T(8,128)(2,1)S(1)} %get-tuple-element.113), channel_id=1, source_target_pairs={{0,5},{1,4},{2,7},{3,6},{4,1},{5,0},{6,3},{7,2},{8,13},{9,12},{10,... | collective-permute-start | bytes 196616 | tf_op jit(solution)/shard_map/ppermute | solution.py:319
  89.6 14.8 %collective-permute-start.21 = (bf16[512,256]{1,0:T(8,128)(2,1)S(1)}, bf16[512,256]{1,0:T(8,128)(2,1)S(1)}, u32[]{:S(2)}, u32[]{:S(2)}) collective-permute-start(bf16[512,256]{1,0:T(8,128)(2,1)S(1)} %get-tuple-element.96.refs_0_), channel_id=1, source_target_pairs={{0,16},{8,24},{16,0},{24,8},{1,17},{9,25},{17,1},{25,9},{2,18},{10... | collective-permute-start | bytes 786440 | tf_op jit(solution)/shard_map/ppermute | solution.py:319
  90.2 14.2 %collective-permute-start.22 = (bf16[512,256]{1,0:T(8,128)(2,1)S(1)}, bf16[512,256]{1,0:T(8,128)(2,1)S(1)}, u32[]{:S(2)}, u32[]{:S(2)}) collective-permute-start(bf16[512,256]{1,0:T(8,128)(2,1)S(1)} %get-tuple-element.96.refs_0_), channel_id=1, source_target_pairs={{0,24},{8,16},{16,8},{24,0},{1,25},{9,17},{17,9},{25,1},{2,26},{10... | collective-permute-start | bytes 786440 | tf_op jit(solution)/shard_map/ppermute | solution.py:319
  92.7 6.1 %collective-permute-start.35 = (bf16[128,256]{1,0:T(8,128)(2,1)S(1)}, bf16[128,256]{1,0:T(8,128)(2,1)S(1)}, u32[]{:S(2)}, u32[]{:S(2)}) collective-permute-start(bf16[128,256]{1,0:T(8,128)(2,1)S(1)} %get-tuple-element.114), channel_id=1, source_target_pairs={{0,6},{1,7},{2,4},{3,5},{4,2},{5,3},{6,0},{7,1},{8,14},{9,15},{10,... | collective-permute-start | bytes 196616 | tf_op jit(solution)/shard_map/ppermute | solution.py:319
  94.4 5.8 %collective-permute-start.36 = (bf16[128,256]{1,0:T(8,128)(2,1)S(1)}, bf16[128,256]{1,0:T(8,128)(2,1)S(1)}, u32[]{:S(2)}, u32[]{:S(2)}) collective-permute-start(bf16[128,256]{1,0:T(8,128)(2,1)S(1)} %get-tuple-element.115), channel_id=1, source_target_pairs={{0,7},{1,6},{2,5},{3,4},{4,3},{5,2},{6,1},{7,0},{8,15},{9,14},{10,... | collective-permute-start | bytes 196616 | tf_op jit(solution)/shard_map/ppermute | solution.py:319
  98.8 9.2 %collective-permute-start.43 = (bf16[512,256]{1,0:T(8,128)(2,1)S(1)}, bf16[512,256]{1,0:T(8,128)(2,1)S(1)}, u32[]{:S(2)}, u32[]{:S(2)}) collective-permute-start(bf16[512,256]{1,0:T(8,128)(2,1)S(1)} %get-tuple-element.128), channel_id=1, source_target_pairs={{0,8},{8,0},{16,24},{24,16},{1,9},{9,1},{17,25},{25,17},{2,10},{10... | collective-permute-start | bytes 786440 | tf_op jit(solution)/shard_map/ppermute | solution.py:319
  100.2 14.6 %collective-permute-start.44 = (bf16[512,256]{1,0:T(8,128)(2,1)S(1)}, bf16[512,256]{1,0:T(8,128)(2,1)S(1)}, u32[]{:S(2)}, u32[]{:S(2)}) collective-permute-start(bf16[512,256]{1,0:T(8,128)(2,1)S(1)} %get-tuple-element.129), channel_id=1, source_target_pairs={{0,16},{8,24},{16,0},{24,8},{1,17},{9,25},{17,1},{25,9},{2,18},{10... | collective-permute-start | bytes 786440 | tf_op jit(solution)/shard_map/ppermute | solution.py:319
  100.8 14.0 %collective-permute-start.45 = (bf16[512,256]{1,0:T(8,128)(2,1)S(1)}, bf16[512,256]{1,0:T(8,128)(2,1)S(1)}, u32[]{:S(2)}, u32[]{:S(2)}) collective-permute-start(bf16[512,256]{1,0:T(8,128)(2,1)S(1)} %get-tuple-element.130), channel_id=1, source_target_pairs={{0,24},{8,16},{16,8},{24,0},{1,25},{9,17},{17,9},{25,1},{2,26},{10... | collective-permute-start | bytes 786440 | tf_op jit(solution)/shard_map/ppermute | solution.py:319
  (4 other events, 40.6 us)

commit v2 on v1

--- a/solution.py
+++ b/solution.py
@@ -8,6 +8,7 @@
 from jax.sharding import PartitionSpec as P
 
 CAP = 32
+CUT = 256
 norm_eps = 1e-06
 BF = jnp.bfloat16
 F32 = jnp.float32
@@ -38,12 +39,13 @@
 
 
 def gelu(v):
-    return 0.5 * v * (1.0 + jnp.tanh(GELU_C * (v + GELU_A * v * v * v)))
+    half = 0.5 * v
+    return half + half * jnp.tanh(v * (GELU_C + (GELU_A * GELU_C) * (v * v)))
 
 
 def gelu_both(v):
     sq = v * v
-    th = jnp.tanh(GELU_C * (v + GELU_A * v * sq))
+    th = jnp.tanh(v * (GELU_C + (GELU_A * GELU_C) * sq))
     half = 0.5 * (1.0 + th)
     slope = half + 0.5 * v * (1.0 - th * th) * (GELU_C + (3.0 * GELU_A * GELU_C) * sq)
     return v * half, slope
@@ -55,6 +57,17 @@
 
 def gather_rows(pick_ref, blocks):
     return dg(pick_ref[...], jnp.concatenate([b[...] for b in blocks], axis=0), 1, 0)
+
+
+def put_row(ref, index, row):
+    pieces = row.shape[1] // 128
+    for c in range(pieces):
+        ref[index * pieces + c : index * pieces + c + 1, :] = row[:, c * 128 : (c + 1) * 128]
+
+
+def get_row(ref, index, width):
+    pieces = width // 128
+    return jnp.concatenate([ref[index * pieces + c : index * pieces + c + 1, :] for c in range(pieces)], axis=1)
 
 
 def inv_rms_of(x):
@@ -156,15 +169,23 @@
     unit_ref[...] = unit
     length_ref[...] = jnp.broadcast_to(length, length_ref.shape)
     logs = logs_ref[:, 0:1]
+    cuts = [slice(i, i + CUT) for i in range(0, low.shape[0], CUT)]
     for s in range(shards):
-        scores = dg(low, queries[s][...], 1, 1) - logs
-        high = jnp.max(scores, axis=0, keepdims=True)
-        stats_ref[s : s + 1, :] = high
-        terms = jnp.exp(scores - high)
-        terms_ref[s] = terms
-        stats_ref[shards + s : shards + s + 1, :] = jnp.sum(terms, axis=0, keepdims=True)
-    stats_ref[2 * shards : 2 * shards + 1, :] = w_ref[...]
-    stats_ref[2 * shards + 1 : 2 * shards + 2, :] = pos_ref[...].astype(F32)
+        high, total = None, None
+        for cut in cuts:
+            scores = dg(low[cut], queries[s][...], 1, 1) - logs[cut]
+            terms_ref[s, cut, :] = scores
+            top = jnp.max(scores, axis=0, keepdims=True)
+            high = top if high is None else jnp.maximum(high, top)
+        put_row(stats_ref, s, high)
+        for cut in cuts:
+            terms = jnp.exp(terms_ref[s, cut, :] - high)
+            terms_ref[s, cut, :] = terms
+            part = jnp.sum(terms, axis=0, keepdims=True)
+            total = part if total is None else total + part
+        put_row(stats_ref, shards + s, total)
+    put_row(stats_ref, 2 * shards, w_ref[...])
+    put_row(stats_ref, 2 * shards + 1, pos_ref[...].astype(F32))
 
 
 def grad_kernel(groups, shards, put_ref, unit_ref, length_ref, terms_ref, *refs):
@@ -172,18 +193,18 @@
     stats = refs[shards : 2 * shards]
     summed_ref, lse_ref = refs[2 * shards : 2 * shards + 2]
     outs = refs[2 * shards + 2 :]
-    rows = unit_ref.shape[0]
+    rows, q_rows = unit_ref.shape[0], terms_ref.shape[2]
     item = iota((rows, 1), 0) + lax.axis_index("dp") * rows
     total = None
     for u in range(shards):
-        highs = [stats[t][(t ^ u) : (t ^ u) + 1, :] for t in range(shards)]
-        sums = [stats[t][shards + (t ^ u) : shards + (t ^ u) + 1, :] for t in range(shards)]
+        highs = [get_row(stats[t], t ^ u, q_rows) for t in range(shards)]
+        sums = [get_row(stats[t], shards + (t ^ u), q_rows) for t in range(shards)]
         high = functools.reduce(jnp.maximum, highs)
         lse = high + jnp.log(sum(l * jnp.exp(m - high) for l, m in zip(sums, highs)))
         if u == 0:
             lse_ref[...] = lse
-        weight = stats[u][2 * shards : 2 * shards + 1, :]
-        target = stats[u][2 * shards + 1 : 2 * shards + 2, :].astype(jnp.int32)
+        weight = get_row(stats[u], 2 * shards, q_rows)
+        target = get_row(stats[u], 2 * shards + 1, q_rows).astype(jnp.int32)
         scale = weight * jnp.exp(highs[0] - lse)
         coeff = (terms_ref[u] * scale - jnp.where(item == target, weight, 0.0)).astype(BF)
         part = dg(coeff, queries[u][...], 1, 0)
@@ -400,7 +421,7 @@
             ((rows, width), BF),
             ((rows, width), F32),
             ((rows, 128), F32),
-            ((2 * shards + 2, q_rows), F32),
+            (((2 * shards + 2) * q_rows // 128, 128), F32),
             ((shards, rows, q_rows), F32),
         ],
         (feats, pick, logs, query_weight, positives, *returned, *all_queries),

time: 117 us -> 116 us (level)
  no operation moved by 1% of the time
where the time goes in v2:
time: 116 us
  starting transfers between devices  53.3 us (46%)
  waiting for transfers between devices  37.5 us (32%)
  Pallas kernels  23.8 us (21%)
    ppermute x46, starting transfers between devices, shift_by(): return lax.ppermute(values, axis, [(i, i ^ s) for i in range(n)])  53.3 us
    ppermute x46, waiting for transfers between devices, shift_by(): return lax.ppermute(values, axis, [(i, i ^ s) for i in range(n)])  37.5 us
    pallas_call x14, Pallas kernels, call(): pl.pallas_call(body, out_shape=shapes, in_specs=[pl.BlockSpec(memory_spac...  23.8 us
  transfers between devices with their start and end apart: 46, of which 16 were waited for; matrix products, arithmetic and copies ran while one was open for 0% of the time, Pallas kernels for 13%

profile of v2, /device:TPU:0, one launch (start us, length us, event | category | flops | bytes accessed | tf_op | source)
XLA Modules:
  0.0 116.1 jit_solution(4511039924032827993)
XLA Ops:
  0.6 1.5 %shard_map.119 = (s32[1,512]{1,0:T(1,128)S(1)}, bf16[128,256]{1,0:T(8,128)(2,1)S(1)}, bf16[128,256]{1,0:T(8,128)(2,1)S(1)}, bf16[128,256]{1,0:T(8,128)(2,1)S(1)}...) custom-call(s32[1,512]{1,0:T(1,128)} %bitcast.15, ...), custom_call_target="tpu_custom_call" | custom-call | flops 268435456 | bytes 1048576 | tf_op jit(solution)/shard_map/pallas_call | solution.py:327
  2.7 2.6 %collective-permute-start.1 = (bf16[128,256]{1,0:T(8,128)(2,1)S(1)}, bf16[128,256]{1,0:T(8,128)(2,1)S(1)}, u32[]{:S(2)}, u32[]{:S(2)}) collective-permute-start(bf16[128,256]{1,0:T(8,128)(2,1)S(1)} %get-tuple-element.77), channel_id=1, source_target_pairs={{0,2},{1,3},{2,0},{3,1},{4,6},{5,7},{6,4},{7,5},{8,10},{9,11},{10,... | collective-permute-start | bytes 196616 | tf_op jit(solution)/shard_map/ppermute | solution.py:340
  5.4 2.8 %collective-permute-start.3 = (bf16[128,256]{1,0:T(8,128)(2,1)S(1)}, bf16[128,256]{1,0:T(8,128)(2,1)S(1)}, u32[]{:S(2)}, u32[]{:S(2)}) collective-permute-start(bf16[128,256]{1,0:T(8,128)(2,1)S(1)} %get-tuple-element.79), channel_id=1, source_target_pairs={{0,4},{1,5},{2,6},{3,7},{4,0},{5,1},{6,2},{7,3},{8,12},{9,13},{10,... | collective-permute-start | bytes 196616 | tf_op jit(solution)/shard_map/ppermute | solution.py:340
  8.2 3.6 %collective-permute-start.5 = (bf16[128,256]{1,0:T(8,128)(2,1)S(1)}, bf16[128,256]{1,0:T(8,128)(2,1)S(1)}, u32[]{:S(2)}, u32[]{:S(2)}) collective-permute-start(bf16[128,256]{1,0:T(8,128)(2,1)S(1)} %get-tuple-element.81), channel_id=1, source_target_pairs={{0,6},{1,7},{2,4},{3,5},{4,2},{5,3},{6,0},{7,1},{8,14},{9,15},{10,... | collective-permute-start | bytes 196616 | tf_op jit(solution)/shard_map/ppermute | solution.py:340
  11.9 0.7 copy-done.2
  12.6 2.2 %shard_map.120 = (bf16[4,256,1024]{2,1,0:T(8,128)(2,1)S(1)}, bf16[4,1024,256]{2,1,0:T(8,128)(2,1)S(1)}, bf16[512,1024]{1,0:T(8,128)(2,1)S(1)}, bf16[1024,512]{1,0:T(8,128)(2,1)S(1)}, f32[512,128]{1,0:T(8,128)S(1)}) custom-call(bf16[4,256,1024]{2,1,0:T(8,128)(2,1)} %win_hbm.1, bf16[4,1024,256]{2,1,0:T(8,128)(2,1)} %wout_hbm.1, ...), custom_call_target="tpu_custom_call" | custom-call | bytes 16777216 | tf_op jit(solution)/shard_map/pallas_call | solution.py:327
  14.9 3.8 %collective-permute-done.4.refs_5_ = bf16[128,256]{1,0:T(8,128)(2,1)S(1)} collective-permute-done((bf16[128,256]{1,0:T(8,128)(2,1)S(1)}, bf16[128,256]{1,0:T(8,128)(2,1)S(1)}, u32[]{:S(2)}, u32[]{:S(2)}) %collective-permute-start.4) | collective-permute-done | bytes 65568 | tf_op jit(solution)/shard_map/ppermute | solution.py:340
  18.7 1.5 %shard_map.121 = (bf16[128,256]{1,0:T(8,128)(2,1)S(1)}, bf16[128,256]{1,0:T(8,128)(2,1)S(1)}, bf16[128,256]{1,0:T(8,128)(2,1)S(1)}, bf16[128,256]{1,0:T(8,128)(2...) custom-call(bf16[4,256,1024]{2,1,0:T(8,128)(2,1)S(1)} %get-tuple-ele, ...), custom_call_target="tpu_custom_call" | custom-call | flops 1073741824 | bytes 6291456 | tf_op jit(solution)/shard_map/pallas_call | solution.py:327
  20.2 4.6 %collective-permute-start.10 = (bf16[128,256]{1,0:T(8,128)(2,1)S(1)}, bf16[128,256]{1,0:T(8,128)(2,1)S(1)}, u32[]{:S(2)}, u32[]{:S(2)}) collective-permute-start(bf16[128,256]{1,0:T(8,128)(2,1)S(1)} %get-tuple-element.87), channel_id=1, source_target_pairs={{0,4},{1,5},{2,6},{3,7},{4,0},{5,1},{6,2},{7,3},{8,12},{9,13},{10,... | collective-permute-start | bytes 196616 | tf_op jit(solution)/shard_map/ppermute | solution.py:340
  24.8 1.5 %collective-permute-start.14 = (bf16[512,256]{1,0:T(8,128)(2,1)S(1)}, bf16[512,256]{1,0:T(8,128)(2,1)S(1)}, u32[]{:S(2)}, u32[]{:S(2)}) collective-permute-start(bf16[512,256]{1,0:T(8,128)(2,1)S(1)} %bitcast.5), channel_id=1, source_target_pairs={{0,8},{8,0},{16,24},{24,16},{1,9},{9,1},{17,25},{25,17},{2,10},{10... | collective-permute-start | bytes 786440 | tf_op jit(solution)/shard_map/ppermute | solution.py:340
  26.3 1.5 %collective-permute-start.15 = (bf16[512,256]{1,0:T(8,128)(2,1)S(1)}, bf16[512,256]{1,0:T(8,128)(2,1)S(1)}, u32[]{:S(2)}, u32[]{:S(2)}) collective-permute-start(bf16[512,256]{1,0:T(8,128)(2,1)S(1)} %bitcast.6), channel_id=1, source_target_pairs={{0,16},{8,24},{16,0},{24,8},{1,17},{9,25},{17,1},{25,9},{2,18},{10... | collective-permute-start | bytes 786440 | tf_op jit(solution)/shard_map/ppermute | solution.py:340
  28.6 0.9 collective-permute-start.12
  29.5 5.5 %collective-permute-done.11.refs_5_ = bf16[128,256]{1,0:T(8,128)(2,1)S(1)} collective-permute-done((bf16[128,256]{1,0:T(8,128)(2,1)S(1)}, bf16[128,256]{1,0:T(8,128)(2,1)S(1)}, u32[]{:S(2)}, u32[]{:S(2)}) %collective-permute-start.11) | collective-permute-done | bytes 65568 | tf_op jit(solution)/shard_map/ppermute | solution.py:340
  35.0 2.6 %collective-permute-start.7 = (bf16[128,256]{1,0:T(8,128)(2,1)S(1)}, bf16[128,256]{1,0:T(8,128)(2,1)S(1)}, u32[]{:S(2)}, u32[]{:S(2)}) collective-permute-start(bf16[128,256]{1,0:T(8,128)(2,1)S(1)} %get-tuple-element.84), channel_id=1, source_target_pairs={{0,1},{1,0},{2,3},{3,2},{4,5},{5,4},{6,7},{7,6},{8,9},{9,8},{10,11... | collective-permute-start | bytes 196616 | tf_op jit(solution)/shard_map/ppermute | solution.py:340
  37.6 2.9 %collective-permute-done.13.refs_7_ = bf16[128,256]{1,0:T(8,128)(2,1)S(1)} collective-permute-done((bf16[128,256]{1,0:T(8,128)(2,1)S(1)}, bf16[128,256]{1,0:T(8,128)(2,1)S(1)}, u32[]{:S(2)}, u32[]{:S(2)}) %collective-permute-start.13) | collective-permute-done | bytes 65568 | tf_op jit(solution)/shard_map/ppermute | solution.py:340
  40.9 4.0 %collective-permute-done.8.refs_2_ = bf16[128,256]{1,0:T(8,128)(2,1)S(1)} collective-permute-done((bf16[128,256]{1,0:T(8,128)(2,1)S(1)}, bf16[128,256]{1,0:T(8,128)(2,1)S(1)}, u32[]{:S(2)}, u32[]{:S(2)}) %collective-permute-start.8) | collective-permute-done | bytes 65568 | tf_op jit(solution)/shard_map/ppermute | solution.py:340
  44.9 2.2 %shard_map.122 = (bf16[512,256]{1,0:T(8,128)(2,1)S(1)}, f32[512,256]{1,0:T(8,128)S(1)}, f32[512,128]{1,0:T(8,128)S(1)}, f32[40,128]{1,0:T(8,128)S(1)}, f32[4,512,512]{2,1,0:T(8,128)S(1)}) custom-call(bf16[512,256]{1,0:T(8,128)(2,1)S(1)} %bitcast.12, bf16[512,1024]{1,0:T(8,128)(2,1)S(1)} %get-tuple-element.71.pick_ref, ...), custom_call_target="tpu_custom_call" | custom-call | flops 1073741824 | bytes 4194304 | tf_op jit(solution)/shard_map/pallas_call | solution.py:327
  47.1 1.5 %collective-permute-start.17 = (f32[40,128]{1,0:T(8,128)S(1)}, f32[40,128]{1,0:T(8,128)S(1)}, u32[]{:S(2)}, u32[]{:S(2)}) collective-permute-start(f32[40,128]{1,0:T(8,128)S(1)} %get-tuple-element.94.refs_4_), channel_id=1, source_target_pairs={{0,8},{8,0},{16,24},{24,16},{1,9},{9,1},{17,25},{25,17},{2,10},{10... | collective-permute-start | bytes 61448 | tf_op jit(solution)/shard_map/ppermute | solution.py:340
  48.7 1.5 %collective-permute-start.18 = (f32[40,128]{1,0:T(8,128)S(1)}, f32[40,128]{1,0:T(8,128)S(1)}, u32[]{:S(2)}, u32[]{:S(2)}) collective-permute-start(f32[40,128]{1,0:T(8,128)S(1)} %get-tuple-element.94.refs_4_), channel_id=1, source_target_pairs={{0,16},{8,24},{16,0},{24,8},{1,17},{9,25},{17,1},{25,9},{2,18},{10... | collective-permute-start | bytes 61448 | tf_op jit(solution)/shard_map/ppermute | solution.py:340
  51.0 1.5 %collective-permute-done.18.refs_6_ = f32[40,128]{1,0:T(8,128)S(1)} collective-permute-done((f32[40,128]{1,0:T(8,128)S(1)}, f32[40,128]{1,0:T(8,128)S(1)}, u32[]{:S(2)}, u32[]{:S(2)}) %collective-permute-start.18) | collective-permute-done | bytes 20512 | tf_op jit(solution)/shard_map/ppermute | solution.py:340
  52.5 2.4 %collective-permute-done.19.refs_7_ = f32[40,128]{1,0:T(8,128)S(1)} collective-permute-done((f32[40,128]{1,0:T(8,128)S(1)}, f32[40,128]{1,0:T(8,128)S(1)}, u32[]{:S(2)}, u32[]{:S(2)}) %collective-permute-start.19) | collective-permute-done | bytes 20512 | tf_op jit(solution)/shard_map/ppermute | solution.py:340
  54.9 1.8 %shard_map.123 = (f32[512,256]{1,0:T(8,128)S(1)}, f32[1,512]{1,0:T(1,128)S(1)}, bf16[128,256]{1,0:T(8,128)(2,1)S(1)}, bf16[128,256]{1,0:T(8,128)(2,1)S(1)}, bf16...) custom-call(bf16[1024,512]{1,0:T(8,128)(2,1)S(1)} %get-tuple-element, ...), custom_call_target="tpu_custom_call" | custom-call | flops 1610612736 | bytes 4194304 | tf_op jit(solution)/shard_map/pallas_call | solution.py:327
  56.7 1.4 %collective-permute-start.24 = (bf16[128,256]{1,0:T(8,128)(2,1)S(1)}, bf16[128,256]{1,0:T(8,128)(2,1)S(1)}, u32[]{:S(2)}, u32[]{:S(2)}) collective-permute-start(bf16[128,256]{1,0:T(8,128)(2,1)S(1)} %get-tuple-element.102), channel_id=1, source_target_pairs={{0,2},{1,3},{2,0},{3,1},{4,6},{5,7},{6,4},{7,5},{8,10},{9,11},{10,... | collective-permute-start | bytes 196616 | tf_op jit(solution)/shard_map/ppermute | solution.py:340
  58.6 2.3 %collective-permute-start.26 = (bf16[128,256]{1,0:T(8,128)(2,1)S(1)}, bf16[128,256]{1,0:T(8,128)(2,1)S(1)}, u32[]{:S(2)}, u32[]{:S(2)}) collective-permute-start(bf16[128,256]{1,0:T(8,128)(2,1)S(1)} %get-tuple-element.104), channel_id=1, source_target_pairs={{0,4},{1,5},{2,6},{3,7},{4,0},{5,1},{6,2},{7,3},{8,12},{9,13},{10,... | collective-permute-start | bytes 196616 | tf_op jit(solution)/shard_map/ppermute | solution.py:340
  61.2 2.5 %collective-permute-start.28 = (bf16[128,256]{1,0:T(8,128)(2,1)S(1)}, bf16[128,256]{1,0:T(8,128)(2,1)S(1)}, u32[]{:S(2)}, u32[]{:S(2)}) collective-permute-start(bf16[128,256]{1,0:T(8,128)(2,1)S(1)} %get-tuple-element.106), channel_id=1, source_target_pairs={{0,6},{1,7},{2,4},{3,5},{4,2},{5,3},{6,0},{7,1},{8,14},{9,15},{10,... | collective-permute-start | bytes 196616 | tf_op jit(solution)/shard_map/ppermute | solution.py:340
  63.7 1.1 collective-permute-start.29
  65.4 2.4 %shard_map.125.slope_ref = f32[4,256,1024]{2,1,0:T(8,128)S(1)} custom-call(bf16[4,256,1024]{2,1,0:T(8,128)(2,1)S(1)} %get-tuple-element.73.win_ref, bf16[128,256]{1,0:T(8,128)(2,1)S(1)} %get-tuple-element.75.refs_0_, bf16[128,256]{1,0:T(8,128)(2,1)S(1)} %collective-permute-done.refs_1_, bf16[128,256]{1,0:T(8,128)(2,1)S(1)} %collective-permute-done.1.refs_2_, ...), custom_call_target="tpu_custom_call" | custom-call | flops 536870912 | bytes 6291456 | tf_op jit(solution)/shard_map/pallas_call | solution.py:327
  68.4 2.8 %collective-permute-done.27.refs_5_ = bf16[128,256]{1,0:T(8,128)(2,1)S(1)} collective-permute-done((bf16[128,256]{1,0:T(8,128)(2,1)S(1)}, bf16[128,256]{1,0:T(8,128)(2,1)S(1)}, u32[]{:S(2)}, u32[]{:S(2)}) %collective-permute-start.27) | collective-permute-done | bytes 65568 | tf_op jit(solution)/shard_map/ppermute | solution.py:340
  71.7 1.6 %shard_map.126 = (bf16[128,256]{1,0:T(8,128)(2,1)S(1)}, bf16[128,256]{1,0:T(8,128)(2,1)S(1)}, bf16[128,256]{1,0:T(8,128)(2,1)S(1)}, bf16[128,256]{1,0:T(8,128)(2...) custom-call(bf16[4,256,1024]{2,1,0:T(8,128)(2,1)S(1)} %get-tuple-ele, ...), custom_call_target="tpu_custom_call" | custom-call | flops 1073741824 | bytes 6291456 | tf_op jit(solution)/shard_map/pallas_call | solution.py:327
  73.4 3.2 %collective-permute-start.31 = (bf16[128,256]{1,0:T(8,128)(2,1)S(1)}, bf16[128,256]{1,0:T(8,128)(2,1)S(1)}, u32[]{:S(2)}, u32[]{:S(2)}) collective-permute-start(bf16[128,256]{1,0:T(8,128)(2,1)S(1)} %get-tuple-element.110), channel_id=1, source_target_pairs={{0,2},{1,3},{2,0},{3,1},{4,6},{5,7},{6,4},{7,5},{8,10},{9,11},{10,... | collective-permute-start | bytes 196616 | tf_op jit(solution)/shard_map/ppermute | solution.py:340
  76.6 1.9 %collective-permute-start.33 = (bf16[128,256]{1,0:T(8,128)(2,1)S(1)}, bf16[128,256]{1,0:T(8,128)(2,1)S(1)}, u32[]{:S(2)}, u32[]{:S(2)}) collective-permute-start(bf16[128,256]{1,0:T(8,128)(2,1)S(1)} %get-tuple-element.112), channel_id=1, source_target_pairs={{0,4},{1,5},{2,6},{3,7},{4,0},{5,1},{6,2},{7,3},{8,12},{9,13},{10,... | collective-permute-start | bytes 196616 | tf_op jit(solution)/shard_map/ppermute | solution.py:340
  78.4 0.7 collective-permute-start.40
  79.7 2.3 %collective-permute-start.42 = (bf16[256,256]{1,0:T(8,128)(2,1)S(1)}, bf16[256,256]{1,0:T(8,128)(2,1)S(1)}, u32[]{:S(2)}, u32[]{:S(2)}) collective-permute-start(bf16[256,256]{1,0:T(8,128)(2,1)S(1)} %get-tuple-element.126), channel_id=1, source_target_pairs={{0,24},{8,16},{16,8},{24,0},{1,25},{9,17},{17,9},{25,1},{2,26},{10... | collective-permute-start | bytes 393224 | tf_op jit(solution)/shard_map/ppermute | solution.py:340
  82.7 0.9 collective-permute-start.34
  83.6 2.6 %shard_map.129 = (bf16[1024,1024]{1,0:T(8,128)(2,1)S(1)}, bf16[1024,1024]{1,0:T(8,128)(2,1)S(1)}, bf16[256,1024]{1,0:T(8,128)(2,1)S(1)}) custom-call(bf16[4,256,1024]{2,1,0:T(8,128)(2,1)S(1)} %get-tuple-element.73.win_ref, bf16[256,256]{1,0:T(8,128)(2,1)S(1)} %get-tuple-element.116.refs_0_, bf16[256,256]{1,0:T(8,128)(2,1)S(1)} %collective-permute-done.37.refs_1_, ...), custom_call_target="tpu_custom_call" | custom-call | flops 536870912 | bytes 6291456 | tf_op jit(solution)/shard_map/pallas_call | solution.py:327
  86.2 3.0 %collective-permute-done.34.refs_5_ = bf16[128,256]{1,0:T(8,128)(2,1)S(1)} collective-permute-done((bf16[128,256]{1,0:T(8,128)(2,1)S(1)}, bf16[128,256]{1,0:T(8,128)(2,1)S(1)}, u32[]{:S(2)}, u32[]{:S(2)}) %collective-permute-start.34) | collective-permute-done | bytes 65568 | tf_op jit(solution)/shard_map/ppermute | solution.py:340
  89.8 2.4 %collective-permute-start.22 = (bf16[512,256]{1,0:T(8,128)(2,1)S(1)}, bf16[512,256]{1,0:T(8,128)(2,1)S(1)}, u32[]{:S(2)}, u32[]{:S(2)}) collective-permute-start(bf16[512,256]{1,0:T(8,128)(2,1)S(1)} %get-tuple-element.96.refs_0_), channel_id=1, source_target_pairs={{0,24},{8,16},{16,8},{24,0},{1,25},{9,17},{17,9},{25,1},{2,26},{10... | collective-permute-start | bytes 786440 | tf_op jit(solution)/shard_map/ppermute | solution.py:340
  92.3 1.8 %collective-permute-start.35 = (bf16[128,256]{1,0:T(8,128)(2,1)S(1)}, bf16[128,256]{1,0:T(8,128)(2,1)S(1)}, u32[]{:S(2)}, u32[]{:S(2)}) collective-permute-start(bf16[128,256]{1,0:T(8,128)(2,1)S(1)} %get-tuple-element.114), channel_id=1, source_target_pairs={{0,6},{1,7},{2,4},{3,5},{4,2},{5,3},{6,0},{7,1},{8,14},{9,15},{10,... | collective-permute-start | bytes 196616 | tf_op jit(solution)/shard_map/ppermute | solution.py:340
  94.1 0.9 collective-permute-start.36
  95.0 1.9 %shard_map.131 = (bf16[512,256]{1,0:T(8,128)(2,1)S(1)}, bf16[512,256]{1,0:T(8,128)(2,1)S(1)}, bf16[512,256]{1,0:T(8,128)(2,1)S(1)}, bf16[512,256]{1,0:T(8,128)(2,1)S(1)}) custom-call(bf16[4,1024,256]{2,1,0:T(8,128)(2,1)S(1)} %get-tuple-element.74.wout_ref, bf16[1024,1024]{1,0:T(8,128)(2,1)S(1)} %get-tuple-element.120.act_ref, ...), custom_call_target="tpu_custom_call" | custom-call | flops 1610612736 | bytes 6291456 | tf_op jit(solution)/shard_map/pallas_call | solution.py:327
  96.9 1.6 %collective-permute-done.35.refs_6_ = bf16[128,256]{1,0:T(8,128)(2,1)S(1)} collective-permute-done((bf16[128,256]{1,0:T(8,128)(2,1)S(1)}, bf16[128,256]{1,0:T(8,128)(2,1)S(1)}, u32[]{:S(2)}, u32[]{:S(2)}) %collective-permute-start.35) | collective-permute-done | bytes 65568 | tf_op jit(solution)/shard_map/ppermute | solution.py:340
  98.9 0.9 collective-permute-done.36.refs_7_
  100.4 1.5 %collective-permute-start.45 = (bf16[512,256]{1,0:T(8,128)(2,1)S(1)}, bf16[512,256]{1,0:T(8,128)(2,1)S(1)}, u32[]{:S(2)}, u32[]{:S(2)}) collective-permute-start(bf16[512,256]{1,0:T(8,128)(2,1)S(1)} %get-tuple-element.130), channel_id=1, source_target_pairs={{0,24},{8,16},{16,8},{24,0},{1,25},{9,17},{17,9},{25,1},{2,26},{10... | collective-permute-start | bytes 786440 | tf_op jit(solution)/shard_map/ppermute | solution.py:340
  101.9 1.3 %shard_map.127 = f32[512,256]{1,0:T(8,128)} custom-call(bf16[512,256]{1,0:T(8,128)(2,1)S(1)} %bitcast.13, bf16[512,1024]{1,0:T(8,128)(2,1)S(1)} %get-tuple-element.71.pick_ref, f32[512,256]{1,0:T(8,128)S(1)} %get-tuple-element.99.summed_ref, bf16[128,256]{1,0:T(8,128)(2,1)S(1)} %get-tuple-element.108.refs_0_, ...), custom_call_target="tpu_custom_call" | custom-call | flops 268435456 | bytes 2097152 | tf_op jit(solution)/shard_map/pallas_call | solution.py:327
  103.3 0.8 collective-permute-done.21.refs_2_
  104.1 3.0 %shard_map.124 = (f32[1,512]{1,0:T(1,128)}, f32[512,256]{1,0:T(8,128)}) custom-call(bf16[512,256]{1,0:T(8,128)(2,1)S(1)} %bitcast.10, s32[1,2048]{1,0:T(1,128)S(1)} %copy-done.3, f32[1,512]{1,0:T(1,128)S(1)} %get-tuple-element.95.lse_ref, f32[1,512]{1,0:T(1,128)S(1)} %copy-done.4, s32[1,512]{1,0:T(1,128)S(1)} %copy-done.5, ...), custom_call_target="tpu_custom_call" | custom-call | flops 1073741824 | bytes 3145728 | tf_op jit(solution)/shard_map/pallas_call | solution.py:327
  107.6 6.8 %collective-permute-done.44.refs_2_ = bf16[512,256]{1,0:T(8,128)(2,1)S(1)} collective-permute-done((bf16[512,256]{1,0:T(8,128)(2,1)S(1)}, bf16[512,256]{1,0:T(8,128)(2,1)S(1)}, u32[]{:S(2)}, u32[]{:S(2)}) %collective-permute-start.44) | collective-permute-done | bytes 262176 | tf_op jit(solution)/shard_map/ppermute | solution.py:340
  114.5 1.6 %shard_map.132 = (f32[64,4,1024]{2,1,0:T(4,128)}, f32[256,4,256]{2,1,0:T(4,128)}) custom-call(bf16[512,256]{1,0:T(8,128)(2,1)S(1)} %get-tuple-element.127.refs_0_, bf16[512,256]{1,0:T(8,128)(2,1)S(1)} %collective-permute-done.43.refs_1_, bf16[512,256]{1,0:T(8,128)(2,1)S(1)} %collective-permute-done.44.refs_2_, ...), custom_call_target="tpu_custom_call" | custom-call | flops 536870912 | bytes 6291456 | tf_op jit(solution)/shard_map/pallas_call | solution.py:327
  (70 shorter events, 8.8 us)
Async XLA Ops:
  2.2 6.0 %collective-permute-start = (bf16[128,256]{1,0:T(8,128)(2,1)S(1)}, bf16[128,256]{1,0:T(8,128)(2,1)S(1)}, u32[]{:S(2)}, u32[]{:S(2)}) collective-permute-start(bf16[128,256]{1,0:T(8,128)(2,1)S(1)} %get-tuple-element.76), channel_id=1, source_target_pairs={{0,1},{1,0},{2,3},{3,2},{4,5},{5,4},{6,7},{7,6},{8,9},{9,8},{10,11... | collective-permute-start | bytes 196616 | tf_op jit(solution)/shard_map/ppermute | solution.py:340
  2.7 9.1 %collective-permute-start.1 = (bf16[128,256]{1,0:T(8,128)(2,1)S(1)}, bf16[128,256]{1,0:T(8,128)(2,1)S(1)}, u32[]{:S(2)}, u32[]{:S(2)}) collective-permute-start(bf16[128,256]{1,0:T(8,128)(2,1)S(1)} %get-tuple-element.77), channel_id=1, source_target_pairs={{0,2},{1,3},{2,0},{3,1},{4,6},{5,7},{6,4},{7,5},{8,10},{9,11},{10,... | collective-permute-start | bytes 196616 | tf_op jit(solution)/shard_map/ppermute | solution.py:340
  5.4 9.5 %collective-permute-start.2 = (bf16[128,256]{1,0:T(8,128)(2,1)S(1)}, bf16[128,256]{1,0:T(8,128)(2,1)S(1)}, u32[]{:S(2)}, u32[]{:S(2)}) collective-permute-start(bf16[128,256]{1,0:T(8,128)(2,1)S(1)} %get-tuple-element.78), channel_id=1, source_target_pairs={{0,3},{1,2},{2,1},{3,0},{4,7},{5,6},{6,5},{7,4},{8,11},{9,10},{10,... | collective-permute-start | bytes 196616 | tf_op jit(solution)/shard_map/ppermute | solution.py:340
  5.4 9.5 %collective-permute-start.3 = (bf16[128,256]{1,0:T(8,128)(2,1)S(1)}, bf16[128,256]{1,0:T(8,128)(2,1)S(1)}, u32[]{:S(2)}, u32[]{:S(2)}) collective-permute-start(bf16[128,256]{1,0:T(8,128)(2,1)S(1)} %get-tuple-element.79), channel_id=1, source_target_pairs={{0,4},{1,5},{2,6},{3,7},{4,0},{5,1},{6,2},{7,3},{8,12},{9,13},{10,... | collective-permute-start | bytes 196616 | tf_op jit(solution)/shard_map/ppermute | solution.py:340
  8.2 10.5 %collective-permute-start.4 = (bf16[128,256]{1,0:T(8,128)(2,1)S(1)}, bf16[128,256]{1,0:T(8,128)(2,1)S(1)}, u32[]{:S(2)}, u32[]{:S(2)}) collective-permute-start(bf16[128,256]{1,0:T(8,128)(2,1)S(1)} %get-tuple-element.80), channel_id=1, source_target_pairs={{0,5},{1,4},{2,7},{3,6},{4,1},{5,0},{6,3},{7,2},{8,13},{9,12},{10,... | collective-permute-start | bytes 196616 | tf_op jit(solution)/shard_map/ppermute | solution.py:340
  8.2 10.5 %collective-permute-start.5 = (bf16[128,256]{1,0:T(8,128)(2,1)S(1)}, bf16[128,256]{1,0:T(8,128)(2,1)S(1)}, u32[]{:S(2)}, u32[]{:S(2)}) collective-permute-start(bf16[128,256]{1,0:T(8,128)(2,1)S(1)} %get-tuple-element.81), channel_id=1, source_target_pairs={{0,6},{1,7},{2,4},{3,5},{4,2},{5,3},{6,0},{7,1},{8,14},{9,15},{10,... | collective-permute-start | bytes 196616 | tf_op jit(solution)/shard_map/ppermute | solution.py:340
  11.8 6.9 %collective-permute-start.6 = (bf16[128,256]{1,0:T(8,128)(2,1)S(1)}, bf16[128,256]{1,0:T(8,128)(2,1)S(1)}, u32[]{:S(2)}, u32[]{:S(2)}) collective-permute-start(bf16[128,256]{1,0:T(8,128)(2,1)S(1)} %get-tuple-element.82), channel_id=1, source_target_pairs={{0,7},{1,6},{2,5},{3,4},{4,3},{5,2},{6,1},{7,0},{8,15},{9,14},{10,... | collective-permute-start | bytes 196616 | tf_op jit(solution)/shard_map/ppermute | solution.py:340
  18.7 26.2 %copy-start.1 = (bf16[1,512,256]{2,1,0:T(8,128)(2,1)S(1)}, bf16[1,512,256]{2,1,0:T(8,128)(2,1)}, u32[]{:S(2)}) copy-start(bf16[1,512,256]{2,1,0:T(8,128)(2,1)} %param.8) | copy-start | bytes 786436
  18.7 26.2 %copy-start.4 = (f32[1,512]{1,0:T(1,128)S(1)}, f32[1,512]{1,0:T(1,128)}, u32[]{:S(2)}) copy-start(f32[1,512]{1,0:T(1,128)} %w_ref.3) | copy-start | bytes 6148
  20.2 8.3 %collective-permute-start.10 = (bf16[128,256]{1,0:T(8,128)(2,1)S(1)}, bf16[128,256]{1,0:T(8,128)(2,1)S(1)}, u32[]{:S(2)}, u32[]{:S(2)}) collective-permute-start(bf16[128,256]{1,0:T(8,128)(2,1)S(1)} %get-tuple-element.87), channel_id=1, source_target_pairs={{0,4},{1,5},{2,6},{3,7},{4,0},{5,1},{6,2},{7,3},{8,12},{9,13},{10,... | collective-permute-start | bytes 196616 | tf_op jit(solution)/shard_map/ppermute | solution.py:340
  24.8 20.1 %collective-permute-start.14 = (bf16[512,256]{1,0:T(8,128)(2,1)S(1)}, bf16[512,256]{1,0:T(8,128)(2,1)S(1)}, u32[]{:S(2)}, u32[]{:S(2)}) collective-permute-start(bf16[512,256]{1,0:T(8,128)(2,1)S(1)} %bitcast.5), channel_id=1, source_target_pairs={{0,8},{8,0},{16,24},{24,16},{1,9},{9,1},{17,25},{25,17},{2,10},{10... | collective-permute-start | bytes 786440 | tf_op jit(solution)/shard_map/ppermute | solution.py:340
  26.3 18.6 %collective-permute-start.15 = (bf16[512,256]{1,0:T(8,128)(2,1)S(1)}, bf16[512,256]{1,0:T(8,128)(2,1)S(1)}, u32[]{:S(2)}, u32[]{:S(2)}) collective-permute-start(bf16[512,256]{1,0:T(8,128)(2,1)S(1)} %bitcast.6), channel_id=1, source_target_pairs={{0,16},{8,24},{16,0},{24,8},{1,17},{9,25},{17,1},{25,9},{2,18},{10... | collective-permute-start | bytes 786440 | tf_op jit(solution)/shard_map/ppermute | solution.py:340
  27.8 17.1 %collective-permute-start.16 = (bf16[512,256]{1,0:T(8,128)(2,1)S(1)}, bf16[512,256]{1,0:T(8,128)(2,1)S(1)}, u32[]{:S(2)}, u32[]{:S(2)}) collective-permute-start(bf16[512,256]{1,0:T(8,128)(2,1)S(1)} %bitcast.7), channel_id=1, source_target_pairs={{0,24},{8,16},{16,8},{24,0},{1,25},{9,17},{17,9},{25,1},{2,26},{10... | collective-permute-start | bytes 786440 | tf_op jit(solution)/shard_map/ppermute | solution.py:340
  28.3 6.7 %collective-permute-start.11 = (bf16[128,256]{1,0:T(8,128)(2,1)S(1)}, bf16[128,256]{1,0:T(8,128)(2,1)S(1)}, u32[]{:S(2)}, u32[]{:S(2)}) collective-permute-start(bf16[128,256]{1,0:T(8,128)(2,1)S(1)} %get-tuple-element.88), channel_id=1, source_target_pairs={{0,5},{1,4},{2,7},{3,6},{4,1},{5,0},{6,3},{7,2},{8,13},{9,12},{10,... | collective-permute-start | bytes 196616 | tf_op jit(solution)/shard_map/ppermute | solution.py:340
  28.6 6.4 %collective-permute-start.12 = (bf16[128,256]{1,0:T(8,128)(2,1)S(1)}, bf16[128,256]{1,0:T(8,128)(2,1)S(1)}, u32[]{:S(2)}, u32[]{:S(2)}) collective-permute-start(bf16[128,256]{1,0:T(8,128)(2,1)S(1)} %get-tuple-element.89), channel_id=1, source_target_pairs={{0,6},{1,7},{2,4},{3,5},{4,2},{5,3},{6,0},{7,1},{8,14},{9,15},{10,... | collective-permute-start | bytes 196616 | tf_op jit(solution)/shard_map/ppermute | solution.py:340
  35.0 5.5 %collective-permute-start.13 = (bf16[128,256]{1,0:T(8,128)(2,1)S(1)}, bf16[128,256]{1,0:T(8,128)(2,1)S(1)}, u32[]{:S(2)}, u32[]{:S(2)}) collective-permute-start(bf16[128,256]{1,0:T(8,128)(2,1)S(1)} %get-tuple-element.90), channel_id=1, source_target_pairs={{0,7},{1,6},{2,5},{3,4},{4,3},{5,2},{6,1},{7,0},{8,15},{9,14},{10,... | collective-permute-start | bytes 196616 | tf_op jit(solution)/shard_map/ppermute | solution.py:340
  35.0 5.5 %collective-permute-start.7 = (bf16[128,256]{1,0:T(8,128)(2,1)S(1)}, bf16[128,256]{1,0:T(8,128)(2,1)S(1)}, u32[]{:S(2)}, u32[]{:S(2)}) collective-permute-start(bf16[128,256]{1,0:T(8,128)(2,1)S(1)} %get-tuple-element.84), channel_id=1, source_target_pairs={{0,1},{1,0},{2,3},{3,2},{4,5},{5,4},{6,7},{7,6},{8,9},{9,8},{10,11... | collective-permute-start | bytes 196616 | tf_op jit(solution)/shard_map/ppermute | solution.py:340
  40.5 4.4 %collective-permute-start.8 = (bf16[128,256]{1,0:T(8,128)(2,1)S(1)}, bf16[128,256]{1,0:T(8,128)(2,1)S(1)}, u32[]{:S(2)}, u32[]{:S(2)}) collective-permute-start(bf16[128,256]{1,0:T(8,128)(2,1)S(1)} %get-tuple-element.85), channel_id=1, source_target_pairs={{0,2},{1,3},{2,0},{3,1},{4,6},{5,7},{6,4},{7,5},{8,10},{9,11},{10,... | collective-permute-start | bytes 196616 | tf_op jit(solution)/shard_map/ppermute | solution.py:340
  40.5 4.4 %collective-permute-start.9 = (bf16[128,256]{1,0:T(8,128)(2,1)S(1)}, bf16[128,256]{1,0:T(8,128)(2,1)S(1)}, u32[]{:S(2)}, u32[]{:S(2)}) collective-permute-start(bf16[128,256]{1,0:T(8,128)(2,1)S(1)} %get-tuple-element.86), channel_id=1, source_target_pairs={{0,3},{1,2},{2,1},{3,0},{4,7},{5,6},{6,5},{7,4},{8,11},{9,10},{10,... | collective-permute-start | bytes 196616 | tf_op jit(solution)/shard_map/ppermute | solution.py:340
  47.1 3.8 %collective-permute-start.17 = (f32[40,128]{1,0:T(8,128)S(1)}, f32[40,128]{1,0:T(8,128)S(1)}, u32[]{:S(2)}, u32[]{:S(2)}) collective-permute-start(f32[40,128]{1,0:T(8,128)S(1)} %get-tuple-element.94.refs_4_), channel_id=1, source_target_pairs={{0,8},{8,0},{16,24},{24,16},{1,9},{9,1},{17,25},{25,17},{2,10},{10... | collective-permute-start | bytes 61448 | tf_op jit(solution)/shard_map/ppermute | solution.py:340
  48.7 3.8 %collective-permute-start.18 = (f32[40,128]{1,0:T(8,128)S(1)}, f32[40,128]{1,0:T(8,128)S(1)}, u32[]{:S(2)}, u32[]{:S(2)}) collective-permute-start(f32[40,128]{1,0:T(8,128)S(1)} %get-tuple-element.94.refs_4_), channel_id=1, source_target_pairs={{0,16},{8,24},{16,0},{24,8},{1,17},{9,25},{17,1},{25,9},{2,18},{10... | collective-permute-start | bytes 61448 | tf_op jit(solution)/shard_map/ppermute | solution.py:340
  50.2 4.7 %collective-permute-start.19 = (f32[40,128]{1,0:T(8,128)S(1)}, f32[40,128]{1,0:T(8,128)S(1)}, u32[]{:S(2)}, u32[]{:S(2)}) collective-permute-start(f32[40,128]{1,0:T(8,128)S(1)} %get-tuple-element.94.refs_4_), channel_id=1, source_target_pairs={{0,24},{8,16},{16,8},{24,0},{1,25},{9,17},{17,9},{25,1},{2,26},{10... | collective-permute-start | bytes 61448 | tf_op jit(solution)/shard_map/ppermute | solution.py:340
  56.7 4.5 %collective-permute-start.23 = (bf16[128,256]{1,0:T(8,128)(2,1)S(1)}, bf16[128,256]{1,0:T(8,128)(2,1)S(1)}, u32[]{:S(2)}, u32[]{:S(2)}) collective-permute-start(bf16[128,256]{1,0:T(8,128)(2,1)S(1)} %get-tuple-element.101), channel_id=1, source_target_pairs={{0,1},{1,0},{2,3},{3,2},{4,5},{5,4},{6,7},{7,6},{8,9},{9,8},{10,11... | collective-permute-start | bytes 196616 | tf_op jit(solution)/shard_map/ppermute | solution.py:340
  56.7 6.9 %collective-permute-start.24 = (bf16[128,256]{1,0:T(8,128)(2,1)S(1)}, bf16[128,256]{1,0:T(8,128)(2,1)S(1)}, u32[]{:S(2)}, u32[]{:S(2)}) collective-permute-start(bf16[128,256]{1,0:T(8,128)(2,1)S(1)} %get-tuple-element.102), channel_id=1, source_target_pairs={{0,2},{1,3},{2,0},{3,1},{4,6},{5,7},{6,4},{7,5},{8,10},{9,11},{10,... | collective-permute-start | bytes 196616 | tf_op jit(solution)/shard_map/ppermute | solution.py:340
  58.1 6.7 %collective-permute-start.25 = (bf16[128,256]{1,0:T(8,128)(2,1)S(1)}, bf16[128,256]{1,0:T(8,128)(2,1)S(1)}, u32[]{:S(2)}, u32[]{:S(2)}) collective-permute-start(bf16[128,256]{1,0:T(8,128)(2,1)S(1)} %get-tuple-element.103), channel_id=1, source_target_pairs={{0,3},{1,2},{2,1},{3,0},{4,7},{5,6},{6,5},{7,4},{8,11},{9,10},{10,... | collective-permute-start | bytes 196616 | tf_op jit(solution)/shard_map/ppermute | solution.py:340
  58.6 9.2 %collective-permute-start.26 = (bf16[128,256]{1,0:T(8,128)(2,1)S(1)}, bf16[128,256]{1,0:T(8,128)(2,1)S(1)}, u32[]{:S(2)}, u32[]{:S(2)}) collective-permute-start(bf16[128,256]{1,0:T(8,128)(2,1)S(1)} %get-tuple-element.104), channel_id=1, source_target_pairs={{0,4},{1,5},{2,6},{3,7},{4,0},{5,1},{6,2},{7,3},{8,12},{9,13},{10,... | collective-permute-start | bytes 196616 | tf_op jit(solution)/shard_map/ppermute | solution.py:340
  60.9 10.3 %collective-permute-start.27 = (bf16[128,256]{1,0:T(8,128)(2,1)S(1)}, bf16[128,256]{1,0:T(8,128)(2,1)S(1)}, u32[]{:S(2)}, u32[]{:S(2)}) collective-permute-start(bf16[128,256]{1,0:T(8,128)(2,1)S(1)} %get-tuple-element.105), channel_id=1, source_target_pairs={{0,5},{1,4},{2,7},{3,6},{4,1},{5,0},{6,3},{7,2},{8,13},{9,12},{10,... | collective-permute-start | bytes 196616 | tf_op jit(solution)/shard_map/ppermute | solution.py:340
  61.2 10.5 %collective-permute-start.28 = (bf16[128,256]{1,0:T(8,128)(2,1)S(1)}, bf16[128,256]{1,0:T(8,128)(2,1)S(1)}, u32[]{:S(2)}, u32[]{:S(2)}) collective-permute-start(bf16[128,256]{1,0:T(8,128)(2,1)S(1)} %get-tuple-element.106), channel_id=1, source_target_pairs={{0,6},{1,7},{2,4},{3,5},{4,2},{5,3},{6,0},{7,1},{8,14},{9,15},{10,... | collective-permute-start | bytes 196616 | tf_op jit(solution)/shard_map/ppermute | solution.py:340
  63.7 8.0 %collective-permute-start.29 = (bf16[128,256]{1,0:T(8,128)(2,1)S(1)}, bf16[128,256]{1,0:T(8,128)(2,1)S(1)}, u32[]{:S(2)}, u32[]{:S(2)}) collective-permute-start(bf16[128,256]{1,0:T(8,128)(2,1)S(1)} %get-tuple-element.107), channel_id=1, source_target_pairs={{0,7},{1,6},{2,5},{3,4},{4,3},{5,2},{6,1},{7,0},{8,15},{9,14},{10,... | collective-permute-start | bytes 196616 | tf_op jit(solution)/shard_map/ppermute | solution.py:340
  64.8 11.7 %collective-permute-start.37 = (bf16[256,256]{1,0:T(8,128)(2,1)S(1)}, bf16[256,256]{1,0:T(8,128)(2,1)S(1)}, u32[]{:S(2)}, u32[]{:S(2)}) collective-permute-start(bf16[256,256]{1,0:T(8,128)(2,1)S(1)} %get-tuple-element.117), channel_id=1, source_target_pairs={{0,8},{8,0},{16,24},{24,16},{1,9},{9,1},{17,25},{25,17},{2,10},{10... | collective-permute-start | bytes 393224 | tf_op jit(solution)/shard_map/ppermute | solution.py:340
  67.8 8.8 %collective-permute-start.38 = (bf16[256,256]{1,0:T(8,128)(2,1)S(1)}, bf16[256,256]{1,0:T(8,128)(2,1)S(1)}, u32[]{:S(2)}, u32[]{:S(2)}) collective-permute-start(bf16[256,256]{1,0:T(8,128)(2,1)S(1)} %get-tuple-element.118), channel_id=1, source_target_pairs={{0,16},{8,24},{16,0},{24,8},{1,17},{9,25},{17,1},{25,9},{2,18},{10... | collective-permute-start | bytes 393224 | tf_op jit(solution)/shard_map/ppermute | solution.py:340
  71.2 7.3 %collective-permute-start.39 = (bf16[256,256]{1,0:T(8,128)(2,1)S(1)}, bf16[256,256]{1,0:T(8,128)(2,1)S(1)}, u32[]{:S(2)}, u32[]{:S(2)}) collective-permute-start(bf16[256,256]{1,0:T(8,128)(2,1)S(1)} %get-tuple-element.119), channel_id=1, source_target_pairs={{0,24},{8,16},{16,8},{24,0},{1,25},{9,17},{17,9},{25,1},{2,26},{10... | collective-permute-start | bytes 393224 | tf_op jit(solution)/shard_map/ppermute | solution.py:340
  73.3 5.9 %collective-permute-start.30 = (bf16[128,256]{1,0:T(8,128)(2,1)S(1)}, bf16[128,256]{1,0:T(8,128)(2,1)S(1)}, u32[]{:S(2)}, u32[]{:S(2)}) collective-permute-start(bf16[128,256]{1,0:T(8,128)(2,1)S(1)} %get-tuple-element.109), channel_id=1, source_target_pairs={{0,1},{1,0},{2,3},{3,2},{4,5},{5,4},{6,7},{7,6},{8,9},{9,8},{10,11... | collective-permute-start | bytes 196616 | tf_op jit(solution)/shard_map/ppermute | solution.py:340
  73.4 6.3 %collective-permute-start.31 = (bf16[128,256]{1,0:T(8,128)(2,1)S(1)}, bf16[128,256]{1,0:T(8,128)(2,1)S(1)}, u32[]{:S(2)}, u32[]{:S(2)}) collective-permute-start(bf16[128,256]{1,0:T(8,128)(2,1)S(1)} %get-tuple-element.110), channel_id=1, source_target_pairs={{0,2},{1,3},{2,0},{3,1},{4,6},{5,7},{6,4},{7,5},{8,10},{9,11},{10,... | collective-permute-start | bytes 196616 | tf_op jit(solution)/shard_map/ppermute | solution.py:340
  76.5 5.7 %collective-permute-start.32 = (bf16[128,256]{1,0:T(8,128)(2,1)S(1)}, bf16[128,256]{1,0:T(8,128)(2,1)S(1)}, u32[]{:S(2)}, u32[]{:S(2)}) collective-permute-start(bf16[128,256]{1,0:T(8,128)(2,1)S(1)} %get-tuple-element.111), channel_id=1, source_target_pairs={{0,3},{1,2},{2,1},{3,0},{4,7},{5,6},{6,5},{7,4},{8,11},{9,10},{10,... | collective-permute-start | bytes 196616 | tf_op jit(solution)/shard_map/ppermute | solution.py:340
  76.6 6.1 %collective-permute-start.33 = (bf16[128,256]{1,0:T(8,128)(2,1)S(1)}, bf16[128,256]{1,0:T(8,128)(2,1)S(1)}, u32[]{:S(2)}, u32[]{:S(2)}) collective-permute-start(bf16[128,256]{1,0:T(8,128)(2,1)S(1)} %get-tuple-element.112), channel_id=1, source_target_pairs={{0,4},{1,5},{2,6},{3,7},{4,0},{5,1},{6,2},{7,3},{8,12},{9,13},{10,... | collective-permute-start | bytes 196616 | tf_op jit(solution)/shard_map/ppermute | solution.py:340
  78.4 11.4 %collective-permute-start.40 = (bf16[256,256]{1,0:T(8,128)(2,1)S(1)}, bf16[256,256]{1,0:T(8,128)(2,1)S(1)}, u32[]{:S(2)}, u32[]{:S(2)}) collective-permute-start(bf16[256,256]{1,0:T(8,128)(2,1)S(1)} %get-tuple-element.124), channel_id=1, source_target_pairs={{0,8},{8,0},{16,24},{24,16},{1,9},{9,1},{17,25},{25,17},{2,10},{10... | collective-permute-start | bytes 393224 | tf_op jit(solution)/shard_map/ppermute | solution.py:340
  79.1 13.2 %collective-permute-start.41 = (bf16[256,256]{1,0:T(8,128)(2,1)S(1)}, bf16[256,256]{1,0:T(8,128)(2,1)S(1)}, u32[]{:S(2)}, u32[]{:S(2)}) collective-permute-start(bf16[256,256]{1,0:T(8,128)(2,1)S(1)} %get-tuple-element.125), channel_id=1, source_target_pairs={{0,16},{8,24},{16,0},{24,8},{1,17},{9,25},{17,1},{25,9},{2,18},{10... | collective-permute-start | bytes 393224 | tf_op jit(solution)/shard_map/ppermute | solution.py:340
  79.7 14.4 %collective-permute-start.42 = (bf16[256,256]{1,0:T(8,128)(2,1)S(1)}, bf16[256,256]{1,0:T(8,128)(2,1)S(1)}, u32[]{:S(2)}, u32[]{:S(2)}) collective-permute-start(bf16[256,256]{1,0:T(8,128)(2,1)S(1)} %get-tuple-element.126), channel_id=1, source_target_pairs={{0,24},{8,16},{16,8},{24,0},{1,25},{9,17},{17,9},{25,1},{2,26},{10... | collective-permute-start | bytes 393224 | tf_op jit(solution)/shard_map/ppermute | solution.py:340
  82.2 18.2 %collective-permute-start.20 = (bf16[512,256]{1,0:T(8,128)(2,1)S(1)}, bf16[512,256]{1,0:T(8,128)(2,1)S(1)}, u32[]{:S(2)}, u32[]{:S(2)}) collective-permute-start(bf16[512,256]{1,0:T(8,128)(2,1)S(1)} %get-tuple-element.96.refs_0_), channel_id=1, source_target_pairs={{0,8},{8,0},{16,24},{24,16},{1,9},{9,1},{17,25},{25,17},{2,10},{10... | collective-permute-start | bytes 786440 | tf_op jit(solution)/shard_map/ppermute | solution.py:340
  82.7 6.6 %collective-permute-start.34 = (bf16[128,256]{1,0:T(8,128)(2,1)S(1)}, bf16[128,256]{1,0:T(8,128)(2,1)S(1)}, u32[]{:S(2)}, u32[]{:S(2)}) collective-permute-start(bf16[128,256]{1,0:T(8,128)(2,1)S(1)} %get-tuple-element.113), channel_id=1, source_target_pairs={{0,5},{1,4},{2,7},{3,6},{4,1},{5,0},{6,3},{7,2},{8,13},{9,12},{10,... | collective-permute-start | bytes 196616 | tf_op jit(solution)/shard_map/ppermute | solution.py:340
  89.3 14.8 %collective-permute-start.21 = (bf16[512,256]{1,0:T(8,128)(2,1)S(1)}, bf16[512,256]{1,0:T(8,128)(2,1)S(1)}, u32[]{:S(2)}, u32[]{:S(2)}) collective-permute-start(bf16[512,256]{1,0:T(8,128)(2,1)S(1)} %get-tuple-element.96.refs_0_), channel_id=1, source_target_pairs={{0,16},{8,24},{16,0},{24,8},{1,17},{9,25},{17,1},{25,9},{2,18},{10... | collective-permute-start | bytes 786440 | tf_op jit(solution)/shard_map/ppermute | solution.py:340
  89.8 14.2 %collective-permute-start.22 = (bf16[512,256]{1,0:T(8,128)(2,1)S(1)}, bf16[512,256]{1,0:T(8,128)(2,1)S(1)}, u32[]{:S(2)}, u32[]{:S(2)}) collective-permute-start(bf16[512,256]{1,0:T(8,128)(2,1)S(1)} %get-tuple-element.96.refs_0_), channel_id=1, source_target_pairs={{0,24},{8,16},{16,8},{24,0},{1,25},{9,17},{17,9},{25,1},{2,26},{10... | collective-permute-start | bytes 786440 | tf_op jit(solution)/shard_map/ppermute | solution.py:340
  92.3 6.2 %collective-permute-start.35 = (bf16[128,256]{1,0:T(8,128)(2,1)S(1)}, bf16[128,256]{1,0:T(8,128)(2,1)S(1)}, u32[]{:S(2)}, u32[]{:S(2)}) collective-permute-start(bf16[128,256]{1,0:T(8,128)(2,1)S(1)} %get-tuple-element.114), channel_id=1, source_target_pairs={{0,6},{1,7},{2,4},{3,5},{4,2},{5,3},{6,0},{7,1},{8,14},{9,15},{10,... | collective-permute-start | bytes 196616 | tf_op jit(solution)/shard_map/ppermute | solution.py:340
  94.1 5.8 %collective-permute-start.36 = (bf16[128,256]{1,0:T(8,128)(2,1)S(1)}, bf16[128,256]{1,0:T(8,128)(2,1)S(1)}, u32[]{:S(2)}, u32[]{:S(2)}) collective-permute-start(bf16[128,256]{1,0:T(8,128)(2,1)S(1)} %get-tuple-element.115), channel_id=1, source_target_pairs={{0,7},{1,6},{2,5},{3,4},{4,3},{5,2},{6,1},{7,0},{8,15},{9,14},{10,... | collective-permute-start | bytes 196616 | tf_op jit(solution)/shard_map/ppermute | solution.py:340
  98.5 9.2 %collective-permute-start.43 = (bf16[512,256]{1,0:T(8,128)(2,1)S(1)}, bf16[512,256]{1,0:T(8,128)(2,1)S(1)}, u32[]{:S(2)}, u32[]{:S(2)}) collective-permute-start(bf16[512,256]{1,0:T(8,128)(2,1)S(1)} %get-tuple-element.128), channel_id=1, source_target_pairs={{0,8},{8,0},{16,24},{24,16},{1,9},{9,1},{17,25},{25,17},{2,10},{10... | collective-permute-start | bytes 786440 | tf_op jit(solution)/shard_map/ppermute | solution.py:340
  99.9 14.6 %collective-permute-start.44 = (bf16[512,256]{1,0:T(8,128)(2,1)S(1)}, bf16[512,256]{1,0:T(8,128)(2,1)S(1)}, u32[]{:S(2)}, u32[]{:S(2)}) collective-permute-start(bf16[512,256]{1,0:T(8,128)(2,1)S(1)} %get-tuple-element.129), channel_id=1, source_target_pairs={{0,16},{8,24},{16,0},{24,8},{1,17},{9,25},{17,1},{25,9},{2,18},{10... | collective-permute-start | bytes 786440 | tf_op jit(solution)/shard_map/ppermute | solution.py:340
  100.4 14.0 %collective-permute-start.45 = (bf16[512,256]{1,0:T(8,128)(2,1)S(1)}, bf16[512,256]{1,0:T(8,128)(2,1)S(1)}, u32[]{:S(2)}, u32[]{:S(2)}) collective-permute-start(bf16[512,256]{1,0:T(8,128)(2,1)S(1)} %get-tuple-element.130), channel_id=1, source_target_pairs={{0,24},{8,16},{16,8},{24,0},{1,25},{9,17},{17,9},{25,1},{2,26},{10... | collective-permute-start | bytes 786440 | tf_op jit(solution)/shard_map/ppermute | solution.py:340
  (4 other events, 40.3 us)
